TPU v7x, 256 devices: a whole 4x4x8 slice. The times are simulated.
256 devices in a mesh: grp: 4 (over y), tok: 64 (over z, x, core).
Axes of the slice: x: 4, y: 4, z: 8, core: 2. Of those that a mesh axis runs over, the one named last changes fastest.
Arguments:
- hidden: bfloat16 [512, 64, 1024], P('tok', 'grp'), may hold values from -6 to 6
- draft_qkv: bfloat16 [3, 512, 64, 1024], P(None, 'tok', None, 'grp'), may hold values from -4 to 4
- self_cache: bfloat16 [512, 2, 512, 1024], P('tok', None, None, 'grp'), may hold values from -4 to 4
- cross_cache: bfloat16 [512, 2, 512, 1024], P('tok', None, None, 'grp'), may hold values from -4 to 4
- parents: int32 [512, 64], P('tok'), may hold values from -1 to 62, as said below
- counts: int32 [512], P('tok'), may hold values from 32 to 64, as said below
- self_len: int32 [512], P('tok'), may hold values from 2 to 512, as said below
- enc_len: int32 [512], P('tok'), may hold values from 2 to 512, as said below
- buckets: int32 [512, 64, 64], P('tok'), may hold values from 0 to 31
- bias_table: float32 [32, 16], P(None, 'grp'), may hold values from -4 to 4
- gain_cross: float32 [1024], replicated, may hold values from 0.25 to 1.75
- gain_ffn: float32 [1024], replicated, may hold values from 0.25 to 1.75
- gain_next: float32 [1024], replicated, may hold values from 0.25 to 1.75
- w_out_self: bfloat16 [1024, 1024], P('grp', 'tok'), may hold values from -0.1875 to 0.1875
- w_query_cross: bfloat16 [1024, 1024], P('tok', 'grp'), may hold values from -1 to 1
- w_out_cross: bfloat16 [1024, 1024], P('grp', 'tok'), may hold values from -0.1875 to 0.1875
- w_gate: bfloat16 [1024, 2816], P('tok', 'grp'), may hold values from -0.1875 to 0.1875
- w_up: bfloat16 [1024, 2816], P('tok', 'grp'), may hold values from -0.1875 to 0.1875
- w_down: bfloat16 [2816, 1024], P('grp', 'tok'), may hold values from -0.109375 to 0.109375
- w_qkv: bfloat16 [1024, 3, 1024], P('tok', None, 'grp'), may hold values from -0.1875 to 0.1875
Outputs:
- out_hidden: bfloat16 [512, 64, 1024], P('tok', 'grp')
- next_qkv: bfloat16 [3, 512, 64, 1024], P(None, 'tok', None, 'grp')
Inputs may be any that keep to these rules, and one draw needn't show every extreme that they name: `parents`: slot 0 of every tree has parent -1; every other slot's parent is an earlier slot. `counts`: some request fills all 64 draft slots. `self_len`: some request fills its whole cache. `enc_len`: some request has all 512 encoder positions.
All inputs are finite; a program needn't handle non-finite values.
Results may differ from a plain program's by a relative error of at most 0.025.
Values may be sent and summed in bfloat16 or wider, within the bound.
A program may use at most 64 MiB of HBM per device.

v0:
```python
import jax
import jax.numpy as jnp
from jax import lax
from jax.sharding import PartitionSpec as P

DH = 64


def ancestor_table(parent_ids):
    count_slots = parent_ids.shape[0]
    slot_ids = jnp.arange(count_slots, dtype=jnp.int32)
    ancestors = jnp.eye(count_slots, dtype=jnp.float32) + (
        parent_ids[:, None] == slot_ids[None, :]
    ).astype(jnp.float32)
    for repeat in range(max(1, count_slots.bit_length())):
        ancestors = jnp.minimum(jnp.dot(ancestors, ancestors, precision=lax.Precision.HIGHEST), 1.0)
    return ancestors


def rms_scale(stream, gain_vec):
    mean_square = jnp.mean(stream * stream, axis=-1, keepdims=True)
    return (stream * lax.rsqrt(mean_square + 1e-06) * gain_vec).astype(jnp.bfloat16)


def draft_attention(projected, cached, parent_ids, draft_count, length, bucket_ids, bias_table):
    requests, draft_slots, head_width = (projected.shape[1], projected.shape[2], projected.shape[3])
    local_heads = bias_table.shape[1]
    head_size = head_width // local_heads
    queries = projected[0].reshape(requests, draft_slots, local_heads, head_size)
    draft_keys = projected[1].reshape(requests, draft_slots, local_heads, head_size)
    draft_values = projected[2].reshape(requests, draft_slots, local_heads, head_size)
    cache_keys = cached[:, 0].reshape(requests, -1, local_heads, head_size)
    cache_values = cached[:, 1].reshape(requests, -1, local_heads, head_size)
    cache_scores = jnp.einsum(
        "rihd,rphd->rhip", queries, cache_keys, preferred_element_type=jnp.float32
    )
    cache_scores = cache_scores + bias_table[-1][None, :, None, None]
    cache_live = jnp.arange(cache_keys.shape[1], dtype=jnp.int32)[None, :] < length[:, None]
    cache_scores = jnp.where(cache_live[:, None, None, :], cache_scores, -1e30)
    onehot = (bucket_ids[..., None] == jnp.arange(bias_table.shape[0], dtype=jnp.int32)).astype(
        jnp.float32
    )
    draft_bias = jnp.einsum("rijb,bh->rhij", onehot, bias_table, precision=lax.Precision.HIGHEST)
    draft_scores = (
        jnp.einsum("rihd,rjhd->rhij", queries, draft_keys, preferred_element_type=jnp.float32)
        + draft_bias
    )
    ancestors = jax.vmap(ancestor_table)(parent_ids)
    draft_live = (ancestors > 0.5) & (
        jnp.arange(draft_slots, dtype=jnp.int32)[None, None, :] < draft_count[:, None, None]
    )
    draft_scores = jnp.where(draft_live[:, None], draft_scores, -1e30)
    highest = jnp.maximum(cache_scores.max(-1, keepdims=True), draft_scores.max(-1, keepdims=True))
    exp_cache = jnp.exp(cache_scores - highest)
    exp_draft = jnp.exp(draft_scores - highest)
    denominator = exp_cache.sum(-1, keepdims=True) + exp_draft.sum(-1, keepdims=True)
    weights_cache = (exp_cache / denominator).astype(jnp.bfloat16)
    weights_draft = (exp_draft / denominator).astype(jnp.bfloat16)
    attended = jnp.einsum(
        "rhip,rphd->rihd", weights_cache, cache_values, preferred_element_type=jnp.float32
    )
    attended = attended + jnp.einsum(
        "rhij,rjhd->rihd", weights_draft, draft_values, preferred_element_type=jnp.float32
    )
    return attended.astype(jnp.bfloat16).reshape(requests * draft_slots, head_width)


def cross_attention(query_rows, cached, length):
    requests, draft_slots, head_width = query_rows.shape
    local_heads = head_width // DH
    queries = query_rows.reshape(requests, draft_slots, local_heads, DH)
    enc_keys = cached[:, 0].reshape(requests, -1, local_heads, DH)
    enc_values = cached[:, 1].reshape(requests, -1, local_heads, DH)
    scores = jnp.einsum("rihd,rphd->rhip", queries, enc_keys, preferred_element_type=jnp.float32)
    live = jnp.arange(enc_keys.shape[1], dtype=jnp.int32)[None, :] < length[:, None]
    scores = jnp.where(live[:, None, None, :], scores, -1e30)
    highest = scores.max(-1, keepdims=True)
    exp_scores = jnp.exp(scores - highest)
    weights = (exp_scores / exp_scores.sum(-1, keepdims=True)).astype(jnp.bfloat16)
    attended = jnp.einsum(
        "rhip,rphd->rihd", weights, enc_values, preferred_element_type=jnp.float32
    )
    return attended.astype(jnp.bfloat16).reshape(requests * draft_slots, head_width)


def layer_sum(summand, base_full):
    return lax.psum(summand.astype(jnp.bfloat16), "grp").astype(jnp.float32) + base_full


def normed_rows(stream, gain_vec):
    scaled = rms_scale(stream, gain_vec)
    return scaled.reshape(-1, scaled.shape[-1])


def shards(
    hidden,
    draft_qkv,
    self_cache,
    cross_cache,
    parents,
    counts,
    self_len,
    enc_len,
    buckets,
    bias_table,
    gain_cross,
    gain_ffn,
    gain_next,
    w_out_self,
    w_query_cross,
    w_out_cross,
    w_gate,
    w_up,
    w_down,
    w_qkv,
):
    requests, share_rows, model_width = hidden.shape
    draft_slots = draft_qkv.shape[2]
    head_width = draft_qkv.shape[3]
    fetched = (
        lax.all_gather(w_out_self, "tok", axis=1, tiled=True),
        lax.all_gather(w_query_cross, "tok", axis=0, tiled=True),
        lax.all_gather(w_out_cross, "tok", axis=1, tiled=True),
        lax.all_gather(w_gate, "tok", axis=0, tiled=True),
        lax.all_gather(w_up, "tok", axis=0, tiled=True),
        lax.all_gather(w_down, "tok", axis=1, tiled=True),
        lax.all_gather(w_qkv, "tok", axis=0, tiled=True),
    )
    self_context = draft_attention(
        draft_qkv, self_cache, parents, counts, self_len, buckets, bias_table
    )
    partial_value = jnp.dot(self_context, fetched[0], preferred_element_type=jnp.float32)
    partial_value = partial_value.reshape(requests, draft_slots, model_width)
    own_rows = hidden.astype(jnp.float32)
    offset = lax.axis_index("grp") * share_rows
    placed = lax.dynamic_update_slice(
        jnp.zeros((requests, draft_slots, model_width), jnp.float32), own_rows, (0, offset, 0)
    )
    stream_one = layer_sum(partial_value + placed, 0.0)
    normed_one = normed_rows(stream_one, gain_cross)
    cross_query = jnp.dot(normed_one, fetched[1], preferred_element_type=jnp.float32)
    cross_query = cross_query.astype(jnp.bfloat16).reshape(requests, draft_slots, head_width)
    cross_context = cross_attention(cross_query, cross_cache, enc_len)
    partial_value = jnp.dot(cross_context, fetched[2], preferred_element_type=jnp.float32)
    stream_two = layer_sum(partial_value.reshape(requests, draft_slots, model_width), stream_one)
    normed_two = normed_rows(stream_two, gain_ffn)
    gate_part = jnp.dot(normed_two, fetched[3], preferred_element_type=jnp.float32)
    up_part = jnp.dot(normed_two, fetched[4], preferred_element_type=jnp.float32)
    gated = (jax.nn.gelu(gate_part, approximate=True) * up_part).astype(jnp.bfloat16)
    partial_value = jnp.dot(gated, fetched[5], preferred_element_type=jnp.float32)
    stream_three = layer_sum(partial_value.reshape(requests, draft_slots, model_width), stream_two)
    normed_three = normed_rows(stream_three, gain_next)
    projected = jnp.dot(
        normed_three,
        fetched[6].reshape(fetched[6].shape[0], -1),
        preferred_element_type=jnp.float32,
    )
    projected = projected.astype(jnp.bfloat16).reshape(requests, draft_slots, 3, head_width)
    next_qkv = jnp.transpose(projected, (2, 0, 1, 3))
    out_hidden = lax.dynamic_slice_in_dim(stream_three, offset, share_rows, 1).astype(jnp.bfloat16)
    return (out_hidden, next_qkv)


def solution(mesh):
    in_specs = (
        P("tok", "grp", None),
        P(None, "tok", None, "grp"),
        P("tok", None, None, "grp"),
        P("tok", None, None, "grp"),
        P("tok", None),
        P("tok"),
        P("tok"),
        P("tok"),
        P("tok", None, None),
        P(None, "grp"),
        P(),
        P(),
        P(),
        P("grp", "tok"),
        P("tok", "grp"),
        P("grp", "tok"),
        P("tok", "grp"),
        P("tok", "grp"),
        P("grp", "tok"),
        P("tok", None, "grp"),
    )
    out_specs = (P("tok", "grp", None), P(None, "tok", None, "grp"))
    return jax.shard_map(shards, mesh=mesh, in_specs=in_specs, out_specs=out_specs, check_vma=False)
```

profile of v0, /device:TPU:1, one launch (start us, length us, event | category | flops | bytes accessed | tf_op | source)
XLA Modules:
  0.0 532.7 jit_solution(6397232074818495033)
XLA Ops:
  8.1 3.9 fusion.56
  12.0 2.4 copy.53
  14.6 2.9 copy.47
  17.5 1.9 fusion.57
  19.4 0.2 reshape_squeeze.21
  19.7 3.6 fusion.1
  23.3 2.6 copy.52
  25.8 1.2 reshape_squeeze.23
  27.1 0.5 convolution_minimum_fusion.6
  27.6 0.4 convolution_minimum_fusion.5
  28.0 0.4 convolution_minimum_fusion.4
  28.4 0.4 convolution_minimum_fusion.3
  28.8 0.4 convolution_minimum_fusion.2
  29.2 0.4 convolution_minimum_fusion.1
  29.7 0.4 fusion.29
  30.3 0.8 fusion.3
  31.0 0.4 copy-done.3
  31.5 0.4 fusion.58
  32.0 1.5 fusion.7
  33.7 1.0 reshape_squeeze.25
  34.7 3.0 fusion.14
  37.8 0.4 fusion.27
  38.2 0.4 copy.56
  38.6 0.3 dot_general.79
  39.0 54.8 %all_gather.21 = bf16[256,1024]{0,1:T(8,128)(2,1)S(1)} all-gather(bf16[256,16]{0,1:T(8,128)(2,1)S(1)} %copy-done.9), channel_id=1, replica_groups=mesh['grp'=4,'tok'=64] {'tok'}, dimensions={1}, use_global_device_ids=true | all-gather | bytes 532480 | tf_op jit(solution)/shard_map/all_gather | solution.py:121
  93.8 0.5 fusion.32
  94.4 1.1 convert_element_type.84
  95.6 3.9 fusion.55
  99.5 2.4 copy.59
  101.9 2.9 copy.57
  104.8 49.2 %all_gather.22 = bf16[1024,256]{1,0:T(8,128)(2,1)S(1)} all-gather(bf16[16,256]{1,0:T(8,128)(2,1)S(1)} %copy-done.10), channel_id=1, replica_groups=mesh['grp'=4,'tok'=64] {'tok'}, dimensions={0}, use_global_device_ids=true | all-gather | bytes 532480 | tf_op jit(solution)/shard_map/all_gather | solution.py:122
  154.0 48.2 %all_gather.23 = bf16[256,1024]{0,1:T(8,128)(2,1)S(1)} all-gather(bf16[256,16]{0,1:T(8,128)(2,1)S(1)} %copy-done.11), channel_id=1, replica_groups=mesh['grp'=4,'tok'=64] {'tok'}, dimensions={1}, use_global_device_ids=true | all-gather | bytes 532480 | tf_op jit(solution)/shard_map/all_gather | solution.py:123
  202.2 1.5 fusion.8
  203.8 1.5 fusion.10
  205.3 0.4 convolution_convert_fusion.3
  205.7 0.2 reshape_reshape.3
  206.0 0.7 fusion.34
  206.7 2.0 fusion.59
  208.7 0.8 fusion.26
  209.4 0.4 copy.60
  209.9 0.3 dot_general.84
  210.2 1.5 convolution_convert_fusion.1
  211.8 0.5 all-gather.5.cloned.1.call-update
  212.4 0.5 all-gather.9.cloned.1.call-update
  213.0 0.5 all-gather.7.cloned.1.call-update
  213.6 0.7 all-gather.11.cloned.1.call-update
  214.3 0.3 all-reduce.8.cloned.1.call-start
  214.6 44.3 %all-reduce.6.cloned.1.call-done = bf16[8,64,1024]{2,1,0:T(8,128)(2,1)} async-done(((bf16[8,64,1024]{2,1,0:T(8,128)(2,1)}), bf16[8,64,1024]{2,1,0:T(8,128)(2,1)}) %all-reduce.6.cloned.1.call-update) | async-done | bytes 1048592 | tf_op jit(solution)/shard_map/psum | solution.py:87
  258.9 1.7 multiply_reduce_fusion.1
  260.6 0.4 multiply_convert_fusion.1
  261.0 28.7 %all-gather.5.cloned.1.call-done = bf16[1024,704]{1,0:T(8,128)(2,1)} async-done(((bf16[16,704]{1,0:T(8,128)(2,1)}), bf16[1024,704]{1,0:T(8,128)(2,1)}) %all-gather.5.cloned.1.call-update) | async-done | bytes 1441808 | tf_op jit(solution)/shard_map/all_gather | solution.py:124
  289.7 3.5 fusion.60
  293.2 73.9 %all-gather.9.cloned.1.call-done = bf16[704,1024]{0,1:T(8,128)(2,1)} async-done(((bf16[704,16]{0,1:T(8,128)(2,1)}), bf16[704,1024]{0,1:T(8,128)(2,1)}) %all-gather.9.cloned.1.call-update) | async-done | bytes 1441808 | tf_op jit(solution)/shard_map/all_gather | solution.py:126
  367.1 77.4 %all-gather.7.cloned.1.call-done = bf16[1024,704]{1,0:T(8,128)(2,1)} async-done(((bf16[16,704]{1,0:T(8,128)(2,1)}), bf16[1024,704]{1,0:T(8,128)(2,1)}) %all-gather.7.cloned.1.call-update) | async-done | bytes 1441808 | tf_op jit(solution)/shard_map/all_gather | solution.py:125
  444.5 5.5 %convolution_convert_fusion = bf16[512,1024]{1,0:T(8,128)(2,1)} fusion(bf16[704,1024]{0,1:T(8,128)(2,1)} %all-gather.9.cloned.1.call-done, bf16[512,1024]{1,0:T(8,128)(2,1)S(1)} %bitcast.67, bf16[1024,704]{1,0:T(8,128)(2,1)} %all-gather.7.cloned.1.call-done, f32[512,704]{0,1:T(8,128)} %fusion.60), kind=kOutput, calls=%fused_computation.29 | convolution fusion | flops 1480523776 | bytes 6422528 | tf_op jit(solution)/shard_map/dot_general | solution.py:150
  450.0 67.0 %all-gather.11.cloned.1.call-done = bf16[1024,3,256]{2,0,1:T(8,128)(2,1)} async-done(((bf16[16,3,256]{2,0,1:T(8,128)(2,1)}), bf16[1024,3,256]{2,0,1:T(8,128)(2,1)}) %all-gather.11.cloned.1.call-update) | async-done | bytes 1572880 | tf_op jit(solution)/shard_map/all_gather | solution.py:127
  517.1 2.6 copy.61
  519.7 1.8 multiply_reduce_fusion
  521.4 0.7 dynamic-slice_convert_fusion
  522.2 0.2 multiply_convert_fusion
  522.4 0.5 copy-done.6
  522.9 1.0 convolution_convert_fusion.2
  524.0 0.4 reshape.141
  524.4 1.0 copy.62
  (64 shorter events, 1.3 us)
Async XLA Ops:
  8.0 194.2 %all-reduce.4.cloned.1.call-start = ((), (), s32[]{:S(2)}) async-start(), calls=%async_computation | async-start | bytes 2097152 | tf_op jit(solution)/shard_map/psum | solution.py:87
  12.0 2.4 copy-start.16
  12.0 2.6 copy-start.17
  17.5 2.2 copy-start.19
  19.7 7.4 %copy-start.12 = (s32[8,64]{1,0:T(8,128)S(1)}, s32[8,64]{1,0:T(8,128)}, u32[]{:S(2)}) copy-start(s32[8,64]{1,0:T(8,128)} %param.24) | copy-start | bytes 6148
  27.1 2.5 copy-start.20
  30.3 1.2 copy-start.3
  31.5 2.0 copy-start.1
  31.9 2.8 copy-start.4
  34.7 3.1 copy-start.7
  37.8 1.2 copy-start.9
  38.6 55.7 %copy-start.8 = (bf16[8,16,1024]{2,1,0:T(8,128)(2,1)S(1)}, bf16[8,16,1024]{2,1,0:T(8,128)(2,1)}, u32[]{:S(2)}) copy-start(bf16[8,16,1024]{2,1,0:T(8,128)(2,1)} %param.20) | copy-start | bytes 786436
  95.6 163.3 %all-reduce.6.cloned.1.call-start = ((), (), s32[]{:S(2)}) async-start(), calls=%async_computation.1 | async-start | bytes 2097152 | tf_op jit(solution)/shard_map/psum | solution.py:87
  101.9 2.9 copy-start.10
  101.9 52.1 %copy-start.11 = (bf16[256,16]{0,1:T(8,128)(2,1)S(1)}, bf16[256,16]{0,1:T(8,128)(2,1)}, u32[]{:S(2)}) copy-start(bf16[256,16]{0,1:T(8,128)(2,1)} %param.35) | copy-start | bytes 24580
  101.9 100.3 %copy-start.18 = (s32[8]{0:T(128)S(1)}, s32[8]{0:T(128)}, u32[]{:S(2)}) copy-start(s32[8]{0:T(128)} %param.27) | copy-start | bytes 100
  104.8 98.9 %copy-start.13 = (f32[1024]{0:T(1024)S(1)}, f32[1024]{0:T(1024)}, u32[]{:S(2)}) copy-start(f32[1024]{0:T(1024)} %param.30) | copy-start | bytes 12292
  206.7 2.0 copy-start.5
  209.9 49.0 %copy-start = (bf16[8,64,1024]{2,1,0:T(8,128)(2,1)S(1)}, bf16[8,64,1024]{2,1,0:T(8,128)(2,1)}, u32[]{:S(2)}) copy-start(bf16[8,64,1024]{2,1,0:T(8,128)(2,1)} %all-reduce.4.cloned.1.call-done) | copy-start | bytes 3145732
  210.2 50.4 %copy-start.14 = (f32[1024]{0:T(1024)S(1)}, f32[1024]{0:T(1024)}, u32[]{:S(2)}) copy-start(f32[1024]{0:T(1024)} %param.31) | copy-start | bytes 12292
  211.8 77.9 %all-gather.5.cloned.1.call-start = ((), (), s32[]{:S(2)}) async-start(), calls=%async_computation.2 | async-start | bytes 1597440 | tf_op jit(solution)/shard_map/all_gather | solution.py:124
  212.4 154.7 %all-gather.9.cloned.1.call-start = ((), (), s32[]{:S(2)}) async-start(), calls=%async_computation.4 | async-start | bytes 1597440 | tf_op jit(solution)/shard_map/all_gather | solution.py:126
  213.0 231.5 %all-gather.7.cloned.1.call-start = ((), (), s32[]{:S(2)}) async-start(), calls=%async_computation.3 | async-start | bytes 1597440 | tf_op jit(solution)/shard_map/all_gather | solution.py:125
  213.5 303.5 %all-gather.11.cloned.1.call-start = ((), (), s32[]{:S(2)}) async-start(), calls=%async_computation.6 | async-start | bytes 1597440 | tf_op jit(solution)/shard_map/all_gather | solution.py:127
  214.3 305.4 %all-reduce.8.cloned.1.call-start = ((), (), s32[]{:S(2)}) async-start(), calls=%async_computation.5 | async-start | bytes 2097152 | tf_op jit(solution)/shard_map/psum | solution.py:87
  258.9 1.7 copy-start.2
  519.6 2.5 copy-start.15
  521.4 1.5 copy-start.6
Sparse Core Ops, SparseCore 0:
  95.7 46.8 all-reduce.3
  211.9 46.8 all-reduce.5
  450.1 46.8 all-reduce.7
Sparse Core Ops, SparseCore 1:
  215.0 74.7 all-gather.4
  292.4 74.7 all-gather.8
  369.8 74.7 all-gather.6
  447.5 69.5 all-gather.10
where the time goes:
time: 533 us
  waiting for transfers between devices  294 us (55%)
  blocking collectives  152 us (29%)
  local copies, waits for them, and re-layouts  33.2 us (6%)
  matrix products  25 us (5%)
  between operations  15.9 us (3%)
  other arithmetic  12.3 us (2%)
    all_gather x1, waiting for transfers between devices, shards(): lax.all_gather(w_up, 'tok', axis=0, tiled=True)  77.4 us
    all_gather x1, waiting for transfers between devices, shards(): lax.all_gather(w_down, 'tok', axis=1, tiled=True)  73.9 us
    all_gather x1, waiting for transfers between devices, shards(): lax.all_gather(w_qkv, 'tok', axis=0, tiled=True)  67 us
    all_gather x1, blocking collectives, shards(): lax.all_gather(w_out_self, 'tok', axis=1, tiled=True)  54.8 us
    all_gather x1, blocking collectives, shards(): lax.all_gather(w_query_cross, 'tok', axis=0, tiled=True)  49.2 us
    all_gather x1, blocking collectives, shards(): lax.all_gather(w_out_cross, 'tok', axis=1, tiled=True)  48.2 us
    psum x3, waiting for transfers between devices, layer_sum(): lax.psum(summand.astype(jnp.bfloat16), 'grp').astype(jnp.float32)  44.3 us
    all_gather x1, waiting for transfers between devices, shards(): lax.all_gather(w_gate, 'tok', axis=0, tiled=True)  28.7 us
  transfers between devices with their start and end apart: 7, of which 5 were waited for; matrix products, arithmetic and copies ran while one was open for 4% of the time, Pallas kernels for 0%

commit v1 on v0

--- a/solution.py
+++ b/solution.py
@@ -1,6 +1,10 @@
+import functools
+
 import jax
 import jax.numpy as jnp
 from jax import lax
+from jax.experimental import pallas as pl
+from jax.experimental.pallas import tpu as pltpu
 from jax.sharding import PartitionSpec as P
 
 DH = 64
@@ -82,6 +86,113 @@
     )
     return attended.astype(jnp.bfloat16).reshape(requests * draft_slots, head_width)
 
+
+def gather_kernel(n_chips, n_in, *refs):
+    srcs = refs[:n_in]
+    outs = refs[n_in:2 * n_in]
+    send_sems, recv_sems, local_sems, fwd_send, fwd_recv = refs[2 * n_in:]
+    grp = lax.axis_index("grp")
+    me = lax.axis_index("tok")
+    chip = me // 2
+    core = me % 2
+    sibling = chip * 2 + (1 - core)
+    mesh_id = pl.DeviceIdType.MESH
+
+    barrier = pltpu.get_barrier_semaphore()
+    for k in range(1, n_chips):
+        peer = lax.rem(chip + k, n_chips) * 2 + core
+        pl.semaphore_signal(barrier, inc=1, device_id=(grp, peer), device_id_type=mesh_id)
+    pl.semaphore_signal(barrier, inc=1, device_id=(grp, sibling), device_id_type=mesh_id)
+    pl.semaphore_wait(barrier, n_chips)
+
+    locals_ = [
+        pltpu.make_async_copy(srcs[i], outs[i].at[chip, core], local_sems.at[i]) for i in range(n_in)
+    ]
+    for copy in locals_:
+        copy.start()
+
+    def remote(i, k):
+        other = lax.rem(chip + k, n_chips)
+        return pltpu.make_async_remote_copy(
+            src_ref=srcs[i],
+            dst_ref=outs[i].at[chip, core],
+            send_sem=send_sems.at[i, k],
+            recv_sem=recv_sems.at[i, chip],
+            device_id=(grp, other * 2 + core),
+            device_id_type=mesh_id,
+        )
+
+    def send(k, carry):
+        for i in range(n_in):
+            remote(i, k).start()
+        return carry
+
+    lax.fori_loop(1, n_chips, send, 0)
+
+    def arrive(k, carry):
+        other = lax.rem(chip + k, n_chips)
+        for i in range(n_in):
+            remote(i, k).wait_send()
+            pltpu.make_async_copy(
+                srcs[i], outs[i].at[other, core], recv_sems.at[i, other]
+            ).wait()
+        return carry
+
+    lax.fori_loop(1, n_chips, arrive, 0)
+    for copy in locals_:
+        copy.wait()
+
+    def forward(i, c):
+        return pltpu.make_async_remote_copy(
+            src_ref=outs[i].at[c, core],
+            dst_ref=outs[i].at[c, core],
+            send_sem=fwd_send.at[i, c],
+            recv_sem=fwd_recv.at[i, c],
+            device_id=(grp, sibling),
+            device_id_type=mesh_id,
+        )
+
+    def push(c, carry):
+        for i in range(n_in):
+            forward(i, c).start()
+        return carry
+
+    lax.fori_loop(0, n_chips, push, 0)
+
+    def land(c, carry):
+        for i in range(n_in):
+            forward(i, c).wait_send()
+            pltpu.make_async_copy(
+                outs[i].at[c, core], outs[i].at[c, 1 - core], fwd_recv.at[i, c]
+            ).wait()
+        return carry
+
+    lax.fori_loop(0, n_chips, land, 0)
+
+
+def fetch_group(n_tok, collective_id, parts, after):
+    parts = list(lax.optimization_barrier((tuple(parts), after))[0])
+    n_chips = n_tok // 2
+    n_in = len(parts)
+    moved = 2 * n_tok * sum(p.size for p in parts) * parts[0].dtype.itemsize
+    gathered = pl.pallas_call(
+        functools.partial(gather_kernel, n_chips, n_in),
+        out_shape=tuple(
+            jax.ShapeDtypeStruct((n_chips, 2) + p.shape, p.dtype) for p in parts
+        ),
+        in_specs=[pl.BlockSpec(memory_space=pl.ANY)] * n_in,
+        out_specs=tuple(pl.BlockSpec(memory_space=pl.ANY) for _ in parts),
+        scratch_shapes=[
+            pltpu.SemaphoreType.DMA((n_in, n_chips)),
+            pltpu.SemaphoreType.DMA((n_in, n_chips)),
+            pltpu.SemaphoreType.DMA((n_in,)),
+            pltpu.SemaphoreType.DMA((n_in, n_chips)),
+            pltpu.SemaphoreType.DMA((n_in, n_chips)),
+        ],
+        compiler_params=pltpu.CompilerParams(collective_id=collective_id, has_side_effects=True),
+        cost_estimate=pl.CostEstimate(flops=0, transcendentals=0, bytes_accessed=moved),
+    )(*parts)
+    return [g.reshape((n_tok * g.shape[2],) + g.shape[3:]) for g in gathered]
 
 def layer_sum(summand, base_full):
     return lax.psum(summand.astype(jnp.bfloat16), "grp").astype(jnp.float32) + base_full
@@ -117,42 +228,47 @@
     requests, share_rows, model_width = hidden.shape
     draft_slots = draft_qkv.shape[2]
     head_width = draft_qkv.shape[3]
-    fetched = (
-        lax.all_gather(w_out_self, "tok", axis=1, tiled=True),
-        lax.all_gather(w_query_cross, "tok", axis=0, tiled=True),
-        lax.all_gather(w_out_cross, "tok", axis=1, tiled=True),
-        lax.all_gather(w_gate, "tok", axis=0, tiled=True),
-        lax.all_gather(w_up, "tok", axis=0, tiled=True),
-        lax.all_gather(w_down, "tok", axis=1, tiled=True),
-        lax.all_gather(w_qkv, "tok", axis=0, tiled=True),
-    )
     self_context = draft_attention(
         draft_qkv, self_cache, parents, counts, self_len, buckets, bias_table
     )
-    partial_value = jnp.dot(self_context, fetched[0], preferred_element_type=jnp.float32)
+    (w_out_self_t,) = fetch_group(lax.axis_size("tok"), 3, (w_out_self.T,), self_context)
+    partial_value = jnp.einsum(
+        "rk,ok->ro", self_context, w_out_self_t, preferred_element_type=jnp.float32
+    )
     partial_value = partial_value.reshape(requests, draft_slots, model_width)
     own_rows = hidden.astype(jnp.float32)
     offset = lax.axis_index("grp") * share_rows
     placed = lax.dynamic_update_slice(
         jnp.zeros((requests, draft_slots, model_width), jnp.float32), own_rows, (0, offset, 0)
     )
-    stream_one = layer_sum(partial_value + placed, 0.0)
+    summand = partial_value + placed
+    n_tok = lax.axis_size("tok")
+    w_query_full, w_out_cross_t, w_gate_full = fetch_group(
+        n_tok, 0, (w_query_cross, w_out_cross.T, w_gate), summand
+    )
+    stream_one = layer_sum(summand, 0.0)
     normed_one = normed_rows(stream_one, gain_cross)
-    cross_query = jnp.dot(normed_one, fetched[1], preferred_element_type=jnp.float32)
+    cross_query = jnp.dot(normed_one, w_query_full, preferred_element_type=jnp.float32)
     cross_query = cross_query.astype(jnp.bfloat16).reshape(requests, draft_slots, head_width)
     cross_context = cross_attention(cross_query, cross_cache, enc_len)
-    partial_value = jnp.dot(cross_context, fetched[2], preferred_element_type=jnp.float32)
+    partial_value = jnp.einsum(
+        "rk,ok->ro", cross_context, w_out_cross_t, preferred_element_type=jnp.float32
+    )
+    w_up_full, w_down_t = fetch_group(n_tok, 1, (w_up, w_down.T), partial_value)
     stream_two = layer_sum(partial_value.reshape(requests, draft_slots, model_width), stream_one)
     normed_two = normed_rows(stream_two, gain_ffn)
-    gate_part = jnp.dot(normed_two, fetched[3], preferred_element_type=jnp.float32)
-    up_part = jnp.dot(normed_two, fetched[4], preferred_element_type=jnp.float32)
+    gate_part = jnp.dot(normed_two, w_gate_full, preferred_element_type=jnp.float32)
+    up_part = jnp.dot(normed_two, w_up_full, preferred_element_type=jnp.float32)
     gated = (jax.nn.gelu(gate_part, approximate=True) * up_part).astype(jnp.bfloat16)
-    partial_value = jnp.dot(gated, fetched[5], preferred_element_type=jnp.float32)
+    partial_value = jnp.einsum("rk,ok->ro", gated, w_down_t, preferred_element_type=jnp.float32)
+    (w_qkv_full,) = fetch_group(
+        n_tok, 2, (w_qkv.reshape(w_qkv.shape[0], -1),), partial_value
+    )
     stream_three = layer_sum(partial_value.reshape(requests, draft_slots, model_width), stream_two)
     normed_three = normed_rows(stream_three, gain_next)
     projected = jnp.dot(
         normed_three,
-        fetched[6].reshape(fetched[6].shape[0], -1),
+        w_qkv_full.reshape(w_qkv_full.shape[0], -1),
         preferred_element_type=jnp.float32,
     )
     projected = projected.astype(jnp.bfloat16).reshape(requests, draft_slots, 3, head_width)

time: 533 us -> 257 us (0.48)
  waiting for transfers between devices: 294 us -> 19.8 us
  blocking collectives: 152 us -> 0 us
  Pallas kernels: 0 us -> 147 us
    all_gather x4 -> x0, waiting for transfers between devices: 247 us -> none  [the longest x1 77.4 us: shards(): lax.all_gather(w_up, 'tok', axis=0, tiled=True)]
    all_gather x3 -> x0, blocking collectives: 152 us -> none  [the longest x1 54.8 us: shards(): lax.all_gather(w_out_self, 'tok', axis=1, tiled=True)]
    pallas_call x0 -> x4, Pallas kernels: none -> 147 us  [fetch_group(): pl.pallas_call(functools.partial(gather_kernel, n_chips, n_in), out_shape...]
    psum x3, waiting for transfers between devices: 44.3 us -> 19.8 us  [layer_sum(): lax.psum(summand.astype(jnp.bfloat16), 'grp').astype(jnp.float32)]
  transfers between devices with their start and end apart: 7 -> 3, of which waited for: 5 -> 1; matrix products, arithmetic and copies ran while one was open for 4% -> 5% of each run, Pallas kernels for 0% -> 49%
where the time goes in v1:
time: 257 us; the launch traced here: 255 us
  Pallas kernels  147 us (57%)
  local copies, waits for them, and re-layouts  35.7 us (14%)
  matrix products  26.5 us (10%)
  waiting for transfers between devices  19.8 us (8%)
  between operations  14.3 us (6%)
  other arithmetic  12.4 us (5%)
    pallas_call x4, Pallas kernels, fetch_group(): pl.pallas_call(functools.partial(gather_kernel, n_chips, n_in), out_shape...  147 us
    psum x3, waiting for transfers between devices, layer_sum(): lax.psum(summand.astype(jnp.bfloat16), 'grp').astype(jnp.float32)  19.8 us
    slice x2, local copies, waits for them, and re-layouts, cross_attention(): enc_keys = cached[:, 0].reshape(requests, -1, local_heads, DH)  7.45 us
    slice x2, local copies, waits for them, and re-layouts, draft_attention(): cache_keys = cached[:, 0].reshape(requests, -1, local_heads, head_size)  7.42 us
    dot_general x1, matrix products, shards(): jnp.einsum('rk,ok->ro', gated, w_down_t, preferred_element_type=jnp.float32)  5.45 us
  transfers between devices with their start and end apart: 3, of which 1 were waited for; matrix products, arithmetic and copies ran while one was open for 5% of the time, Pallas kernels for 49%

profile of v1, /device:TPU:1, one launch (start us, length us, event | category | flops | bytes accessed | tf_op | source)
XLA Modules:
  0.0 255.3 jit_solution(4803713618527332283)
XLA Ops:
  7.2 1.9 fusion.59
  9.1 0.2 reshape_squeeze.21
  9.5 0.2 slice_reduce_fusion
  9.6 4.6 %fusion.58 = (bf16[8,1,512,256]{3,2,1,0:T(8,128)(2,1)}, bf16[8,1,512,256]{3,2,1,0:T(8,128)(2,1)}) fusion(bf16[8,2,512,256]{3,2,1,0:T(8,128)(2,1)} %param.22), kind=kLoop, calls=%fused_computation.97 | loop fusion | bytes 8388608 | tf_op jit(solution)/shard_map/slice | solution.py:36
  14.2 2.9 %copy.32 = bf16[8,1,512,256]{2,3,0,1:T(8,128)(2,1)S(1)} copy(bf16[8,1,512,256]{3,2,1,0:T(8,128)(2,1)} %get-tuple-element.30) | data formatting | bytes 4194304 | tf_op jit(solution)/shard_map/slice | solution.py:36
  17.1 1.2 reshape_squeeze.23
  18.3 4.6 %fusion.1 = f32[8,64,64,4]{2,3,1,0:T(4,128)} fusion(s32[8,64,64]{2,1,0:T(8,128)} %param.28, f32[32,4]{0,1:T(4,128)S(1)} %copy-done.16), kind=kOutput, calls=%fused_computation.2 | convolution fusion | flops 51380224 | bytes 655872 | tf_op jit(solution)/shard_map/rijb,bh->rhij/dot_general | solution.py:47
  22.9 2.5 copy.37
  25.4 0.5 convolution_minimum_fusion.6
  25.9 0.4 convolution_minimum_fusion.5
  26.3 0.4 convolution_minimum_fusion.4
  26.7 0.4 convolution_minimum_fusion.3
  27.1 0.4 convolution_minimum_fusion.2
  27.5 0.4 convolution_minimum_fusion.1
  28.0 0.4 fusion.29
  28.4 0.2 copy.34
  28.6 0.8 fusion.3
  29.4 0.4 copy-done.4
  29.8 0.4 fusion.60
  30.3 1.5 fusion.7
  31.8 0.4 copy-done.5
  32.2 0.2 fusion.30
  32.4 0.8 copy-done.3
  33.2 2.4 copy.38
  35.6 0.2 reshape_squeeze.25
  35.9 4.1 %fusion.14 = f32[8,4,64,64]{3,2,1,0:T(8,128)S(1)} fusion(bf16[8,512,4,64]{1,3,2,0:T(8,128)(2,1)} %bitcast.79, f32[8,4,64,512]{3,2,1,0:T(8,128)} %copy-done.1, f32[8,4,64]{2,1,0:T(4,128)S(1)} %add.92, f32[8,4,64]{2,1,0:T(4,128)S(1)} %max.8, f32[4]{0:T(128)S(1)} %slice_reduce_fusion, pred[8,512]{1,0:T(8,128)(4,1)S(1)} %iota_compare_fusion.5), kind=kOutput, calls=%fused_computation.28 | convolution fusion | flops 139460608 | bytes 6836240 | tf_op jit(solution)/shard_map/rhip,rphd->rihd/dot_general | solution.py:63
  40.0 0.4 fusion.27
  40.4 0.4 copy.41
  40.8 0.3 dot_general.77
  41.2 22.4 %shard_map.203 = bf16[32,2,16,256]{3,2,1,0:T(8,128)(2,1)} custom-call(bf16[16,256]{1,0:T(8,128)(2,1)} %bitcast.91), custom_call_target="tpu_custom_call" | custom-call | bytes 1048576 | tf_op jit(solution)/shard_map/pallas_call | solution.py:178
  63.5 1.5 fusion.62
  65.1 0.1 add_dynamic-update-slice_fusion
  65.2 1.1 convert_element_type.87
  66.4 4.6 %fusion.57 = (bf16[8,1,512,256]{3,2,1,0:T(8,128)(2,1)}, bf16[8,1,512,256]{3,2,1,0:T(8,128)(2,1)}) fusion(bf16[8,2,512,256]{3,2,1,0:T(8,128)(2,1)} %param.23), kind=kLoop, calls=%fused_computation.96 | loop fusion | bytes 8388608 | tf_op jit(solution)/shard_map/slice | solution.py:76
  71.0 2.9 %copy.42 = bf16[8,1,512,256]{2,3,0,1:T(8,128)(2,1)S(1)} copy(bf16[8,1,512,256]{3,2,1,0:T(8,128)(2,1)} %get-tuple-element.28) | data formatting | bytes 4194304 | tf_op jit(solution)/shard_map/slice | solution.py:76
  73.9 4.0 %copy.44 = bf16[8,1,512,256]{2,3,0,1:T(8,128)(2,1)} copy(bf16[8,1,512,256]{3,2,1,0:T(8,128)(2,1)} %get-tuple-element.29) | data formatting | bytes 4194304 | tf_op jit(solution)/shard_map/slice | solution.py:77
  77.8 42.6 %shard_map.204 = (bf16[32,2,16,256]{3,2,1,0:T(8,128)(2,1)}, bf16[32,2,16,256]{3,2,1,0:T(8,128)(2,1)}, bf16[32,2,16,704]{3,2,1,0:T(8,128)(2,1)}) custom-call(bf16[16,256]{1,0:T(8,128)(2,1)} %refs_0_, bf16[16,256]{1,0:T(8,128)(2,1)} %bitcast.92, bf16[16,704]{1,0:T(8,128)(2,1)} %refs_2_), custom_call_target="tpu_custom_call" | custom-call | bytes 4980736 | tf_op jit(solution)/shard_map/pallas_call | solution.py:178
  120.5 1.5 fusion.8
  122.1 1.5 fusion.10
  123.6 0.4 convolution_convert_fusion.1
  124.1 0.2 reshape_reshape.3
  124.3 0.7 fusion.36
  125.0 2.0 fusion.61
  127.0 0.8 fusion.26
  127.8 0.3 copy.45
  128.2 0.3 reshape.162
  128.5 0.4 copy-done.9
  128.8 1.4 fusion.63
  130.4 0.6 copy.50
  131.0 50.0 %shard_map.205 = (bf16[32,2,16,704]{3,2,1,0:T(8,128)(2,1)}, bf16[32,2,16,704]{3,2,1,0:T(8,128)(2,1)}) custom-call(bf16[16,704]{1,0:T(8,128)(2,1)} %refs_0_.1, bf16[16,704]{1,0:T(8,128)(2,1)} %bitcast.90), custom_call_target="tpu_custom_call" | custom-call | bytes 5767168 | tf_op jit(solution)/shard_map/pallas_call | solution.py:178
  181.1 1.7 multiply_reduce_fusion.1
  182.8 0.4 multiply_convert_fusion.1
  183.2 1.0 copy-done.19
  184.2 2.1 fusion.64
  186.3 5.4 %fusion.31 = bf16[512,1024]{1,0:T(8,128)(2,1)} fusion(bf16[1024,704]{1,0:T(8,128)(2,1)} %bitcast.95, bf16[512,1024]{1,0:T(8,128)(2,1)S(1)} %bitcast.83, bf16[1024,704]{1,0:T(8,128)(2,1)} %bitcast.94, f32[512,704]{0,1:T(8,128)} %fusion.64), kind=kOutput, calls=%fused_computation.59 | convolution fusion | flops 1479999488 | bytes 6422528 | tf_op jit(solution)/shard_map/rk,ok->ro/dot_general | solution.py:263
  191.8 31.5 %shard_map.206 = bf16[32,2,16,768]{3,2,1,0:T(8,128)(2,1)} custom-call(bf16[16,768]{1,0:T(8,128)(2,1)} %bitcast.88), custom_call_target="tpu_custom_call" | custom-call | bytes 3145728 | tf_op jit(solution)/shard_map/pallas_call | solution.py:178
  223.3 19.8 %all-reduce.8.cloned.1.call-done = bf16[8,64,1024]{2,1,0:T(8,128)(2,1)} async-done(((bf16[8,64,1024]{2,1,0:T(8,128)(2,1)}), bf16[8,64,1024]{2,1,0:T(8,128)(2,1)}) %all-reduce.8.cloned.1.call-update) | async-done | bytes 1048592 | tf_op jit(solution)/shard_map/psum | solution.py:198
  243.1 1.8 multiply_reduce_fusion
  244.9 0.7 dynamic-slice_convert_fusion
  245.6 0.2 multiply_convert_fusion
  245.8 0.5 copy-done.8
  246.3 1.0 convolution_convert_fusion
  247.3 0.4 reshape.171
  247.7 1.0 copy.47
  (55 shorter events, 0.6 us)
Async XLA Ops:
  7.2 2.2 copy-start.17
  7.2 2.3 copy-start.16
  7.2 113.3 %all-reduce.4.cloned.1.call-start = ((), (), s32[]{:S(2)}) async-start(), calls=%async_computation | async-start | bytes 2097152 | tf_op jit(solution)/shard_map/psum | solution.py:198
  18.3 7.1 %copy-start.12 = (s32[8,64]{1,0:T(8,128)S(1)}, s32[8,64]{1,0:T(8,128)}, u32[]{:S(2)}) copy-start(s32[8,64]{1,0:T(8,128)} %param.24) | copy-start | bytes 6148
  25.4 2.5 copy-start.21
  28.6 1.2 copy-start.4
  29.8 2.0 copy-start.1
  30.3 2.0 copy-start.5
  30.3 3.0 %copy-start.3 = (bf16[8,1,512,256]{3,2,1,0:T(8,128)(2,1)S(1)}, bf16[8,1,512,256]{3,2,1,0:T(8,128)(2,1)}, u32[]{:S(2)}) copy-start(bf16[8,1,512,256]{3,2,1,0:T(8,128)(2,1)} %get-tuple-element.31) | copy-start | bytes 6291460
  35.9 4.1 %copy-start.6 = (f32[8,4,64,64]{2,3,1,0:T(8,128)S(1)}, f32[8,4,64,64]{2,3,1,0:T(8,128)}, u32[]{:S(2)}) copy-start(f32[8,4,64,64]{2,3,1,0:T(8,128)} %copy-done.5) | copy-start | bytes 1572868
  40.8 24.2 %copy-start.10 = (bf16[8,16,1024]{2,1,0:T(8,128)(2,1)S(1)}, bf16[8,16,1024]{2,1,0:T(8,128)(2,1)}, u32[]{:S(2)}) copy-start(bf16[8,16,1024]{2,1,0:T(8,128)(2,1)} %param.20) | copy-start | bytes 786436
  66.3 114.7 %all-reduce.6.cloned.1.call-start = ((), (), s32[]{:S(2)}) async-start(), calls=%async_computation.1 | async-start | bytes 2097152 | tf_op jit(solution)/shard_map/psum | solution.py:198
  73.8 46.6 %copy-start.18 = (s32[8]{0:T(128)S(1)}, s32[8]{0:T(128)}, u32[]{:S(2)}) copy-start(s32[8]{0:T(128)} %param.27) | copy-start | bytes 100
  73.8 48.2 %copy-start.13 = (f32[1024]{0:T(1024)S(1)}, f32[1024]{0:T(1024)}, u32[]{:S(2)}) copy-start(f32[1024]{0:T(1024)} %param.30) | copy-start | bytes 12292
  120.4 3.2 %copy-start.20 = (bf16[32,2,16,256]{3,2,1,0:T(8,128)(2,1)S(1)}, bf16[32,2,16,256]{3,2,1,0:T(8,128)(2,1)}, u32[]{:S(2)}) copy-start(bf16[32,2,16,256]{3,2,1,0:T(8,128)(2,1)} %get-tuple-element.16) | copy-start | bytes 1572868
  125.0 2.0 copy-start.7
  127.8 1.0 copy-start.9
  128.1 2.2 copy-start.11
  128.1 52.9 %copy-start = (bf16[8,64,1024]{2,1,0:T(8,128)(2,1)S(1)}, bf16[8,64,1024]{2,1,0:T(8,128)(2,1)}, u32[]{:S(2)}) copy-start(bf16[8,64,1024]{2,1,0:T(8,128)(2,1)} %all-reduce.4.cloned.1.call-done) | copy-start | bytes 3145732
  128.8 54.0 %copy-start.14 = (f32[1024]{0:T(1024)S(1)}, f32[1024]{0:T(1024)}, u32[]{:S(2)}) copy-start(f32[1024]{0:T(1024)} %param.31) | copy-start | bytes 12292
  130.3 112.8 %all-reduce.8.cloned.1.call-start = ((), (), s32[]{:S(2)}) async-start(), calls=%async_computation.2 | async-start | bytes 2097152 | tf_op jit(solution)/shard_map/psum | solution.py:198
  181.0 1.8 copy-start.2
  182.8 1.4 copy-start.19
  223.3 22.3 %copy-start.15 = (f32[1024]{0:T(1024)S(1)}, f32[1024]{0:T(1024)}, u32[]{:S(2)}) copy-start(f32[1024]{0:T(1024)} %param.32) | copy-start | bytes 12292
  244.8 1.5 copy-start.8
Sparse Core Ops, SparseCore 0:
  66.4 49.3 all-reduce.3
  130.4 50.5 all-reduce.5
  191.9 51.1 all-reduce.7

commit v2 on v1

--- a/solution.py
+++ b/solution.py
@@ -87,10 +87,17 @@
     return attended.astype(jnp.bfloat16).reshape(requests * draft_slots, head_width)
 
 
-def gather_kernel(n_chips, n_in, *refs):
+def gather_kernel(n_chips, n_in, n_grp, *refs):
     srcs = refs[:n_in]
-    outs = refs[n_in:2 * n_in]
-    send_sems, recv_sems, local_sems, fwd_send, fwd_recv = refs[2 * n_in:]
+    if n_grp:
+        summand = refs[n_in]
+        outs = refs[n_in + 1:2 * n_in + 1]
+        summed = refs[2 * n_in + 1]
+        rest = refs[2 * n_in + 2:]
+        send_sems, recv_sems, local_sems, fwd_send, fwd_recv, parts_in, rs_send, rs_recv, ag_send, ag_recv = rest
+    else:
+        outs = refs[n_in:2 * n_in]
+        send_sems, recv_sems, local_sems, fwd_send, fwd_recv = refs[2 * n_in:]
     grp = lax.axis_index("grp")
     me = lax.axis_index("tok")
     chip = me // 2
@@ -103,7 +110,11 @@
         peer = lax.rem(chip + k, n_chips) * 2 + core
         pl.semaphore_signal(barrier, inc=1, device_id=(grp, peer), device_id_type=mesh_id)
     pl.semaphore_signal(barrier, inc=1, device_id=(grp, sibling), device_id_type=mesh_id)
-    pl.semaphore_wait(barrier, n_chips)
+    for j in range(1, max(n_grp, 1)):
+        pl.semaphore_signal(
+            barrier, inc=1, device_id=(lax.rem(grp + j, n_grp), me), device_id_type=mesh_id
+        )
+    pl.semaphore_wait(barrier, n_chips + max(n_grp - 1, 0))
 
     locals_ = [
         pltpu.make_async_copy(srcs[i], outs[i].at[chip, core], local_sems.at[i]) for i in range(n_in)
@@ -129,6 +140,46 @@
 
     lax.fori_loop(1, n_chips, send, 0)
 
+    if n_grp:
+        quarter = summand.shape[1] // n_grp
+
+        def scatter(j):
+            target = lax.rem(grp + j, n_grp)
+            return pltpu.make_async_remote_copy(
+                src_ref=summand.at[:, pl.ds(target * quarter, quarter)],
+                dst_ref=parts_in.at[grp],
+                send_sem=rs_send.at[j],
+                recv_sem=rs_recv.at[grp],
+                device_id=(target, me),
+                device_id_type=mesh_id,
+            )
+
+        for j in range(1, n_grp):
+            scatter(j).start()
+        for j in range(1, n_grp):
+            scatter(j).wait_send()
+            source = lax.rem(grp + j, n_grp)
+            pltpu.make_async_copy(parts_in.at[source], parts_in.at[source], rs_recv.at[source]).wait()
+        mine = pl.ds(grp * quarter, quarter)
+        total = summand[:, mine, :].astype(jnp.float32)
+        for j in range(1, n_grp):
+            total = total + parts_in[lax.rem(grp + j, n_grp)].astype(jnp.float32)
+        summed[:, mine, :] = total.astype(summed.dtype)
+
+        def spread(j):
+            target = lax.rem(grp + j, n_grp)
+            return pltpu.make_async_remote_copy(
+                src_ref=summed.at[:, mine],
+                dst_ref=summed.at[:, mine],
+                send_sem=ag_send.at[j],
+                recv_sem=ag_recv.at[grp],
+                device_id=(target, me),
+                device_id_type=mesh_id,
+            )
+
+        for j in range(1, n_grp):
+            spread(j).start()
+
     def arrive(k, carry):
         other = lax.rem(chip + k, n_chips)
         for i in range(n_in):
@@ -169,30 +220,58 @@
 
     lax.fori_loop(0, n_chips, land, 0)
 
-
-def fetch_group(n_tok, collective_id, parts, after):
-    parts = list(lax.optimization_barrier((tuple(parts), after))[0])
+    if n_grp:
+        for j in range(1, n_grp):
+            spread(j).wait_send()
+            source = lax.rem(grp + j, n_grp)
+            rows = pl.ds(source * quarter, quarter)
+            pltpu.make_async_copy(summed.at[:, rows], summed.at[:, rows], ag_recv.at[source]).wait()
+
+
+def fetch_group(n_tok, collective_id, parts, after, summand=None):
+    if summand is None:
+        parts = list(lax.optimization_barrier((tuple(parts), after))[0])
     n_chips = n_tok // 2
     n_in = len(parts)
+    n_grp = 0 if summand is None else lax.axis_size("grp")
     moved = 2 * n_tok * sum(p.size for p in parts) * parts[0].dtype.itemsize
-    gathered = pl.pallas_call(
-        functools.partial(gather_kernel, n_chips, n_in),
-        out_shape=tuple(
-            jax.ShapeDtypeStruct((n_chips, 2) + p.shape, p.dtype) for p in parts
-        ),
-        in_specs=[pl.BlockSpec(memory_space=pl.ANY)] * n_in,
-        out_specs=tuple(pl.BlockSpec(memory_space=pl.ANY) for _ in parts),
-        scratch_shapes=[
-            pltpu.SemaphoreType.DMA((n_in, n_chips)),
-            pltpu.SemaphoreType.DMA((n_in, n_chips)),
-            pltpu.SemaphoreType.DMA((n_in,)),
-            pltpu.SemaphoreType.DMA((n_in, n_chips)),
-            pltpu.SemaphoreType.DMA((n_in, n_chips)),
-        ],
+    out_shape = [jax.ShapeDtypeStruct((n_chips, 2) + p.shape, p.dtype) for p in parts]
+    out_specs = [pl.BlockSpec(memory_space=pl.ANY) for _ in parts]
+    in_specs = [pl.BlockSpec(memory_space=pl.ANY)] * n_in
+    operands = list(parts)
+    scratch = [
+        pltpu.SemaphoreType.DMA((n_in, n_chips)),
+        pltpu.SemaphoreType.DMA((n_in, n_chips)),
+        pltpu.SemaphoreType.DMA((n_in,)),
+        pltpu.SemaphoreType.DMA((n_in, n_chips)),
+        pltpu.SemaphoreType.DMA((n_in, n_chips)),
+    ]
+    if n_grp:
+        requests, slots, width = summand.shape
+        operands.append(summand)
+        in_specs.append(pl.BlockSpec(memory_space=pltpu.VMEM))
+        out_shape.append(jax.ShapeDtypeStruct(summand.shape, summand.dtype))
+        out_specs.append(pl.BlockSpec(memory_space=pltpu.VMEM))
+        scratch += [
+            pltpu.VMEM((n_grp, requests, slots // n_grp, width), summand.dtype),
+            pltpu.SemaphoreType.DMA((n_grp,)),
+            pltpu.SemaphoreType.DMA((n_grp,)),
+            pltpu.SemaphoreType.DMA((n_grp,)),
+            pltpu.SemaphoreType.DMA((n_grp,)),
+        ]
+    results = pl.pallas_call(
+        functools.partial(gather_kernel, n_chips, n_in, n_grp),
+        out_shape=tuple(out_shape),
+        in_specs=in_specs,
+        out_specs=tuple(out_specs),
+        scratch_shapes=scratch,
         compiler_params=pltpu.CompilerParams(collective_id=collective_id, has_side_effects=True),
         cost_estimate=pl.CostEstimate(flops=0, transcendentals=0, bytes_accessed=moved),
-    )(*parts)
-    return [g.reshape((n_tok * g.shape[2],) + g.shape[3:]) for g in gathered]
+    )(*operands)
+    gathered = [g.reshape((n_tok * g.shape[2],) + g.shape[3:]) for g in results[:n_in]]
+    if n_grp:
+        return gathered, results[n_in]
+    return gathered
 
 def layer_sum(summand, base_full):
     return lax.psum(summand.astype(jnp.bfloat16), "grp").astype(jnp.float32) + base_full
@@ -243,10 +322,10 @@
     )
     summand = partial_value + placed
     n_tok = lax.axis_size("tok")
-    w_query_full, w_out_cross_t, w_gate_full = fetch_group(
-        n_tok, 0, (w_query_cross, w_out_cross.T, w_gate), summand
-    )
-    stream_one = layer_sum(summand, 0.0)
+    (w_query_full, w_out_cross_t, w_gate_full), summed = fetch_group(
+        n_tok, 0, (w_query_cross, w_out_cross.T, w_gate), None, summand.astype(jnp.bfloat16)
+    )
+    stream_one = summed.astype(jnp.float32)
     normed_one = normed_rows(stream_one, gain_cross)
     cross_query = jnp.dot(normed_one, w_query_full, preferred_element_type=jnp.float32)
     cross_query = cross_query.astype(jnp.bfloat16).reshape(requests, draft_slots, head_width)
@@ -254,17 +333,21 @@
     partial_value = jnp.einsum(
         "rk,ok->ro", cross_context, w_out_cross_t, preferred_element_type=jnp.float32
     )
-    w_up_full, w_down_t = fetch_group(n_tok, 1, (w_up, w_down.T), partial_value)
-    stream_two = layer_sum(partial_value.reshape(requests, draft_slots, model_width), stream_one)
+    (w_up_full, w_down_t), summed = fetch_group(
+        n_tok, 1, (w_up, w_down.T), None,
+        partial_value.reshape(requests, draft_slots, model_width).astype(jnp.bfloat16),
+    )
+    stream_two = summed.astype(jnp.float32) + stream_one
     normed_two = normed_rows(stream_two, gain_ffn)
     gate_part = jnp.dot(normed_two, w_gate_full, preferred_element_type=jnp.float32)
     up_part = jnp.dot(normed_two, w_up_full, preferred_element_type=jnp.float32)
     gated = (jax.nn.gelu(gate_part, approximate=True) * up_part).astype(jnp.bfloat16)
     partial_value = jnp.einsum("rk,ok->ro", gated, w_down_t, preferred_element_type=jnp.float32)
-    (w_qkv_full,) = fetch_group(
-        n_tok, 2, (w_qkv.reshape(w_qkv.shape[0], -1),), partial_value
-    )
-    stream_three = layer_sum(partial_value.reshape(requests, draft_slots, model_width), stream_two)
+    (w_qkv_full,), summed = fetch_group(
+        n_tok, 2, (w_qkv.reshape(w_qkv.shape[0], -1),), None,
+        partial_value.reshape(requests, draft_slots, model_width).astype(jnp.bfloat16),
+    )
+    stream_three = summed.astype(jnp.float32) + stream_two
     normed_three = normed_rows(stream_three, gain_next)
     projected = jnp.dot(
         normed_three,

time: 257 us -> 228 us (0.89)
  waiting for transfers between devices: 19.8 us -> 0 us
  between operations: 14.3 us -> 1.13 us
  Pallas kernels: 147 us -> 158 us
  local copies, waits for them, and re-layouts: 35.7 us -> 30.3 us
    psum x3 -> x0, waiting for transfers between devices: 19.8 us -> none  [layer_sum(): lax.psum(summand.astype(jnp.bfloat16), 'grp').astype(jnp.float32)]
    pallas_call x4, Pallas kernels: 147 us -> 158 us  [fetch_group(): pl.pallas_call(functools.partial(gather_kernel, n_chips, n_in, n_grp), ou...]
  transfers between devices with their start and end apart: 3 -> 0, of which waited for: 1 -> 0; matrix products, arithmetic and copies ran while one was open for 5% -> 0% of each run, Pallas kernels for 49% -> 0%
where the time goes in v2:
time: 228 us
  Pallas kernels  158 us (69%)
  local copies, waits for them, and re-layouts  30.3 us (13%)
  matrix products  25.7 us (11%)
  other arithmetic  12 us (5%)
    pallas_call x4, Pallas kernels, fetch_group(): pl.pallas_call(functools.partial(gather_kernel, n_chips, n_in, n_grp), ou...  158 us
    slice x2, local copies, waits for them, and re-layouts, cross_attention(): enc_keys = cached[:, 0].reshape(requests, -1, local_heads, DH)  6.82 us
    slice x2, local copies, waits for them, and re-layouts, draft_attention(): cache_keys = cached[:, 0].reshape(requests, -1, local_heads, head_size)  6.77 us

profile of v2, /device:TPU:1, one launch (start us, length us, event | category | flops | bytes accessed | tf_op | source)
XLA Modules:
  0.0 227.5 jit_solution(15067784599050850574)
XLA Ops:
  0.6 3.9 %fusion.49 = (bf16[8,1,512,256]{3,2,1,0:T(8,128)(2,1)}, bf16[8,1,512,256]{3,2,1,0:T(8,128)(2,1)S(1)}) fusion(bf16[8,2,512,256]{3,2,1,0:T(8,128)(2,1)} %param.22), kind=kLoop, calls=%fused_computation.90 | loop fusion | bytes 8388608 | tf_op jit(solution)/shard_map/slice | solution.py:36
  4.5 2.4 %copy.41 = bf16[8,1,512,256]{2,3,0,1:T(8,128)(2,1)} copy(bf16[8,1,512,256]{3,2,1,0:T(8,128)(2,1)S(1)} %get-tuple-element.27) | data formatting | bytes 4194304 | tf_op jit(solution)/shard_map/slice | solution.py:37
  6.9 0.2 slice_reduce_fusion
  7.2 2.9 %copy.35 = bf16[8,1,512,256]{2,3,0,1:T(8,128)(2,1)S(1)} copy(bf16[8,1,512,256]{3,2,1,0:T(8,128)(2,1)} %get-tuple-element.26) | data formatting | bytes 4194304 | tf_op jit(solution)/shard_map/slice | solution.py:36
  10.1 1.2 fusion.50
  11.2 0.2 reshape_squeeze.21
  11.5 2.6 %fusion.3 = (f32[8,4,64]{2,1,0:T(4,128)S(1)}, f32[8,4,64,512]{3,2,1,0:T(8,128)}) fusion(f32[4]{0:T(128)S(1)} %slice_reduce_fusion, pred[8,512]{1,0:T(8,128)(4,1)S(1)} %iota_compare_fusion.5, bf16[8,512,4,64]{1,3,2,0:T(8,128)(2,1)S(1)} %bitcast.74, bf16[8,64,4,64]{3,2,1,0:T(4,128)(2,1)S(1)} %reshape_squeeze.21), kind=kOutput, calls=%fused_computation.9 | convolution fusion | flops 137361408 | bytes 6565904 | tf_op jit(solution)/shard_map/rihd,rphd->rhip/dot_general | solution.py:38
  14.1 2.6 %fusion.1 = f32[8,64,64,4]{2,3,1,0:T(4,128)S(1)} fusion(s32[8,64,64]{2,1,0:T(8,128)S(1)} %copy-done.19, f32[32,4]{0,1:T(4,128)S(1)} %copy-done.12), kind=kOutput, calls=%fused_computation.2 | convolution fusion | flops 51380224 | bytes 655872 | tf_op jit(solution)/shard_map/rijb,bh->rhij/dot_general | solution.py:47
  16.7 0.3 copy.40
  17.1 0.2 reshape_squeeze.23
  17.4 0.5 convolution_minimum_fusion.6
  17.9 0.4 convolution_minimum_fusion.5
  18.3 0.4 convolution_minimum_fusion.4
  18.7 0.4 convolution_minimum_fusion.3
  19.1 0.4 convolution_minimum_fusion.2
  19.5 0.4 convolution_minimum_fusion.1
  19.9 0.4 fusion.29
  20.3 0.2 copy.37
  20.5 0.4 fusion.51
  21.0 3.7 %fusion.7 = f32[8,4,64]{2,1,0:T(4,128)S(1)} fusion(f32[8,4,64,512]{3,2,1,0:T(8,128)} %get-tuple-element.32, f32[8,4,64]{2,1,0:T(4,128)S(1)} %max.8, f32[4]{0:T(128)S(1)} %slice_reduce_fusion, pred[8,512]{1,0:T(8,128)(4,1)S(1)} %iota_compare_fusion.5), kind=kLoop, calls=%fused_computation.12 | loop fusion | flops 4192256 | bytes 4214800 | tf_op jit(solution)/shard_map/reduce_sum | solution.py:60
  24.7 0.2 fusion.30
  25.0 2.2 fusion.14
  27.2 0.2 reshape_squeeze.25
  27.4 1.6 fusion.27
  29.1 0.4 copy.44
  29.5 0.3 dot_general.81
  29.8 22.2 %shard_map.203 = bf16[32,2,16,256]{3,2,1,0:T(8,128)(2,1)} custom-call(bf16[16,256]{1,0:T(8,128)(2,1)} %bitcast.89), custom_call_target="tpu_custom_call" | custom-call | bytes 1048576 | tf_op jit(solution)/shard_map/pallas_call | solution.py:262
  52.1 1.5 fusion.53
  53.6 0.1 add_dynamic-update-slice_fusion
  53.7 1.1 convert_element_type.81.refs_3_
  54.8 45.0 %shard_map.204 = (bf16[32,2,16,256]{3,2,1,0:T(8,128)(2,1)}, bf16[32,2,16,256]{3,2,1,0:T(8,128)(2,1)}, bf16[32,2,16,704]{3,2,1,0:T(8,128)(2,1)}, bf16[8,64,1024]{2,1,0:T(8,128)(2,1)}) custom-call(bf16[16,256]{1,0:T(8,128)(2,1)} %refs_0_.2, bf16[16,256]{1,0:T(8,128)(2,1)} %bitcast.90, bf16[16,704]{1,0:T(8,128)(2,1)} %refs_2_.1, ...), custom_call_target="tpu_custom_call" | custom-call | bytes 4980736 | tf_op jit(solution)/shard_map/pallas_call | solution.py:262
  99.9 3.9 %fusion.48 = (bf16[8,1,512,256]{3,2,1,0:T(8,128)(2,1)}, bf16[8,1,512,256]{3,2,1,0:T(8,128)(2,1)S(1)}) fusion(bf16[8,2,512,256]{3,2,1,0:T(8,128)(2,1)} %param.23), kind=kLoop, calls=%fused_computation.89 | loop fusion | bytes 8388608 | tf_op jit(solution)/shard_map/slice | solution.py:76
  103.7 2.4 %copy.47 = bf16[8,1,512,256]{2,3,0,1:T(8,128)(2,1)} copy(bf16[8,1,512,256]{3,2,1,0:T(8,128)(2,1)S(1)} %get-tuple-element.25) | data formatting | bytes 4194304 | tf_op jit(solution)/shard_map/slice | solution.py:77
  106.1 2.9 %copy.45 = bf16[8,1,512,256]{2,3,0,1:T(8,128)(2,1)S(1)} copy(bf16[8,1,512,256]{3,2,1,0:T(8,128)(2,1)} %get-tuple-element.24) | data formatting | bytes 4194304 | tf_op jit(solution)/shard_map/slice | solution.py:76
  109.1 0.3 fusion.8
  109.4 0.3 fusion.10
  109.7 0.4 copy-done.18
  110.1 0.4 convolution_convert_fusion.3
  110.6 1.0 reshape_reshape.3
  111.6 1.7 fusion.31
  113.4 1.9 fusion.52
  115.4 0.8 fusion.26
  116.2 0.4 copy.48
  116.6 0.3 dot_general.86
  116.9 0.3 copy-done.5
  117.2 1.4 convolution_convert_fusion.1.refs_2_
  118.7 52.4 %shard_map.205 = (bf16[32,2,16,704]{3,2,1,0:T(8,128)(2,1)}, bf16[32,2,16,704]{3,2,1,0:T(8,128)(2,1)}, bf16[8,64,1024]{2,1,0:T(8,128)(2,1)}) custom-call(bf16[16,704]{1,0:T(8,128)(2,1)} %refs_0_.3, bf16[16,704]{1,0:T(8,128)(2,1)} %bitcast.88, bf16[8,64,1024]{2,1,0:T(8,128)(2,1)} %convolution_convert_fusion.1.refs_2_), custom_call_target="tpu_custom_call" | custom-call | bytes 5767168 | tf_op jit(solution)/shard_map/pallas_call | solution.py:262
  171.1 0.6 copy.56
  171.7 1.6 multiply_reduce_fusion.1
  173.3 0.4 multiply_convert_fusion.1
  173.7 1.0 copy-done.15
  174.7 1.0 fusion.54
  175.7 0.4 copy-done.17
  176.1 2.1 fusion.22
  178.2 1.4 copy.49
  179.6 3.4 %convolution_convert_fusion.refs_1_ = bf16[8,64,1024]{2,1,0:T(8,128)(2,1)} fusion(bf16[8,64,704]{2,1,0:T(8,128)(2,1)S(1)} %bitcast.84, bf16[1024,704,1]{1,0,2:T(8,128)(2,1)} %bitcast.92), kind=kOutput, calls=%fused_computation.29 | convolution fusion | flops 738721792 | bytes 3211264 | tf_op jit(solution)/shard_map/rk,ok->ro/dot_general | solution.py:345
  183.0 38.8 %shard_map.206 = (bf16[32,2,16,768]{3,2,1,0:T(8,128)(2,1)}, bf16[8,64,1024]{2,1,0:T(8,128)(2,1)}) custom-call(bf16[16,768]{1,0:T(8,128)(2,1)} %bitcast.86, bf16[8,64,1024]{2,1,0:T(8,128)(2,1)} %convolution_convert_fusion.refs_1_), custom_call_target="tpu_custom_call" | custom-call | bytes 3145728 | tf_op jit(solution)/shard_map/pallas_call | solution.py:262
  221.9 1.8 multiply_reduce_fusion
  223.6 0.7 dynamic-slice_convert_fusion
  224.4 0.2 multiply_convert_fusion
  224.6 0.5 copy-done.16
  225.1 1.0 convolution_convert_fusion.2
  226.1 0.4 reshape.169
  226.5 1.0 copy.51
  (46 shorter events, 0.3 us)
Async XLA Ops:
  4.5 2.4 %copy-start.12 = (f32[32,4]{0,1:T(4,128)S(1)}, f32[32,4]{0,1:T(4,128)}, u32[]{:S(2)}) copy-start(f32[32,4]{0,1:T(4,128)} %param.29) | copy-start | bytes 1540
  4.5 2.6 %copy-start.13 = (s32[8]{0:T(128)S(1)}, s32[8]{0:T(128)}, u32[]{:S(2)}) copy-start(s32[8]{0:T(128)} %param.26) | copy-start | bytes 100
  11.5 2.6 %copy-start.19 = (s32[8,64,64]{2,1,0:T(8,128)S(1)}, s32[8,64,64]{2,1,0:T(8,128)}, u32[]{:S(2)}) copy-start(s32[8,64,64]{2,1,0:T(8,128)} %param.28) | copy-start | bytes 393220
  14.1 3.2 %copy-start.8 = (s32[8,64]{1,0:T(8,128)S(1)}, s32[8,64]{1,0:T(8,128)}, u32[]{:S(2)}) copy-start(s32[8,64]{1,0:T(8,128)} %param.24) | copy-start | bytes 6148
  17.4 2.5 %copy-start.20 = (s32[8]{0:T(128)S(1)}, s32[8]{0:T(128)}, u32[]{:S(2)}) copy-start(s32[8]{0:T(128)} %param.25) | copy-start | bytes 100
  20.5 4.4 %copy-start.3 = (bf16[8,1,512,256]{2,3,0,1:T(8,128)(2,1)S(1)}, bf16[8,1,512,256]{2,3,0,1:T(8,128)(2,1)}, u32[]{:S(2)}) copy-start(bf16[8,1,512,256]{2,3,0,1:T(8,128)(2,1)} %copy.41) | copy-start | bytes 6291460
  21.0 4.0 %copy-start.1 = (f32[8,4,64,512]{3,2,1,0:T(8,128)S(1)}, f32[8,4,64,512]{3,2,1,0:T(8,128)}, u32[]{:S(2)}) copy-start(f32[8,4,64,512]{3,2,1,0:T(8,128)} %get-tuple-element.32) | copy-start | bytes 12582916
  29.5 24.1 %copy-start.6 = (bf16[8,16,1024]{2,1,0:T(8,128)(2,1)S(1)}, bf16[8,16,1024]{2,1,0:T(8,128)(2,1)}, u32[]{:S(2)}) copy-start(bf16[8,16,1024]{2,1,0:T(8,128)(2,1)} %param.20) | copy-start | bytes 786436
  106.1 3.0 %copy-start = (bf16[8,64,1024]{2,1,0:T(8,128)(2,1)S(1)}, bf16[8,64,1024]{2,1,0:T(8,128)(2,1)}, u32[]{:S(2)}) copy-start(bf16[8,64,1024]{2,1,0:T(8,128)(2,1)} %get-tuple-element.11) | copy-start | bytes 3145732
  106.1 3.3 %copy-start.9 = (f32[1024]{0:T(1024)S(1)}, f32[1024]{0:T(1024)}, u32[]{:S(2)}) copy-start(f32[1024]{0:T(1024)} %param.30) | copy-start | bytes 12292
  109.1 1.0 copy-start.18
  111.6 1.7 copy-start.14
  113.4 2.0 copy-start.4
  116.2 1.0 copy-start.5
  116.6 54.5 %copy-start.7 = (bf16[16,3,256]{2,0,1:T(8,128)(2,1)S(1)}, bf16[16,3,256]{2,0,1:T(8,128)(2,1)}, u32[]{:S(2)}) copy-start(bf16[16,3,256]{2,0,1:T(8,128)(2,1)} %param.39) | copy-start | bytes 73732
  117.2 56.1 %copy-start.10 = (f32[1024]{0:T(1024)S(1)}, f32[1024]{0:T(1024)}, u32[]{:S(2)}) copy-start(f32[1024]{0:T(1024)} %param.31) | copy-start | bytes 12292
  171.0 2.3 %copy-start.2 = (bf16[8,64,1024]{2,1,0:T(8,128)(2,1)S(1)}, bf16[8,64,1024]{2,1,0:T(8,128)(2,1)}, u32[]{:S(2)}) copy-start(bf16[8,64,1024]{2,1,0:T(8,128)(2,1)} %get-tuple-element.14) | copy-start | bytes 3145732
  173.3 1.4 copy-start.15
  174.7 1.4 copy-start.17
  221.9 2.5 %copy-start.11 = (f32[1024]{0:T(1024)S(1)}, f32[1024]{0:T(1024)}, u32[]{:S(2)}) copy-start(f32[1024]{0:T(1024)} %param.32) | copy-start | bytes 12292
  223.6 1.5 copy-start.16

commit v3 on v2

--- a/solution.py
+++ b/solution.py
@@ -85,6 +85,49 @@
         "rhip,rphd->rihd", weights, enc_values, preferred_element_type=jnp.float32
     )
     return attended.astype(jnp.bfloat16).reshape(requests * draft_slots, head_width)
+
+
+def cross_kernel(len_ref, q_ref, kv_ref, o_ref):
+    length = len_ref[pl.program_id(0)]
+    q = q_ref[0]
+    keys = kv_ref[0, 0]
+    values = kv_ref[0, 1]
+    live = lax.broadcasted_iota(jnp.int32, (q.shape[0], keys.shape[0]), 1) < length
+    for h in range(q.shape[1] // DH):
+        cols = slice(h * DH, (h + 1) * DH)
+        scores = lax.dot_general(
+            q[:, cols], keys[:, cols], (((1,), (1,)), ((), ())), preferred_element_type=jnp.float32
+        )
+        scores = jnp.where(live, scores, -1e30)
+        exp_scores = jnp.exp(scores - scores.max(-1, keepdims=True))
+        weights = (exp_scores / exp_scores.sum(-1, keepdims=True)).astype(jnp.bfloat16)
+        o_ref[0, :, cols] = jnp.dot(
+            weights, values[:, cols], preferred_element_type=jnp.float32
+        ).astype(o_ref.dtype)
+
+
+def cross_attention_kernel(query_rows, cached, length):
+    requests, draft_slots, head_width = query_rows.shape
+    positions = cached.shape[2]
+    attended = pl.pallas_call(
+        cross_kernel,
+        out_shape=jax.ShapeDtypeStruct(query_rows.shape, jnp.bfloat16),
+        grid_spec=pltpu.PrefetchScalarGridSpec(
+            num_scalar_prefetch=1,
+            grid=(requests,),
+            in_specs=[
+                pl.BlockSpec((1, draft_slots, head_width), lambda r, lens: (r, 0, 0)),
+                pl.BlockSpec((1, 2, positions, head_width), lambda r, lens: (r, 0, 0, 0)),
+            ],
+            out_specs=pl.BlockSpec((1, draft_slots, head_width), lambda r, lens: (r, 0, 0)),
+        ),
+        cost_estimate=pl.CostEstimate(
+            flops=4 * requests * draft_slots * positions * head_width,
+            transcendentals=requests * draft_slots * positions * (head_width // DH),
+            bytes_accessed=2 * cached.size + 4 * query_rows.size,
+        ),
+    )(length, query_rows, cached)
+    return attended.reshape(requests * draft_slots, head_width)
 
 
 def gather_kernel(n_chips, n_in, n_grp, *refs):
@@ -329,7 +372,7 @@
     normed_one = normed_rows(stream_one, gain_cross)
     cross_query = jnp.dot(normed_one, w_query_full, preferred_element_type=jnp.float32)
     cross_query = cross_query.astype(jnp.bfloat16).reshape(requests, draft_slots, head_width)
-    cross_context = cross_attention(cross_query, cross_cache, enc_len)
+    cross_context = cross_attention_kernel(cross_query, cross_cache, enc_len)
     partial_value = jnp.einsum(
         "rk,ok->ro", cross_context, w_out_cross_t, preferred_element_type=jnp.float32
     )

time: 228 us -> 232 us (1.018)
  Pallas kernels: 158 us -> 174 us
  local copies, waits for them, and re-layouts: 30.3 us -> 18.6 us
    pallas_call x0 -> x1, Pallas kernels: none -> 15.6 us  [cross_attention_kernel(): pl.pallas_call(cross_kernel, out_shape=jax.ShapeDtypeStruct(query_rows.sh...]
    slice x3 -> x0, local copies, waits for them, and re-layouts: 9.2 us -> none  [the longest x2 6.82 us: cross_attention(): enc_keys = cached[:, 0].reshape(requests, -1, local_heads, DH)]
    dot_general x2 -> x0, matrix products: 2.5 us -> none  [the longest x1 1.74 us: cross_attention(): jnp.einsum('rihd,rphd->rhip', queries, enc_keys, preferred_element_type=j...]
where the time goes in v3:
time: 232 us; the launch traced here: 231 us
  Pallas kernels  174 us (75%)
  matrix products  24.9 us (11%)
  local copies, waits for them, and re-layouts  18.6 us (8%)
  other arithmetic  12.5 us (5%)
    pallas_call x4, Pallas kernels, fetch_group(): pl.pallas_call(functools.partial(gather_kernel, n_chips, n_in, n_grp), ou...  158 us
    pallas_call x1, Pallas kernels, cross_attention_kernel(): pl.pallas_call(cross_kernel, out_shape=jax.ShapeDtypeStruct(query_rows.sh...  15.6 us
    slice x2, local copies, waits for them, and re-layouts, draft_attention(): cache_keys = cached[:, 0].reshape(requests, -1, local_heads, head_size)  6.76 us
    reduce_sum x3, other arithmetic, rms_scale(): mean_square = jnp.mean(stream * stream, axis=-1, keepdims=True)  4.97 us

profile of v3, /device:TPU:1, one launch (start us, length us, event | category | flops | bytes accessed | tf_op | source)
XLA Modules:
  0.0 231.1 jit_solution(1088808846694349666)
XLA Ops:
  0.6 3.9 %fusion.36 = (bf16[8,1,512,256]{3,2,1,0:T(8,128)(2,1)}, bf16[8,1,512,256]{3,2,1,0:T(8,128)(2,1)S(1)}) fusion(bf16[8,2,512,256]{3,2,1,0:T(8,128)(2,1)} %param.22), kind=kLoop, calls=%fused_computation.75 | loop fusion | bytes 8388608 | tf_op jit(solution)/shard_map/slice | solution.py:36
  4.5 2.4 %copy.38 = bf16[8,1,512,256]{2,3,0,1:T(8,128)(2,1)} copy(bf16[8,1,512,256]{3,2,1,0:T(8,128)(2,1)S(1)} %get-tuple-element.25) | data formatting | bytes 4194304 | tf_op jit(solution)/shard_map/slice | solution.py:37
  6.9 0.2 slice_reduce_fusion
  7.1 0.1 iota_compare_fusion.5
  7.2 2.9 %copy.32 = bf16[8,1,512,256]{2,3,0,1:T(8,128)(2,1)S(1)} copy(bf16[8,1,512,256]{3,2,1,0:T(8,128)(2,1)} %get-tuple-element.24) | data formatting | bytes 4194304 | tf_op jit(solution)/shard_map/slice | solution.py:36
  10.0 1.2 fusion.37
  11.2 0.2 reshape_squeeze.15
  11.4 0.0 copy-start.17
  11.5 2.6 %fusion.2 = (f32[8,4,64]{2,1,0:T(4,128)S(1)}, f32[8,4,64,512]{3,2,1,0:T(8,128)}) fusion(f32[4]{0:T(128)S(1)} %slice_reduce_fusion, pred[8,512]{1,0:T(8,128)(4,1)S(1)} %iota_compare_fusion.5, bf16[8,512,4,64]{1,3,2,0:T(8,128)(2,1)S(1)} %bitcast.69, bf16[8,64,4,64]{3,2,1,0:T(4,128)(2,1)S(1)} %reshape_squeeze.15), kind=kOutput, calls=%fused_computation.6 | convolution fusion | flops 137361408 | bytes 6565904 | tf_op jit(solution)/shard_map/rihd,rphd->rhip/dot_general | solution.py:38
  14.1 0.0 copy-done.17
  14.1 2.6 %fusion = f32[8,64,64,4]{2,3,1,0:T(4,128)S(1)} fusion(s32[8,64,64]{2,1,0:T(8,128)S(1)} %copy-done.17, f32[32,4]{0,1:T(4,128)S(1)} %copy-done.11), kind=kOutput, calls=%fused_computation.1 | convolution fusion | flops 51380224 | bytes 655872 | tf_op jit(solution)/shard_map/rijb,bh->rhij/dot_general | solution.py:47
  16.7 0.3 copy.37
  17.1 0.2 reshape_squeeze.17
  17.3 0.0 copy-start.18
  17.3 0.5 convolution_minimum_fusion.6
  17.9 0.4 convolution_minimum_fusion.5
  18.3 0.4 convolution_minimum_fusion.4
  18.6 0.4 convolution_minimum_fusion.3
  19.0 0.4 convolution_minimum_fusion.2
  19.4 0.4 convolution_minimum_fusion.1
  19.8 0.1 iota_compare_fusion.6
  19.9 0.4 fusion.20
  20.3 0.2 copy.34
  20.5 0.4 fusion.38
  21.0 0.0 copy-start.1
  21.0 3.7 %fusion.3 = f32[8,4,64]{2,1,0:T(4,128)S(1)} fusion(f32[8,4,64,512]{3,2,1,0:T(8,128)} %get-tuple-element.30, f32[8,4,64]{2,1,0:T(4,128)S(1)} %max.8, f32[4]{0:T(128)S(1)} %slice_reduce_fusion, pred[8,512]{1,0:T(8,128)(4,1)S(1)} %iota_compare_fusion.5), kind=kLoop, calls=%fused_computation.7 | loop fusion | flops 4192256 | bytes 4214800 | tf_op jit(solution)/shard_map/reduce_sum | solution.py:60
  24.7 0.2 fusion.21
  24.9 2.2 fusion.7
  27.2 0.2 reshape_squeeze.19
  27.4 1.6 fusion.18
  29.0 0.4 copy.41
  29.5 0.0 copy-start.5
  29.5 0.3 dot_general.73
  29.8 22.2 %shard_map.203 = bf16[32,2,16,256]{3,2,1,0:T(8,128)(2,1)} custom-call(bf16[16,256]{1,0:T(8,128)(2,1)} %bitcast.83), custom_call_target="tpu_custom_call" | custom-call | bytes 1048576 | tf_op jit(solution)/shard_map/pallas_call | solution.py:305
  52.0 1.5 fusion.39
  53.6 0.1 add_dynamic-update-slice_fusion
  53.7 0.0 copy-start.8
  53.7 1.1 convert_element_type.72.refs_3_
  54.8 45.0 %shard_map.204 = (bf16[32,2,16,256]{3,2,1,0:T(8,128)(2,1)}, bf16[32,2,16,256]{3,2,1,0:T(8,128)(2,1)}, bf16[32,2,16,704]{3,2,1,0:T(8,128)(2,1)}, bf16[8,64,1024]{2,1,0:T(8,128)(2,1)}) custom-call(bf16[16,256]{1,0:T(8,128)(2,1)} %refs_0_.2, bf16[16,256]{1,0:T(8,128)(2,1)} %bitcast.84, bf16[16,704]{1,0:T(8,128)(2,1)} %refs_2_.1, ...), custom_call_target="tpu_custom_call" | custom-call | bytes 4980736 | tf_op jit(solution)/shard_map/pallas_call | solution.py:305
  99.9 1.6 fusion.4
  101.5 1.5 fusion.6
  103.0 1.1 convolution_convert_fusion.3
  104.1 15.6 %shard_map.205 = bf16[8,64,256]{2,1,0:T(8,128)(2,1)} custom-call(s32[8]{0:T(128)} %len_ref.1, bf16[8,64,256]{2,1,0:T(8,128)(2,1)} %bitcast.79, bf16[8,2,512,256]{3,2,1,0:T(8,128)(2,1)} %kv_ref.1), custom_call_target="tpu_custom_call" | custom-call | flops 268435456 | bytes 4718592 | tf_op jit(solution)/shard_map/pallas_call | solution.py:112
  119.8 0.0 copy-start.9
  119.8 2.5 %convolution_convert_fusion.1.refs_2_ = bf16[8,64,1024]{2,1,0:T(8,128)(2,1)} fusion(bf16[8,64,256]{2,1,0:T(8,128)(2,1)} %shard_map.205, bf16[1024,256,1]{1,0,2:T(8,128)(2,1)S(1)} %bitcast.78), kind=kOutput, calls=%fused_computation.22 | convolution fusion | flops 268959744 | bytes 1835008 | tf_op jit(solution)/shard_map/rk,ok->ro/dot_general | solution.py:376
  122.2 52.3 %shard_map.206 = (bf16[32,2,16,704]{3,2,1,0:T(8,128)(2,1)}, bf16[32,2,16,704]{3,2,1,0:T(8,128)(2,1)}, bf16[8,64,1024]{2,1,0:T(8,128)(2,1)}) custom-call(bf16[16,704]{1,0:T(8,128)(2,1)} %refs_0_.3, bf16[16,704]{1,0:T(8,128)(2,1)} %bitcast.82, bf16[8,64,1024]{2,1,0:T(8,128)(2,1)} %convolution_convert_fusion.1.refs_2_), custom_call_target="tpu_custom_call" | custom-call | bytes 5767168 | tf_op jit(solution)/shard_map/pallas_call | solution.py:305
  174.6 0.6 copy.49
  175.2 1.6 multiply_reduce_fusion.1
  176.8 0.4 multiply_convert_fusion.1
  177.2 1.0 copy-done.13
  178.2 1.0 fusion.40
  179.2 0.4 copy-done.15
  179.6 2.1 fusion.15
  181.7 1.4 copy.42
  183.1 3.4 %convolution_convert_fusion.refs_1_ = bf16[8,64,1024]{2,1,0:T(8,128)(2,1)} fusion(bf16[8,64,704]{2,1,0:T(8,128)(2,1)S(1)} %bitcast.77, bf16[1024,704,1]{1,0,2:T(8,128)(2,1)} %bitcast.86), kind=kOutput, calls=%fused_computation.21 | convolution fusion | flops 738721792 | bytes 3211264 | tf_op jit(solution)/shard_map/rk,ok->ro/dot_general | solution.py:388
  186.5 38.9 %shard_map.207 = (bf16[32,2,16,768]{3,2,1,0:T(8,128)(2,1)}, bf16[8,64,1024]{2,1,0:T(8,128)(2,1)}) custom-call(bf16[16,768]{1,0:T(8,128)(2,1)} %bitcast.80, bf16[8,64,1024]{2,1,0:T(8,128)(2,1)} %convolution_convert_fusion.refs_1_), custom_call_target="tpu_custom_call" | custom-call | bytes 3145728 | tf_op jit(solution)/shard_map/pallas_call | solution.py:305
  225.4 0.0 copy-start.10
  225.5 1.8 multiply_reduce_fusion
  227.2 0.7 dynamic-slice_convert_fusion
  228.0 0.2 multiply_convert_fusion
  228.2 0.5 copy-done.14
  228.7 1.0 convolution_convert_fusion.2
  229.7 0.4 reshape.154
  230.1 1.0 copy.44
  (33 shorter events, 0.1 us)
Async XLA Ops:
  4.5 2.4 %copy-start.11 = (f32[32,4]{0,1:T(4,128)S(1)}, f32[32,4]{0,1:T(4,128)}, u32[]{:S(2)}) copy-start(f32[32,4]{0,1:T(4,128)} %param.29) | copy-start | bytes 1540
  4.5 2.6 %copy-start.12 = (s32[8]{0:T(128)S(1)}, s32[8]{0:T(128)}, u32[]{:S(2)}) copy-start(s32[8]{0:T(128)} %param.26) | copy-start | bytes 100
  11.4 2.7 %copy-start.17 = (s32[8,64,64]{2,1,0:T(8,128)S(1)}, s32[8,64,64]{2,1,0:T(8,128)}, u32[]{:S(2)}) copy-start(s32[8,64,64]{2,1,0:T(8,128)} %param.28) | copy-start | bytes 393220
  14.1 3.2 %copy-start.7 = (s32[8,64]{1,0:T(8,128)S(1)}, s32[8,64]{1,0:T(8,128)}, u32[]{:S(2)}) copy-start(s32[8,64]{1,0:T(8,128)} %param.24) | copy-start | bytes 6148
  17.3 2.5 %copy-start.18 = (s32[8]{0:T(128)S(1)}, s32[8]{0:T(128)}, u32[]{:S(2)}) copy-start(s32[8]{0:T(128)} %param.25) | copy-start | bytes 100
  20.5 4.4 %copy-start.3 = (bf16[8,1,512,256]{2,3,0,1:T(8,128)(2,1)S(1)}, bf16[8,1,512,256]{2,3,0,1:T(8,128)(2,1)}, u32[]{:S(2)}) copy-start(bf16[8,1,512,256]{2,3,0,1:T(8,128)(2,1)} %copy.38) | copy-start | bytes 6291460
  21.0 4.0 %copy-start.1 = (f32[8,4,64,512]{3,2,1,0:T(8,128)S(1)}, f32[8,4,64,512]{3,2,1,0:T(8,128)}, u32[]{:S(2)}) copy-start(f32[8,4,64,512]{3,2,1,0:T(8,128)} %get-tuple-element.30) | copy-start | bytes 12582916
  29.5 24.1 %copy-start.5 = (bf16[8,16,1024]{2,1,0:T(8,128)(2,1)S(1)}, bf16[8,16,1024]{2,1,0:T(8,128)(2,1)}, u32[]{:S(2)}) copy-start(bf16[8,16,1024]{2,1,0:T(8,128)(2,1)} %param.20) | copy-start | bytes 786436
  53.7 47.8 %copy-start.8 = (f32[1024]{0:T(1024)S(1)}, f32[1024]{0:T(1024)}, u32[]{:S(2)}) copy-start(f32[1024]{0:T(1024)} %param.30) | copy-start | bytes 12292
  99.9 3.1 %copy-start.16 = (bf16[32,2,16,256]{3,2,1,0:T(8,128)(2,1)S(1)}, bf16[32,2,16,256]{3,2,1,0:T(8,128)(2,1)}, u32[]{:S(2)}) copy-start(bf16[32,2,16,256]{3,2,1,0:T(8,128)(2,1)} %get-tuple-element.12) | copy-start | bytes 1572868
  104.1 15.6 %copy-start.4 = (bf16[32,2,16,256]{3,2,1,0:T(8,128)(2,1)S(1)}, bf16[32,2,16,256]{3,2,1,0:T(8,128)(2,1)}, u32[]{:S(2)}) copy-start(bf16[32,2,16,256]{3,2,1,0:T(8,128)(2,1)} %get-tuple-element.13) | copy-start | bytes 1572868
  119.8 54.8 %copy-start.6 = (bf16[16,3,256]{2,0,1:T(8,128)(2,1)S(1)}, bf16[16,3,256]{2,0,1:T(8,128)(2,1)}, u32[]{:S(2)}) copy-start(bf16[16,3,256]{2,0,1:T(8,128)(2,1)} %param.39) | copy-start | bytes 73732
  119.8 55.4 %copy-start = (bf16[8,64,1024]{2,1,0:T(8,128)(2,1)S(1)}, bf16[8,64,1024]{2,1,0:T(8,128)(2,1)}, u32[]{:S(2)}) copy-start(bf16[8,64,1024]{2,1,0:T(8,128)(2,1)} %get-tuple-element.11) | copy-start | bytes 3145732
  119.8 57.1 %copy-start.9 = (f32[1024]{0:T(1024)S(1)}, f32[1024]{0:T(1024)}, u32[]{:S(2)}) copy-start(f32[1024]{0:T(1024)} %param.31) | copy-start | bytes 12292
  174.5 2.3 copy-start.2
  176.8 1.4 copy-start.13
  178.2 1.4 copy-start.15
  225.4 2.5 %copy-start.10 = (f32[1024]{0:T(1024)S(1)}, f32[1024]{0:T(1024)}, u32[]{:S(2)}) copy-start(f32[1024]{0:T(1024)} %param.32) | copy-start | bytes 12292
  227.2 1.5 copy-start.14

commit v4 on v2

--- a/solution.py
+++ b/solution.py
@@ -180,19 +180,6 @@
         for j in range(1, n_grp):
             spread(j).start()
 
-    def arrive(k, carry):
-        other = lax.rem(chip + k, n_chips)
-        for i in range(n_in):
-            remote(i, k).wait_send()
-            pltpu.make_async_copy(
-                srcs[i], outs[i].at[other, core], recv_sems.at[i, other]
-            ).wait()
-        return carry
-
-    lax.fori_loop(1, n_chips, arrive, 0)
-    for copy in locals_:
-        copy.wait()
-
     def forward(i, c):
         return pltpu.make_async_remote_copy(
             src_ref=outs[i].at[c, core],
@@ -203,12 +190,22 @@
             device_id_type=mesh_id,
         )
 
-    def push(c, carry):
+    for i in range(n_in):
+        locals_[i].wait()
+        forward(i, chip).start()
+
+    def arrive(k, carry):
+        other = lax.rem(chip + k, n_chips)
         for i in range(n_in):
-            forward(i, c).start()
+            pltpu.make_async_copy(
+                srcs[i], outs[i].at[other, core], recv_sems.at[i, other]
+            ).wait()
+            forward(i, other).start()
+        for i in range(n_in):
+            remote(i, k).wait_send()
         return carry
 
-    lax.fori_loop(0, n_chips, push, 0)
+    lax.fori_loop(1, n_chips, arrive, 0)
 
     def land(c, carry):
         for i in range(n_in):

time: 228 us -> 227 us (level)
  no operation moved by 1% of the time
where the time goes in v4:
time: 227 us; the launch traced here: 226 us
  Pallas kernels  157 us (69%)
  local copies, waits for them, and re-layouts  30.3 us (13%)
  matrix products  25.7 us (11%)
  other arithmetic  12 us (5%)
    pallas_call x4, Pallas kernels, fetch_group(): pl.pallas_call(functools.partial(gather_kernel, n_chips, n_in, n_grp), ou...  157 us
    slice x2, local copies, waits for them, and re-layouts, cross_attention(): enc_keys = cached[:, 0].reshape(requests, -1, local_heads, DH)  6.82 us
    slice x2, local copies, waits for them, and re-layouts, draft_attention(): cache_keys = cached[:, 0].reshape(requests, -1, local_heads, head_size)  6.77 us

profile of v4, /device:TPU:1, one launch (start us, length us, event | category | flops | bytes accessed | tf_op | source)
XLA Modules:
  0.0 226.3 jit_solution(11944032555957182432)
XLA Ops:
  0.6 3.9 %fusion.49 = (bf16[8,1,512,256]{3,2,1,0:T(8,128)(2,1)}, bf16[8,1,512,256]{3,2,1,0:T(8,128)(2,1)S(1)}) fusion(bf16[8,2,512,256]{3,2,1,0:T(8,128)(2,1)} %param.22), kind=kLoop, calls=%fused_computation.90 | loop fusion | bytes 8388608 | tf_op jit(solution)/shard_map/slice | solution.py:36
  4.5 2.4 %copy.41 = bf16[8,1,512,256]{2,3,0,1:T(8,128)(2,1)} copy(bf16[8,1,512,256]{3,2,1,0:T(8,128)(2,1)S(1)} %get-tuple-element.27) | data formatting | bytes 4194304 | tf_op jit(solution)/shard_map/slice | solution.py:37
  6.9 0.2 slice_reduce_fusion
  7.2 2.9 %copy.35 = bf16[8,1,512,256]{2,3,0,1:T(8,128)(2,1)S(1)} copy(bf16[8,1,512,256]{3,2,1,0:T(8,128)(2,1)} %get-tuple-element.26) | data formatting | bytes 4194304 | tf_op jit(solution)/shard_map/slice | solution.py:36
  10.1 1.2 fusion.50
  11.2 0.2 reshape_squeeze.21
  11.5 2.6 %fusion.3 = (f32[8,4,64]{2,1,0:T(4,128)S(1)}, f32[8,4,64,512]{3,2,1,0:T(8,128)}) fusion(f32[4]{0:T(128)S(1)} %slice_reduce_fusion, pred[8,512]{1,0:T(8,128)(4,1)S(1)} %iota_compare_fusion.5, bf16[8,512,4,64]{1,3,2,0:T(8,128)(2,1)S(1)} %bitcast.74, bf16[8,64,4,64]{3,2,1,0:T(4,128)(2,1)S(1)} %reshape_squeeze.21), kind=kOutput, calls=%fused_computation.9 | convolution fusion | flops 137361408 | bytes 6565904 | tf_op jit(solution)/shard_map/rihd,rphd->rhip/dot_general | solution.py:38
  14.1 2.6 %fusion.1 = f32[8,64,64,4]{2,3,1,0:T(4,128)S(1)} fusion(s32[8,64,64]{2,1,0:T(8,128)S(1)} %copy-done.19, f32[32,4]{0,1:T(4,128)S(1)} %copy-done.12), kind=kOutput, calls=%fused_computation.2 | convolution fusion | flops 51380224 | bytes 655872 | tf_op jit(solution)/shard_map/rijb,bh->rhij/dot_general | solution.py:47
  16.7 0.3 copy.40
  17.1 0.2 reshape_squeeze.23
  17.4 0.5 convolution_minimum_fusion.6
  17.9 0.4 convolution_minimum_fusion.5
  18.3 0.4 convolution_minimum_fusion.4
  18.7 0.4 convolution_minimum_fusion.3
  19.1 0.4 convolution_minimum_fusion.2
  19.5 0.4 convolution_minimum_fusion.1
  19.9 0.4 fusion.29
  20.3 0.2 copy.37
  20.5 0.4 fusion.51
  21.0 3.7 %fusion.7 = f32[8,4,64]{2,1,0:T(4,128)S(1)} fusion(f32[8,4,64,512]{3,2,1,0:T(8,128)} %get-tuple-element.32, f32[8,4,64]{2,1,0:T(4,128)S(1)} %max.8, f32[4]{0:T(128)S(1)} %slice_reduce_fusion, pred[8,512]{1,0:T(8,128)(4,1)S(1)} %iota_compare_fusion.5), kind=kLoop, calls=%fused_computation.12 | loop fusion | flops 4192256 | bytes 4214800 | tf_op jit(solution)/shard_map/reduce_sum | solution.py:60
  24.7 0.2 fusion.30
  25.0 2.2 fusion.14
  27.2 0.2 reshape_squeeze.25
  27.4 1.6 fusion.27
  29.1 0.4 copy.44
  29.5 0.3 dot_general.81
  29.8 22.1 %shard_map.203 = bf16[32,2,16,256]{3,2,1,0:T(8,128)(2,1)} custom-call(bf16[16,256]{1,0:T(8,128)(2,1)} %bitcast.89), custom_call_target="tpu_custom_call" | custom-call | bytes 1048576 | tf_op jit(solution)/shard_map/pallas_call | solution.py:259
  52.0 1.5 fusion.53
  53.5 0.1 add_dynamic-update-slice_fusion
  53.6 1.1 convert_element_type.81.refs_3_
  54.7 44.2 %shard_map.204 = (bf16[32,2,16,256]{3,2,1,0:T(8,128)(2,1)}, bf16[32,2,16,256]{3,2,1,0:T(8,128)(2,1)}, bf16[32,2,16,704]{3,2,1,0:T(8,128)(2,1)}, bf16[8,64,1024]{2,1,0:T(8,128)(2,1)}) custom-call(bf16[16,256]{1,0:T(8,128)(2,1)} %refs_0_.2, bf16[16,256]{1,0:T(8,128)(2,1)} %bitcast.90, bf16[16,704]{1,0:T(8,128)(2,1)} %refs_2_.1, ...), custom_call_target="tpu_custom_call" | custom-call | bytes 4980736 | tf_op jit(solution)/shard_map/pallas_call | solution.py:259
  99.0 3.9 %fusion.48 = (bf16[8,1,512,256]{3,2,1,0:T(8,128)(2,1)}, bf16[8,1,512,256]{3,2,1,0:T(8,128)(2,1)S(1)}) fusion(bf16[8,2,512,256]{3,2,1,0:T(8,128)(2,1)} %param.23), kind=kLoop, calls=%fused_computation.89 | loop fusion | bytes 8388608 | tf_op jit(solution)/shard_map/slice | solution.py:76
  102.8 2.4 %copy.47 = bf16[8,1,512,256]{2,3,0,1:T(8,128)(2,1)} copy(bf16[8,1,512,256]{3,2,1,0:T(8,128)(2,1)S(1)} %get-tuple-element.25) | data formatting | bytes 4194304 | tf_op jit(solution)/shard_map/slice | solution.py:77
  105.2 2.9 %copy.45 = bf16[8,1,512,256]{2,3,0,1:T(8,128)(2,1)S(1)} copy(bf16[8,1,512,256]{3,2,1,0:T(8,128)(2,1)} %get-tuple-element.24) | data formatting | bytes 4194304 | tf_op jit(solution)/shard_map/slice | solution.py:76
  108.2 0.3 fusion.8
  108.5 0.3 fusion.10
  108.8 0.4 copy-done.18
  109.2 0.4 convolution_convert_fusion.3
  109.6 1.0 reshape_reshape.3
  110.7 1.7 fusion.31
  112.5 1.9 fusion.52
  114.5 0.8 fusion.26
  115.3 0.4 copy.48
  115.7 0.3 dot_general.86
  116.0 0.3 copy-done.5
  116.3 1.4 convolution_convert_fusion.1.refs_2_
  117.8 50.5 %shard_map.205 = (bf16[32,2,16,704]{3,2,1,0:T(8,128)(2,1)}, bf16[32,2,16,704]{3,2,1,0:T(8,128)(2,1)}, bf16[8,64,1024]{2,1,0:T(8,128)(2,1)}) custom-call(bf16[16,704]{1,0:T(8,128)(2,1)} %refs_0_.3, bf16[16,704]{1,0:T(8,128)(2,1)} %bitcast.88, bf16[8,64,1024]{2,1,0:T(8,128)(2,1)} %convolution_convert_fusion.1.refs_2_), custom_call_target="tpu_custom_call" | custom-call | bytes 5767168 | tf_op jit(solution)/shard_map/pallas_call | solution.py:259
  168.3 0.6 copy.56
  168.9 1.6 multiply_reduce_fusion.1
  170.5 0.4 multiply_convert_fusion.1
  170.9 1.0 copy-done.15
  171.9 1.0 fusion.54
  172.9 0.4 copy-done.17
  173.3 2.1 fusion.22
  175.4 1.4 copy.49
  176.8 3.4 %convolution_convert_fusion.refs_1_ = bf16[8,64,1024]{2,1,0:T(8,128)(2,1)} fusion(bf16[8,64,704]{2,1,0:T(8,128)(2,1)S(1)} %bitcast.84, bf16[1024,704,1]{1,0,2:T(8,128)(2,1)} %bitcast.92), kind=kOutput, calls=%fused_computation.29 | convolution fusion | flops 738721792 | bytes 3211264 | tf_op jit(solution)/shard_map/rk,ok->ro/dot_general | solution.py:342
  180.2 40.4 %shard_map.206 = (bf16[32,2,16,768]{3,2,1,0:T(8,128)(2,1)}, bf16[8,64,1024]{2,1,0:T(8,128)(2,1)}) custom-call(bf16[16,768]{1,0:T(8,128)(2,1)} %bitcast.86, bf16[8,64,1024]{2,1,0:T(8,128)(2,1)} %convolution_convert_fusion.refs_1_), custom_call_target="tpu_custom_call" | custom-call | bytes 3145728 | tf_op jit(solution)/shard_map/pallas_call | solution.py:259
  220.7 1.8 multiply_reduce_fusion
  222.4 0.7 dynamic-slice_convert_fusion
  223.2 0.2 multiply_convert_fusion
  223.4 0.5 copy-done.16
  223.9 1.0 convolution_convert_fusion.2
  224.9 0.4 reshape.169
  225.3 1.0 copy.51
  (46 shorter events, 0.3 us)
Async XLA Ops:
  4.5 2.4 %copy-start.12 = (f32[32,4]{0,1:T(4,128)S(1)}, f32[32,4]{0,1:T(4,128)}, u32[]{:S(2)}) copy-start(f32[32,4]{0,1:T(4,128)} %param.29) | copy-start | bytes 1540
  4.5 2.6 %copy-start.13 = (s32[8]{0:T(128)S(1)}, s32[8]{0:T(128)}, u32[]{:S(2)}) copy-start(s32[8]{0:T(128)} %param.26) | copy-start | bytes 100
  11.5 2.6 %copy-start.19 = (s32[8,64,64]{2,1,0:T(8,128)S(1)}, s32[8,64,64]{2,1,0:T(8,128)}, u32[]{:S(2)}) copy-start(s32[8,64,64]{2,1,0:T(8,128)} %param.28) | copy-start | bytes 393220
  14.1 3.2 %copy-start.8 = (s32[8,64]{1,0:T(8,128)S(1)}, s32[8,64]{1,0:T(8,128)}, u32[]{:S(2)}) copy-start(s32[8,64]{1,0:T(8,128)} %param.24) | copy-start | bytes 6148
  17.4 2.5 %copy-start.20 = (s32[8]{0:T(128)S(1)}, s32[8]{0:T(128)}, u32[]{:S(2)}) copy-start(s32[8]{0:T(128)} %param.25) | copy-start | bytes 100
  20.5 4.4 %copy-start.3 = (bf16[8,1,512,256]{2,3,0,1:T(8,128)(2,1)S(1)}, bf16[8,1,512,256]{2,3,0,1:T(8,128)(2,1)}, u32[]{:S(2)}) copy-start(bf16[8,1,512,256]{2,3,0,1:T(8,128)(2,1)} %copy.41) | copy-start | bytes 6291460
  21.0 4.0 %copy-start.1 = (f32[8,4,64,512]{3,2,1,0:T(8,128)S(1)}, f32[8,4,64,512]{3,2,1,0:T(8,128)}, u32[]{:S(2)}) copy-start(f32[8,4,64,512]{3,2,1,0:T(8,128)} %get-tuple-element.32) | copy-start | bytes 12582916
  29.5 24.0 %copy-start.6 = (bf16[8,16,1024]{2,1,0:T(8,128)(2,1)S(1)}, bf16[8,16,1024]{2,1,0:T(8,128)(2,1)}, u32[]{:S(2)}) copy-start(bf16[8,16,1024]{2,1,0:T(8,128)(2,1)} %param.20) | copy-start | bytes 786436
  105.2 3.0 %copy-start = (bf16[8,64,1024]{2,1,0:T(8,128)(2,1)S(1)}, bf16[8,64,1024]{2,1,0:T(8,128)(2,1)}, u32[]{:S(2)}) copy-start(bf16[8,64,1024]{2,1,0:T(8,128)(2,1)} %get-tuple-element.11) | copy-start | bytes 3145732
  105.2 3.3 %copy-start.9 = (f32[1024]{0:T(1024)S(1)}, f32[1024]{0:T(1024)}, u32[]{:S(2)}) copy-start(f32[1024]{0:T(1024)} %param.30) | copy-start | bytes 12292
  108.2 1.0 copy-start.18
  110.7 1.7 copy-start.14
  112.5 2.0 copy-start.4
  115.3 1.0 copy-start.5
  115.7 52.6 %copy-start.7 = (bf16[16,3,256]{2,0,1:T(8,128)(2,1)S(1)}, bf16[16,3,256]{2,0,1:T(8,128)(2,1)}, u32[]{:S(2)}) copy-start(bf16[16,3,256]{2,0,1:T(8,128)(2,1)} %param.39) | copy-start | bytes 73732
  116.3 54.2 %copy-start.10 = (f32[1024]{0:T(1024)S(1)}, f32[1024]{0:T(1024)}, u32[]{:S(2)}) copy-start(f32[1024]{0:T(1024)} %param.31) | copy-start | bytes 12292
  168.2 2.3 %copy-start.2 = (bf16[8,64,1024]{2,1,0:T(8,128)(2,1)S(1)}, bf16[8,64,1024]{2,1,0:T(8,128)(2,1)}, u32[]{:S(2)}) copy-start(bf16[8,64,1024]{2,1,0:T(8,128)(2,1)} %get-tuple-element.14) | copy-start | bytes 3145732
  170.5 1.4 copy-start.15
  171.9 1.4 copy-start.17
  220.7 2.5 %copy-start.11 = (f32[1024]{0:T(1024)S(1)}, f32[1024]{0:T(1024)}, u32[]{:S(2)}) copy-start(f32[1024]{0:T(1024)} %param.32) | copy-start | bytes 12292
  222.4 1.5 copy-start.16

commit v5 on v4

--- a/solution.py
+++ b/solution.py
@@ -270,6 +270,22 @@
         return gathered, results[n_in]
     return gathered
 
+def doubling_gather(block, n_tok):
+    position = lax.axis_index("tok")
+    held = block[None]
+    step = 1
+    while step < n_tok:
+        arrived = lax.ppermute(held, "tok", perm=[(i, i ^ step) for i in range(n_tok)])
+        upper = (position // step) % 2 == 1
+        held = jnp.where(
+            upper,
+            jnp.concatenate([arrived, held], axis=0),
+            jnp.concatenate([held, arrived], axis=0),
+        )
+        step *= 2
+    return held.reshape((n_tok * block.shape[0],) + block.shape[1:])
+
+
 def layer_sum(summand, base_full):
     return lax.psum(summand.astype(jnp.bfloat16), "grp").astype(jnp.float32) + base_full
 
@@ -307,7 +323,7 @@
     self_context = draft_attention(
         draft_qkv, self_cache, parents, counts, self_len, buckets, bias_table
     )
-    (w_out_self_t,) = fetch_group(lax.axis_size("tok"), 3, (w_out_self.T,), self_context)
+    w_out_self_t = doubling_gather(w_out_self.T, lax.axis_size("tok"))
     partial_value = jnp.einsum(
         "rk,ok->ro", self_context, w_out_self_t, preferred_element_type=jnp.float32
     )

time: 227 us -> 236 us (1.040)
  Pallas kernels: 157 us -> 133 us
  starting transfers between devices: 0 us -> 15.5 us
  local copies, waits for them, and re-layouts: 30.3 us -> 36.3 us
  other arithmetic: 12 us -> 17.5 us
  matrix products: 25.7 us -> 29.4 us
  waiting for transfers between devices: 0 us -> 2.42 us
    pallas_call x4 -> x3, Pallas kernels: 157 us -> 133 us  [fetch_group(): pl.pallas_call(functools.partial(gather_kernel, n_chips, n_in, n_grp), ou...]
    ppermute x0 -> x6, starting transfers between devices: none -> 15.5 us  [doubling_gather(): lax.ppermute(held, 'tok', perm=[(i, i ^ step) for i in range(n_tok)])]
    select_n x0 -> x6, other arithmetic: none -> 2.95 us  [doubling_gather(): jnp.where(upper, jnp.concatenate([arrived, held], axis=0), jnp.concatenat...]
    dot_general x1, matrix products: 2.22 us -> 5.02 us  [draft_attention(): jnp.einsum('rhip,rphd->rihd', weights_cache, cache_values, preferred_elem...]
    ppermute x0 -> x6, waiting for transfers between devices: none -> 2.42 us  [doubling_gather(): lax.ppermute(held, 'tok', perm=[(i, i ^ step) for i in range(n_tok)])]
  transfers between devices with their start and end apart: 0 -> 6, of which waited for: 0 -> 2; matrix products, arithmetic and copies ran while one was open for 0% -> 22% of each run, Pallas kernels for 0% -> 0%
where the time goes in v5:
time: 236 us; the launch traced here: 235 us
  Pallas kernels  133 us (56%)
  local copies, waits for them, and re-layouts  36.3 us (15%)
  matrix products  29.4 us (12%)
  other arithmetic  17.5 us (7%)
  starting transfers between devices  15.5 us (7%)
  waiting for transfers between devices  2.42 us (1%)
    pallas_call x3, Pallas kernels, fetch_group(): pl.pallas_call(functools.partial(gather_kernel, n_chips, n_in, n_grp), ou...  133 us
    ppermute x6, starting transfers between devices, doubling_gather(): lax.ppermute(held, 'tok', perm=[(i, i ^ step) for i in range(n_tok)])  15.5 us
    slice x2, local copies, waits for them, and re-layouts, draft_attention(): cache_keys = cached[:, 0].reshape(requests, -1, local_heads, head_size)  7.44 us
    slice x2, local copies, waits for them, and re-layouts, cross_attention(): enc_keys = cached[:, 0].reshape(requests, -1, local_heads, DH)  6.78 us
    reduce_sum x3, other arithmetic, rms_scale(): mean_square = jnp.mean(stream * stream, axis=-1, keepdims=True)  5.06 us
    dot_general x1, matrix products, draft_attention(): jnp.einsum('rhip,rphd->rihd', weights_cache, cache_values, preferred_elem...  5.02 us
  transfers between devices with their start and end apart: 6, of which 2 were waited for; matrix products, arithmetic and copies ran while one was open for 22% of the time, Pallas kernels for 0%

profile of v5, /device:TPU:1, one launch (start us, length us, event | category | flops | bytes accessed | tf_op | source)
XLA Modules:
  0.0 235.2 jit_solution(13604685306683410184)
XLA Ops:
  0.6 3.3 %collective-permute-start = (bf16[1,16,256]{2,1,0:T(8,128)(2,1)}, bf16[1,16,256]{2,1,0:T(8,128)(2,1)}, u32[]{:S(2)}, u32[]{:S(2)}) collective-permute-start(bf16[1,16,256]{2,1,0:T(8,128)(2,1)} %bitcast.92), channel_id=1, source_target_pairs={{0,1},{1,0},{2,3},{3,2},{4,5},{5,4},{6,7},{7,6},{8,9},{9,8},{10,11... | collective-permute-start | bytes 24584 | tf_op jit(solution)/shard_map/ppermute | solution.py:278
  4.0 4.6 %fusion.49 = (bf16[8,1,512,256]{3,2,1,0:T(8,128)(2,1)}, bf16[8,1,512,256]{3,2,1,0:T(8,128)(2,1)}) fusion(bf16[8,2,512,256]{3,2,1,0:T(8,128)(2,1)} %param.22), kind=kLoop, calls=%fused_computation.96 | loop fusion | bytes 8388608 | tf_op jit(solution)/shard_map/slice | solution.py:36
  8.8 2.9 %copy.35 = bf16[8,1,512,256]{2,3,0,1:T(8,128)(2,1)S(1)} copy(bf16[8,1,512,256]{3,2,1,0:T(8,128)(2,1)} %get-tuple-element.26) | data formatting | bytes 4194304 | tf_op jit(solution)/shard_map/slice | solution.py:36
  11.7 1.9 fusion.50
  13.9 3.6 %fusion.1 = f32[8,64,64,4]{2,3,1,0:T(4,128)} fusion(s32[8,64,64]{2,1,0:T(8,128)S(1)} %copy-done.27, f32[32,4]{0,1:T(4,128)S(1)} %copy-done.20), kind=kOutput, calls=%fused_computation.2 | convolution fusion | flops 51380224 | bytes 655872 | tf_op jit(solution)/shard_map/rijb,bh->rhij/dot_general | solution.py:47
  17.5 2.6 %copy.40 = f32[8,64,64,4]{1,2,3,0:T(8,128)} copy(f32[8,64,64,4]{2,3,1,0:T(4,128)} %fusion.1) | data formatting | bytes 1048576 | tf_op jit(solution)/shard_map/rijb,bh->rhij/dot_general | solution.py:47
  20.1 1.2 reshape_squeeze.23
  21.3 0.5 convolution_minimum_fusion.6
  21.8 0.4 convolution_minimum_fusion.5
  22.2 0.4 convolution_minimum_fusion.4
  22.6 0.4 convolution_minimum_fusion.3
  23.0 0.4 convolution_minimum_fusion.2
  23.4 0.4 convolution_minimum_fusion.1
  23.9 0.4 fusion.29
  24.5 2.6 %fusion.3 = (f32[8,4,64]{2,1,0:T(4,128)S(1)}, f32[8,4,64,512]{3,2,1,0:T(8,128)}) fusion(f32[4]{0:T(128)S(1)} %slice_reduce_fusion, pred[8,512]{1,0:T(8,128)(4,1)S(1)} %iota_compare_fusion.5, bf16[8,512,4,64]{1,3,2,0:T(8,128)(2,1)S(1)} %bitcast.76, bf16[8,64,4,64]{3,2,1,0:T(4,128)(2,1)S(1)} %reshape_squeeze.21), kind=kOutput, calls=%fused_computation.9 | convolution fusion | flops 137361408 | bytes 6565904 | tf_op jit(solution)/shard_map/rihd,rphd->rhip/dot_general | solution.py:38
  27.2 1.4 fusion.51
  28.6 0.8 maximum_select_fusion.5
  29.4 3.7 %fusion.7 = f32[8,4,64]{2,1,0:T(4,128)S(1)} fusion(f32[8,4,64,512]{3,2,1,0:T(8,128)} %get-tuple-element.32, f32[8,4,64]{2,1,0:T(4,128)S(1)} %max.8, f32[4]{0:T(128)S(1)} %copy-done.15, pred[8,512]{1,0:T(8,128)(4,1)S(1)} %copy-done.10), kind=kLoop, calls=%fused_computation.12 | loop fusion | flops 4192256 | bytes 4214800 | tf_op jit(solution)/shard_map/reduce_sum | solution.py:60
  33.2 2.0 collective-permute-start.2
  35.4 2.4 %copy.41 = bf16[8,1,512,256]{2,3,0,1:T(8,128)(2,1)} copy(bf16[8,1,512,256]{3,2,1,0:T(8,128)(2,1)S(1)} %copy-done.2) | data formatting | bytes 4194304 | tf_op jit(solution)/shard_map/slice | solution.py:37
  37.9 1.9 collective-permute-start.3
  39.8 5.0 %fusion.14 = f32[8,4,64,64]{3,2,1,0:T(8,128)} fusion(bf16[8,512,4,64]{1,3,2,0:T(8,128)(2,1)} %bitcast.80, f32[8,4,64,512]{3,2,1,0:T(8,128)} %get-tuple-element.32, f32[8,4,64]{2,1,0:T(4,128)S(1)} %add.111, f32[8,4,64]{2,1,0:T(4,128)S(1)} %max.8, f32[4]{0:T(128)S(1)} %copy-done.15, pred[8,512]{1,0:T(8,128)(4,1)S(1)} %copy-done.10), kind=kOutput, calls=%fused_computation.28 | convolution fusion | flops 139460608 | bytes 6836240 | tf_op jit(solution)/shard_map/rhip,rphd->rihd/dot_general | solution.py:63
  44.9 3.1 %collective-permute-start.4 = (bf16[16,16,256]{2,1,0:T(8,128)(2,1)S(1)}, bf16[16,16,256]{2,1,0:T(8,128)(2,1)}, u32[]{:S(2)}, u32[]{:S(2)}) collective-permute-start(bf16[16,16,256]{2,1,0:T(8,128)(2,1)S(1)} %maximum_select_fusion.2), channel_id=1, source_target_pairs={{0,16},{1,17},{2,18},{3,19},{4,20},{5,21},{6,22},{7,23},{8,24},{9,... | collective-permute-start | bytes 393224 | tf_op jit(solution)/shard_map/ppermute | solution.py:278
  47.9 3.9 %fusion.48 = (bf16[8,1,512,256]{3,2,1,0:T(8,128)(2,1)}, bf16[8,1,512,256]{3,2,1,0:T(8,128)(2,1)S(1)}) fusion(bf16[8,2,512,256]{3,2,1,0:T(8,128)(2,1)} %param.23), kind=kLoop, calls=%fused_computation.95 | loop fusion | bytes 8388608 | tf_op jit(solution)/shard_map/slice | solution.py:76
  51.8 1.0 reshape_squeeze.25
  52.9 1.7 collective-permute-done.4
  54.5 1.0 maximum_select_fusion.1
  55.6 5.2 %collective-permute-start.5 = (bf16[32,16,256]{2,1,0:T(8,128)(2,1)S(1)}, bf16[32,16,256]{2,1,0:T(8,128)(2,1)}, u32[]{:S(2)}, u32[]{:S(2)}) collective-permute-start(bf16[32,16,256]{2,1,0:T(8,128)(2,1)S(1)} %maximum_select_fusion.1), channel_id=1, source_target_pairs={{0,32},{1,33},{2,34},{3,35},{4,36},{5,37},{6,38},{7,39},{8,40},{9,... | collective-permute-start | bytes 786440 | tf_op jit(solution)/shard_map/ppermute | solution.py:278
  60.8 2.6 %fusion.27 = bf16[8,64,4,64]{3,1,2,0:T(8,128)(2,1)} fusion(f32[8,4,64,64]{3,2,1,0:T(8,128)} %fusion.14, f32[8,4,64,64]{2,3,1,0:T(8,128)S(1)} %copy-done.3, bf16[8,64,4,64]{3,2,1,0:T(4,128)(2,1)} %reshape_squeeze.25, f32[8,4,64]{2,1,0:T(4,128)} %copy-done.12, f32[8,4,64]{2,1,0:T(4,128)S(1)} %max.8), kind=kOutput, calls=%fused_computation.47 | convolution fusion | flops 17432576 | bytes 1589248 | tf_op jit(solution)/shard_map/rhij,rjhd->rihd/dot_general | solution.py:66
  63.4 1.5 copy.44
  64.9 1.0 dot_general.81
  65.9 2.4 %copy.47 = bf16[8,1,512,256]{2,3,0,1:T(8,128)(2,1)} copy(bf16[8,1,512,256]{3,2,1,0:T(8,128)(2,1)S(1)} %get-tuple-element.25) | data formatting | bytes 4194304 | tf_op jit(solution)/shard_map/slice | solution.py:77
  68.3 2.9 %copy.45 = bf16[8,1,512,256]{2,3,0,1:T(8,128)(2,1)S(1)} copy(bf16[8,1,512,256]{3,2,1,0:T(8,128)(2,1)} %get-tuple-element.24) | data formatting | bytes 4194304 | tf_op jit(solution)/shard_map/slice | solution.py:76
  71.3 0.6 copy.56
  71.9 0.7 collective-permute-done.5
  72.7 1.1 maximum_select_fusion
  73.8 0.5 fusion.53
  74.4 1.1 convert_element_type.81.refs_3_
  75.5 42.8 %shard_map.203 = (bf16[32,2,16,256]{3,2,1,0:T(8,128)(2,1)}, bf16[32,2,16,256]{3,2,1,0:T(8,128)(2,1)}, bf16[32,2,16,704]{3,2,1,0:T(8,128)(2,1)}, bf16[8,64,1024]{2,1,0:T(8,128)(2,1)}) custom-call(bf16[16,256]{1,0:T(8,128)(2,1)} %refs_0_.2, bf16[16,256]{1,0:T(8,128)(2,1)} %bitcast.91, bf16[16,704]{1,0:T(8,128)(2,1)} %refs_2_.1, ...), custom_call_target="tpu_custom_call" | custom-call | bytes 4980736 | tf_op jit(solution)/shard_map/pallas_call | solution.py:259
  118.4 1.6 fusion.8
  119.9 1.5 fusion.10
  121.5 0.4 convolution_convert_fusion.3
  122.2 0.7 fusion.31
  122.9 2.0 fusion.52
  124.9 0.8 fusion.26
  125.7 0.4 copy.48
  126.1 0.3 dot_general.86
  126.7 1.5 convolution_convert_fusion.1.refs_2_
  128.2 48.5 %shard_map.204 = (bf16[32,2,16,704]{3,2,1,0:T(8,128)(2,1)}, bf16[32,2,16,704]{3,2,1,0:T(8,128)(2,1)}, bf16[8,64,1024]{2,1,0:T(8,128)(2,1)}) custom-call(bf16[16,704]{1,0:T(8,128)(2,1)} %refs_0_.3, bf16[16,704]{1,0:T(8,128)(2,1)} %bitcast.90, bf16[8,64,1024]{2,1,0:T(8,128)(2,1)} %convolution_convert_fusion.1.refs_2_), custom_call_target="tpu_custom_call" | custom-call | bytes 5767168 | tf_op jit(solution)/shard_map/pallas_call | solution.py:259
  176.7 1.7 multiply_reduce_fusion.1
  178.5 0.4 multiply_convert_fusion.1
  178.9 1.0 copy-done.23
  179.8 1.0 fusion.54
  180.8 0.4 copy-done.25
  181.2 2.1 fusion.22
  183.3 1.4 copy.49
  184.7 3.4 %convolution_convert_fusion.refs_1_ = bf16[8,64,1024]{2,1,0:T(8,128)(2,1)} fusion(bf16[8,64,704]{2,1,0:T(8,128)(2,1)S(1)} %bitcast.86, bf16[1024,704,1]{1,0,2:T(8,128)(2,1)} %bitcast.95), kind=kOutput, calls=%fused_computation.29 | convolution fusion | flops 738721792 | bytes 3211264 | tf_op jit(solution)/shard_map/rk,ok->ro/dot_general | solution.py:358
  188.1 41.3 %shard_map.205 = (bf16[32,2,16,768]{3,2,1,0:T(8,128)(2,1)}, bf16[8,64,1024]{2,1,0:T(8,128)(2,1)}) custom-call(bf16[16,768]{1,0:T(8,128)(2,1)} %bitcast.88, bf16[8,64,1024]{2,1,0:T(8,128)(2,1)} %convolution_convert_fusion.refs_1_), custom_call_target="tpu_custom_call" | custom-call | bytes 3145728 | tf_op jit(solution)/shard_map/pallas_call | solution.py:259
  229.5 1.8 multiply_reduce_fusion
  231.3 0.7 dynamic-slice_convert_fusion
  232.3 0.5 copy-done.24
  232.8 1.0 convolution_convert_fusion.2
  233.8 0.4 reshape.178
  234.1 1.0 copy.51
  (79 shorter events, 2.1 us)
Async XLA Ops:
  0.6 28.0 %collective-permute-start = (bf16[1,16,256]{2,1,0:T(8,128)(2,1)}, bf16[1,16,256]{2,1,0:T(8,128)(2,1)}, u32[]{:S(2)}, u32[]{:S(2)}) collective-permute-start(bf16[1,16,256]{2,1,0:T(8,128)(2,1)} %bitcast.92), channel_id=1, source_target_pairs={{0,1},{1,0},{2,3},{3,2},{4,5},{5,4},{6,7},{7,6},{8,9},{9,8},{10,11... | collective-permute-start | bytes 24584 | tf_op jit(solution)/shard_map/ppermute | solution.py:278
  4.0 4.6 %copy-start.20 = (f32[32,4]{0,1:T(4,128)S(1)}, f32[32,4]{0,1:T(4,128)}, u32[]{:S(2)}) copy-start(f32[32,4]{0,1:T(4,128)} %param.29) | copy-start | bytes 1540
  4.0 4.8 %copy-start.21 = (s32[8]{0:T(128)S(1)}, s32[8]{0:T(128)}, u32[]{:S(2)}) copy-start(s32[8]{0:T(128)} %param.26) | copy-start | bytes 100
  8.7 15.7 %copy-start.14 = (f32[4]{0:T(128)}, f32[4]{0:T(128)S(1)}, u32[]{:S(2)}) copy-start(f32[4]{0:T(128)S(1)} %slice_reduce_fusion) | copy-start | bytes 52
  8.8 15.7 %copy-start.9 = (pred[8,512]{1,0:T(8,128)(4,1)}, pred[8,512]{1,0:T(8,128)(4,1)S(1)}, u32[]{:S(2)}) copy-start(pred[8,512]{1,0:T(8,128)(4,1)S(1)} %iota_compare_fusion.5) | copy-start | bytes 12292
  11.7 2.2 copy-start.27
  13.9 7.4 %copy-start.16 = (s32[8,64]{1,0:T(8,128)S(1)}, s32[8,64]{1,0:T(8,128)}, u32[]{:S(2)}) copy-start(s32[8,64]{1,0:T(8,128)} %param.24) | copy-start | bytes 6148
  21.3 2.5 %copy-start.28 = (s32[8]{0:T(128)S(1)}, s32[8]{0:T(128)}, u32[]{:S(2)}) copy-start(s32[8]{0:T(128)} %param.25) | copy-start | bytes 100
  24.5 2.7 %copy-start.4 = (f32[8,64,64,4]{1,2,3,0:T(8,128)S(1)}, f32[8,64,64,4]{1,2,3,0:T(8,128)}, u32[]{:S(2)}) copy-start(f32[8,64,64,4]{1,2,3,0:T(8,128)} %copy.40) | copy-start | bytes 1572868
  27.1 1.5 copy-start.13
  27.2 2.3 copy-start.10
  27.2 2.3 copy-start.15
  29.4 3.8 %collective-permute-start.1 = (bf16[2,16,256]{2,1,0:T(8,128)(2,1)S(1)}, bf16[2,16,256]{2,1,0:T(8,128)(2,1)S(1)}, u32[]{:S(2)}, u32[]{:S(2)}) collective-permute-start(bf16[2,16,256]{2,1,0:T(8,128)(2,1)S(1)} %maximum_select_fusion.5), channel_id=1, source_target_pairs={{0,2},{1,3},{2,0},{3,1},{4,6},{5,7},{6,4},{7,5},{8,10},{9,11},{10,... | collective-permute-start | bytes 49160 | tf_op jit(solution)/shard_map/ppermute | solution.py:278
  29.4 5.8 %copy-start.3 = (f32[8,4,64,64]{2,3,1,0:T(8,128)S(1)}, f32[8,4,64,64]{2,3,1,0:T(8,128)}, u32[]{:S(2)}) copy-start(f32[8,4,64,64]{2,3,1,0:T(8,128)} %get-tuple-element.34) | copy-start | bytes 1572868
  29.4 6.0 %copy-start.2 = (bf16[8,1,512,256]{3,2,1,0:T(8,128)(2,1)S(1)}, bf16[8,1,512,256]{3,2,1,0:T(8,128)(2,1)}, u32[]{:S(2)}) copy-start(bf16[8,1,512,256]{3,2,1,0:T(8,128)(2,1)} %get-tuple-element.27) | copy-start | bytes 6291460
  33.2 4.7 %collective-permute-start.2 = (bf16[4,16,256]{2,1,0:T(8,128)(2,1)S(1)}, bf16[4,16,256]{2,1,0:T(8,128)(2,1)S(1)}, u32[]{:S(2)}, u32[]{:S(2)}) collective-permute-start(bf16[4,16,256]{2,1,0:T(8,128)(2,1)S(1)} %maximum_select_fusion.4), channel_id=1, source_target_pairs={{0,4},{1,5},{2,6},{3,7},{4,0},{5,1},{6,2},{7,3},{8,12},{9,13},{10,... | collective-permute-start | bytes 98312 | tf_op jit(solution)/shard_map/ppermute | solution.py:278
  37.9 7.0 %copy-start.12 = (f32[8,4,64]{2,1,0:T(4,128)}, f32[8,4,64]{2,1,0:T(4,128)S(1)}, u32[]{:S(2)}) copy-start(f32[8,4,64]{2,1,0:T(4,128)S(1)} %add.111) | copy-start | bytes 24580
  37.9 6.9 %collective-permute-start.3 = (bf16[8,16,256]{2,1,0:T(8,128)(2,1)S(1)}, bf16[8,16,256]{2,1,0:T(8,128)(2,1)S(1)}, u32[]{:S(2)}, u32[]{:S(2)}) collective-permute-start(bf16[8,16,256]{2,1,0:T(8,128)(2,1)S(1)} %maximum_select_fusion.3), channel_id=1, source_target_pairs={{0,8},{1,9},{2,10},{3,11},{4,12},{5,13},{6,14},{7,15},{8,0},{9,1},... | collective-permute-start | bytes 196616 | tf_op jit(solution)/shard_map/ppermute | solution.py:278
  44.9 9.7 %collective-permute-start.4 = (bf16[16,16,256]{2,1,0:T(8,128)(2,1)S(1)}, bf16[16,16,256]{2,1,0:T(8,128)(2,1)}, u32[]{:S(2)}, u32[]{:S(2)}) collective-permute-start(bf16[16,16,256]{2,1,0:T(8,128)(2,1)S(1)} %maximum_select_fusion.2), channel_id=1, source_target_pairs={{0,16},{1,17},{2,18},{3,19},{4,20},{5,21},{6,22},{7,23},{8,24},{9,... | collective-permute-start | bytes 393224 | tf_op jit(solution)/shard_map/ppermute | solution.py:278
  55.6 17.1 %collective-permute-start.5 = (bf16[32,16,256]{2,1,0:T(8,128)(2,1)S(1)}, bf16[32,16,256]{2,1,0:T(8,128)(2,1)}, u32[]{:S(2)}, u32[]{:S(2)}) collective-permute-start(bf16[32,16,256]{2,1,0:T(8,128)(2,1)S(1)} %maximum_select_fusion.1), channel_id=1, source_target_pairs={{0,32},{1,33},{2,34},{3,35},{4,36},{5,37},{6,38},{7,39},{8,40},{9,... | collective-permute-start | bytes 786440 | tf_op jit(solution)/shard_map/ppermute | solution.py:278
  68.3 2.9 %copy-start.11 = (bf16[16,3,256]{2,0,1:T(8,128)(2,1)S(1)}, bf16[16,3,256]{2,0,1:T(8,128)(2,1)}, u32[]{:S(2)}) copy-start(bf16[16,3,256]{2,0,1:T(8,128)(2,1)} %param.39) | copy-start | bytes 73732
  68.3 3.5 %copy-start.22 = (s32[8]{0:T(128)S(1)}, s32[8]{0:T(128)}, u32[]{:S(2)}) copy-start(s32[8]{0:T(128)} %param.27) | copy-start | bytes 100
  68.3 5.5 %copy-start.6 = (bf16[8,64,256]{2,1,0:T(8,128)(2,1)S(1)}, bf16[8,64,256]{2,1,0:T(8,128)(2,1)}, u32[]{:S(2)}) copy-start(bf16[8,64,256]{2,1,0:T(8,128)(2,1)} %dot_general.81) | copy-start | bytes 786436
  71.2 3.0 %copy-start.8 = (bf16[8,16,1024]{2,1,0:T(8,128)(2,1)S(1)}, bf16[8,16,1024]{2,1,0:T(8,128)(2,1)}, u32[]{:S(2)}) copy-start(bf16[8,16,1024]{2,1,0:T(8,128)(2,1)} %param.20) | copy-start | bytes 786436
  74.4 45.5 %copy-start.17 = (f32[1024]{0:T(1024)S(1)}, f32[1024]{0:T(1024)}, u32[]{:S(2)}) copy-start(f32[1024]{0:T(1024)} %param.30) | copy-start | bytes 12292
  118.3 3.1 %copy-start.26 = (bf16[32,2,16,256]{3,2,1,0:T(8,128)(2,1)S(1)}, bf16[32,2,16,256]{3,2,1,0:T(8,128)(2,1)}, u32[]{:S(2)}) copy-start(bf16[32,2,16,256]{3,2,1,0:T(8,128)(2,1)} %get-tuple-element.12) | copy-start | bytes 1572868
  122.9 2.0 copy-start.5
  125.6 1.0 copy-start.7
  126.1 50.6 %copy-start = (bf16[8,64,1024]{2,1,0:T(8,128)(2,1)S(1)}, bf16[8,64,1024]{2,1,0:T(8,128)(2,1)}, u32[]{:S(2)}) copy-start(bf16[8,64,1024]{2,1,0:T(8,128)(2,1)} %get-tuple-element.11) | copy-start | bytes 3145732
  126.7 51.8 %copy-start.18 = (f32[1024]{0:T(1024)S(1)}, f32[1024]{0:T(1024)}, u32[]{:S(2)}) copy-start(f32[1024]{0:T(1024)} %param.31) | copy-start | bytes 12292
  176.7 1.8 copy-start.1
  178.4 1.4 copy-start.23
  179.8 1.4 copy-start.25
  229.5 2.5 %copy-start.19 = (f32[1024]{0:T(1024)S(1)}, f32[1024]{0:T(1024)}, u32[]{:S(2)}) copy-start(f32[1024]{0:T(1024)} %param.32) | copy-start | bytes 12292
  231.3 1.5 copy-start.24

commit v6 on v4

--- a/solution.py
+++ b/solution.py
@@ -270,6 +270,65 @@
         return gathered, results[n_in]
     return gathered
 
+def direct_kernel(n_tok, src_ref, out_ref, send_sems, recv_sems, local_sem):
+    grp = lax.axis_index("grp")
+    me = lax.axis_index("tok")
+    mesh_id = pl.DeviceIdType.MESH
+    barrier = pltpu.get_barrier_semaphore()
+    for k in range(1, n_tok):
+        pl.semaphore_signal(
+            barrier, inc=1, device_id=(grp, lax.rem(me + k, n_tok)), device_id_type=mesh_id
+        )
+    pl.semaphore_wait(barrier, n_tok - 1)
+    local = pltpu.make_async_copy(src_ref, out_ref.at[me], local_sem)
+    local.start()
+
+    def remote(k):
+        return pltpu.make_async_remote_copy(
+            src_ref=src_ref,
+            dst_ref=out_ref.at[me],
+            send_sem=send_sems.at[k],
+            recv_sem=recv_sems.at[me],
+            device_id=(grp, lax.rem(me + k, n_tok)),
+            device_id_type=mesh_id,
+        )
+
+    def send(k, carry):
+        remote(k).start()
+        return carry
+
+    lax.fori_loop(1, n_tok, send, 0)
+
+    def arrive(k, carry):
+        other = lax.rem(me + k, n_tok)
+        pltpu.make_async_copy(src_ref, out_ref.at[other], recv_sems.at[other]).wait()
+        remote(k).wait_send()
+        return carry
+
+    lax.fori_loop(1, n_tok, arrive, 0)
+    local.wait()
+
+
+def direct_gather(block, n_tok, after):
+    block, _ = lax.optimization_barrier((block, after))
+    gathered = pl.pallas_call(
+        functools.partial(direct_kernel, n_tok),
+        out_shape=jax.ShapeDtypeStruct((n_tok,) + block.shape, block.dtype),
+        in_specs=[pl.BlockSpec(memory_space=pl.ANY)],
+        out_specs=pl.BlockSpec(memory_space=pl.ANY),
+        scratch_shapes=[
+            pltpu.SemaphoreType.DMA((n_tok,)),
+            pltpu.SemaphoreType.DMA((n_tok,)),
+            pltpu.SemaphoreType.DMA(()),
+        ],
+        compiler_params=pltpu.CompilerParams(collective_id=3, has_side_effects=True),
+        cost_estimate=pl.CostEstimate(
+            flops=0, transcendentals=0, bytes_accessed=2 * n_tok * block.size * block.dtype.itemsize
+        ),
+    )(block)
+    return gathered.reshape((n_tok * block.shape[0],) + block.shape[1:])
+
+
 def layer_sum(summand, base_full):
     return lax.psum(summand.astype(jnp.bfloat16), "grp").astype(jnp.float32) + base_full
 
@@ -307,7 +366,7 @@
     self_context = draft_attention(
         draft_qkv, self_cache, parents, counts, self_len, buckets, bias_table
     )
-    (w_out_self_t,) = fetch_group(lax.axis_size("tok"), 3, (w_out_self.T,), self_context)
+    w_out_self_t = direct_gather(w_out_self.T, lax.axis_size("tok"), self_context)
     partial_value = jnp.einsum(
         "rk,ok->ro", self_context, w_out_self_t, preferred_element_type=jnp.float32
     )

time: 227 us -> 233 us (1.026)
  Pallas kernels: 157 us -> 163 us
    pallas_call x0 -> x1, Pallas kernels: none -> 27.2 us  [direct_gather(): pl.pallas_call(functools.partial(direct_kernel, n_tok), out_shape=jax.Sha...]
    pallas_call x4 -> x3, Pallas kernels: 157 us -> 136 us  [fetch_group(): pl.pallas_call(functools.partial(gather_kernel, n_chips, n_in, n_grp), ou...]
where the time goes in v6:
time: 233 us; the launch traced here: 232 us
  Pallas kernels  163 us (70%)
  local copies, waits for them, and re-layouts  30.3 us (13%)
  matrix products  25.7 us (11%)
  other arithmetic  12 us (5%)
    pallas_call x3, Pallas kernels, fetch_group(): pl.pallas_call(functools.partial(gather_kernel, n_chips, n_in, n_grp), ou...  136 us
    pallas_call x1, Pallas kernels, direct_gather(): pl.pallas_call(functools.partial(direct_kernel, n_tok), out_shape=jax.Sha...  27.2 us
    slice x2, local copies, waits for them, and re-layouts, cross_attention(): enc_keys = cached[:, 0].reshape(requests, -1, local_heads, DH)  6.82 us
    slice x2, local copies, waits for them, and re-layouts, draft_attention(): cache_keys = cached[:, 0].reshape(requests, -1, local_heads, head_size)  6.77 us

profile of v6, /device:TPU:1, one launch (start us, length us, event | category | flops | bytes accessed | tf_op | source)
XLA Modules:
  0.0 232.0 jit_solution(6982250992368645748)
XLA Ops:
  0.6 3.9 %fusion.49 = (bf16[8,1,512,256]{3,2,1,0:T(8,128)(2,1)}, bf16[8,1,512,256]{3,2,1,0:T(8,128)(2,1)S(1)}) fusion(bf16[8,2,512,256]{3,2,1,0:T(8,128)(2,1)} %param.22), kind=kLoop, calls=%fused_computation.90 | loop fusion | bytes 8388608 | tf_op jit(solution)/shard_map/slice | solution.py:36
  4.5 2.4 %copy.41 = bf16[8,1,512,256]{2,3,0,1:T(8,128)(2,1)} copy(bf16[8,1,512,256]{3,2,1,0:T(8,128)(2,1)S(1)} %get-tuple-element.27) | data formatting | bytes 4194304 | tf_op jit(solution)/shard_map/slice | solution.py:37
  6.9 0.2 slice_reduce_fusion
  7.2 2.9 %copy.35 = bf16[8,1,512,256]{2,3,0,1:T(8,128)(2,1)S(1)} copy(bf16[8,1,512,256]{3,2,1,0:T(8,128)(2,1)} %get-tuple-element.26) | data formatting | bytes 4194304 | tf_op jit(solution)/shard_map/slice | solution.py:36
  10.1 1.2 fusion.50
  11.2 0.2 reshape_squeeze.21
  11.5 2.6 %fusion.3 = (f32[8,4,64]{2,1,0:T(4,128)S(1)}, f32[8,4,64,512]{3,2,1,0:T(8,128)}) fusion(f32[4]{0:T(128)S(1)} %slice_reduce_fusion, pred[8,512]{1,0:T(8,128)(4,1)S(1)} %iota_compare_fusion.5, bf16[8,512,4,64]{1,3,2,0:T(8,128)(2,1)S(1)} %bitcast.74, bf16[8,64,4,64]{3,2,1,0:T(4,128)(2,1)S(1)} %reshape_squeeze.21), kind=kOutput, calls=%fused_computation.9 | convolution fusion | flops 137361408 | bytes 6565904 | tf_op jit(solution)/shard_map/rihd,rphd->rhip/dot_general | solution.py:38
  14.1 2.6 %fusion.1 = f32[8,64,64,4]{2,3,1,0:T(4,128)S(1)} fusion(s32[8,64,64]{2,1,0:T(8,128)S(1)} %copy-done.19, f32[32,4]{0,1:T(4,128)S(1)} %copy-done.12), kind=kOutput, calls=%fused_computation.2 | convolution fusion | flops 51380224 | bytes 655872 | tf_op jit(solution)/shard_map/rijb,bh->rhij/dot_general | solution.py:47
  16.7 0.3 copy.40
  17.1 0.2 reshape_squeeze.23
  17.4 0.5 convolution_minimum_fusion.6
  17.9 0.4 convolution_minimum_fusion.5
  18.3 0.4 convolution_minimum_fusion.4
  18.7 0.4 convolution_minimum_fusion.3
  19.1 0.4 convolution_minimum_fusion.2
  19.5 0.4 convolution_minimum_fusion.1
  19.9 0.4 fusion.29
  20.3 0.2 copy.37
  20.5 0.4 fusion.51
  21.0 3.7 %fusion.7 = f32[8,4,64]{2,1,0:T(4,128)S(1)} fusion(f32[8,4,64,512]{3,2,1,0:T(8,128)} %get-tuple-element.32, f32[8,4,64]{2,1,0:T(4,128)S(1)} %max.8, f32[4]{0:T(128)S(1)} %slice_reduce_fusion, pred[8,512]{1,0:T(8,128)(4,1)S(1)} %iota_compare_fusion.5), kind=kLoop, calls=%fused_computation.12 | loop fusion | flops 4192256 | bytes 4214800 | tf_op jit(solution)/shard_map/reduce_sum | solution.py:60
  24.7 0.2 fusion.30
  25.0 2.2 fusion.14
  27.2 0.2 reshape_squeeze.25
  27.4 1.6 fusion.27
  29.1 0.4 copy.44
  29.5 0.3 dot_general.81
  29.8 27.2 %shard_map.203 = bf16[64,16,256]{2,1,0:T(8,128)(2,1)} custom-call(bf16[16,256]{1,0:T(8,128)(2,1)} %bitcast.89), custom_call_target="tpu_custom_call" | custom-call | bytes 1048576 | tf_op jit(solution)/shard_map/pallas_call | solution.py:314
  57.0 1.5 fusion.53
  58.6 0.1 add_dynamic-update-slice_fusion
  58.7 1.1 convert_element_type.81.refs_3_
  59.8 44.7 %shard_map.204 = (bf16[32,2,16,256]{3,2,1,0:T(8,128)(2,1)}, bf16[32,2,16,256]{3,2,1,0:T(8,128)(2,1)}, bf16[32,2,16,704]{3,2,1,0:T(8,128)(2,1)}, bf16[8,64,1024]{2,1,0:T(8,128)(2,1)}) custom-call(bf16[16,256]{1,0:T(8,128)(2,1)} %refs_0_.2, bf16[16,256]{1,0:T(8,128)(2,1)} %bitcast.90, bf16[16,704]{1,0:T(8,128)(2,1)} %refs_2_.1, ...), custom_call_target="tpu_custom_call" | custom-call | bytes 4980736 | tf_op jit(solution)/shard_map/pallas_call | solution.py:259
  104.5 3.9 %fusion.48 = (bf16[8,1,512,256]{3,2,1,0:T(8,128)(2,1)}, bf16[8,1,512,256]{3,2,1,0:T(8,128)(2,1)S(1)}) fusion(bf16[8,2,512,256]{3,2,1,0:T(8,128)(2,1)} %param.23), kind=kLoop, calls=%fused_computation.89 | loop fusion | bytes 8388608 | tf_op jit(solution)/shard_map/slice | solution.py:76
  108.3 2.4 %copy.47 = bf16[8,1,512,256]{2,3,0,1:T(8,128)(2,1)} copy(bf16[8,1,512,256]{3,2,1,0:T(8,128)(2,1)S(1)} %get-tuple-element.25) | data formatting | bytes 4194304 | tf_op jit(solution)/shard_map/slice | solution.py:77
  110.7 2.9 %copy.45 = bf16[8,1,512,256]{2,3,0,1:T(8,128)(2,1)S(1)} copy(bf16[8,1,512,256]{3,2,1,0:T(8,128)(2,1)} %get-tuple-element.24) | data formatting | bytes 4194304 | tf_op jit(solution)/shard_map/slice | solution.py:76
  113.7 0.3 fusion.8
  114.0 0.3 fusion.10
  114.3 0.4 copy-done.18
  114.7 0.4 convolution_convert_fusion.3
  115.2 1.0 reshape_reshape.3
  116.2 1.7 fusion.31
  118.0 1.9 fusion.52
  120.0 0.8 fusion.26
  120.8 0.4 copy.48
  121.2 0.3 dot_general.86
  121.6 0.3 copy-done.5
  121.8 1.4 convolution_convert_fusion.1.refs_2_
  123.3 50.0 %shard_map.205 = (bf16[32,2,16,704]{3,2,1,0:T(8,128)(2,1)}, bf16[32,2,16,704]{3,2,1,0:T(8,128)(2,1)}, bf16[8,64,1024]{2,1,0:T(8,128)(2,1)}) custom-call(bf16[16,704]{1,0:T(8,128)(2,1)} %refs_0_.3, bf16[16,704]{1,0:T(8,128)(2,1)} %bitcast.88, bf16[8,64,1024]{2,1,0:T(8,128)(2,1)} %convolution_convert_fusion.1.refs_2_), custom_call_target="tpu_custom_call" | custom-call | bytes 5767168 | tf_op jit(solution)/shard_map/pallas_call | solution.py:259
  173.3 0.6 copy.56
  173.9 1.6 multiply_reduce_fusion.1
  175.6 0.4 multiply_convert_fusion.1
  176.0 1.0 copy-done.15
  177.0 1.0 fusion.54
  177.9 0.4 copy-done.17
  178.4 2.1 fusion.22
  180.5 1.4 copy.49
  181.8 3.4 %convolution_convert_fusion.refs_1_ = bf16[8,64,1024]{2,1,0:T(8,128)(2,1)} fusion(bf16[8,64,704]{2,1,0:T(8,128)(2,1)S(1)} %bitcast.84, bf16[1024,704,1]{1,0,2:T(8,128)(2,1)} %bitcast.92), kind=kOutput, calls=%fused_computation.29 | convolution fusion | flops 738721792 | bytes 3211264 | tf_op jit(solution)/shard_map/rk,ok->ro/dot_general | solution.py:401
  185.2 41.0 %shard_map.206 = (bf16[32,2,16,768]{3,2,1,0:T(8,128)(2,1)}, bf16[8,64,1024]{2,1,0:T(8,128)(2,1)}) custom-call(bf16[16,768]{1,0:T(8,128)(2,1)} %bitcast.86, bf16[8,64,1024]{2,1,0:T(8,128)(2,1)} %convolution_convert_fusion.refs_1_), custom_call_target="tpu_custom_call" | custom-call | bytes 3145728 | tf_op jit(solution)/shard_map/pallas_call | solution.py:259
  226.3 1.8 multiply_reduce_fusion
  228.1 0.7 dynamic-slice_convert_fusion
  228.8 0.2 multiply_convert_fusion
  229.1 0.5 copy-done.16
  229.6 1.0 convolution_convert_fusion.2
  230.6 0.4 reshape.169
  230.9 1.0 copy.51
  (46 shorter events, 0.3 us)
Async XLA Ops:
  4.5 2.4 %copy-start.12 = (f32[32,4]{0,1:T(4,128)S(1)}, f32[32,4]{0,1:T(4,128)}, u32[]{:S(2)}) copy-start(f32[32,4]{0,1:T(4,128)} %param.29) | copy-start | bytes 1540
  4.5 2.6 %copy-start.13 = (s32[8]{0:T(128)S(1)}, s32[8]{0:T(128)}, u32[]{:S(2)}) copy-start(s32[8]{0:T(128)} %param.26) | copy-start | bytes 100
  11.5 2.6 %copy-start.19 = (s32[8,64,64]{2,1,0:T(8,128)S(1)}, s32[8,64,64]{2,1,0:T(8,128)}, u32[]{:S(2)}) copy-start(s32[8,64,64]{2,1,0:T(8,128)} %param.28) | copy-start | bytes 393220
  14.1 3.2 %copy-start.8 = (s32[8,64]{1,0:T(8,128)S(1)}, s32[8,64]{1,0:T(8,128)}, u32[]{:S(2)}) copy-start(s32[8,64]{1,0:T(8,128)} %param.24) | copy-start | bytes 6148
  17.4 2.5 %copy-start.20 = (s32[8]{0:T(128)S(1)}, s32[8]{0:T(128)}, u32[]{:S(2)}) copy-start(s32[8]{0:T(128)} %param.25) | copy-start | bytes 100
  20.5 4.4 %copy-start.3 = (bf16[8,1,512,256]{2,3,0,1:T(8,128)(2,1)S(1)}, bf16[8,1,512,256]{2,3,0,1:T(8,128)(2,1)}, u32[]{:S(2)}) copy-start(bf16[8,1,512,256]{2,3,0,1:T(8,128)(2,1)} %copy.41) | copy-start | bytes 6291460
  21.0 4.0 %copy-start.1 = (f32[8,4,64,512]{3,2,1,0:T(8,128)S(1)}, f32[8,4,64,512]{3,2,1,0:T(8,128)}, u32[]{:S(2)}) copy-start(f32[8,4,64,512]{3,2,1,0:T(8,128)} %get-tuple-element.32) | copy-start | bytes 12582916
  29.5 29.1 %copy-start.6 = (bf16[8,16,1024]{2,1,0:T(8,128)(2,1)S(1)}, bf16[8,16,1024]{2,1,0:T(8,128)(2,1)}, u32[]{:S(2)}) copy-start(bf16[8,16,1024]{2,1,0:T(8,128)(2,1)} %param.20) | copy-start | bytes 786436
  110.7 3.0 %copy-start = (bf16[8,64,1024]{2,1,0:T(8,128)(2,1)S(1)}, bf16[8,64,1024]{2,1,0:T(8,128)(2,1)}, u32[]{:S(2)}) copy-start(bf16[8,64,1024]{2,1,0:T(8,128)(2,1)} %get-tuple-element.11) | copy-start | bytes 3145732
  110.7 3.3 %copy-start.9 = (f32[1024]{0:T(1024)S(1)}, f32[1024]{0:T(1024)}, u32[]{:S(2)}) copy-start(f32[1024]{0:T(1024)} %param.30) | copy-start | bytes 12292
  113.7 1.0 copy-start.18
  116.2 1.7 copy-start.14
  118.0 2.0 copy-start.4
  120.8 1.0 copy-start.5
  121.2 52.1 %copy-start.7 = (bf16[16,3,256]{2,0,1:T(8,128)(2,1)S(1)}, bf16[16,3,256]{2,0,1:T(8,128)(2,1)}, u32[]{:S(2)}) copy-start(bf16[16,3,256]{2,0,1:T(8,128)(2,1)} %param.39) | copy-start | bytes 73732
  121.8 53.8 %copy-start.10 = (f32[1024]{0:T(1024)S(1)}, f32[1024]{0:T(1024)}, u32[]{:S(2)}) copy-start(f32[1024]{0:T(1024)} %param.31) | copy-start | bytes 12292
  173.3 2.3 copy-start.2
  175.6 1.4 copy-start.15
  177.0 1.4 copy-start.17
  226.3 2.5 %copy-start.11 = (f32[1024]{0:T(1024)S(1)}, f32[1024]{0:T(1024)}, u32[]{:S(2)}) copy-start(f32[1024]{0:T(1024)} %param.32) | copy-start | bytes 12292
  228.1 1.5 copy-start.16

commit v7 on v3

--- a/solution.py
+++ b/solution.py
@@ -100,10 +100,11 @@
         )
         scores = jnp.where(live, scores, -1e30)
         exp_scores = jnp.exp(scores - scores.max(-1, keepdims=True))
-        weights = (exp_scores / exp_scores.sum(-1, keepdims=True)).astype(jnp.bfloat16)
-        o_ref[0, :, cols] = jnp.dot(
-            weights, values[:, cols], preferred_element_type=jnp.float32
-        ).astype(o_ref.dtype)
+        total = exp_scores.sum(-1, keepdims=True)
+        unscaled = jnp.dot(
+            exp_scores.astype(jnp.bfloat16), values[:, cols], preferred_element_type=jnp.float32
+        )
+        o_ref[0, :, cols] = (unscaled / total).astype(o_ref.dtype)
 
 
 def cross_attention_kernel(query_rows, cached, length):
@@ -223,19 +224,6 @@
         for j in range(1, n_grp):
             spread(j).start()
 
-    def arrive(k, carry):
-        other = lax.rem(chip + k, n_chips)
-        for i in range(n_in):
-            remote(i, k).wait_send()
-            pltpu.make_async_copy(
-                srcs[i], outs[i].at[other, core], recv_sems.at[i, other]
-            ).wait()
-        return carry
-
-    lax.fori_loop(1, n_chips, arrive, 0)
-    for copy in locals_:
-        copy.wait()
-
     def forward(i, c):
         return pltpu.make_async_remote_copy(
             src_ref=outs[i].at[c, core],
@@ -246,12 +234,22 @@
             device_id_type=mesh_id,
         )
 
-    def push(c, carry):
+    for i in range(n_in):
+        locals_[i].wait()
+        forward(i, chip).start()
+
+    def arrive(k, carry):
+        other = lax.rem(chip + k, n_chips)
         for i in range(n_in):
-            forward(i, c).start()
+            pltpu.make_async_copy(
+                srcs[i], outs[i].at[other, core], recv_sems.at[i, other]
+            ).wait()
+            forward(i, other).start()
+        for i in range(n_in):
+            remote(i, k).wait_send()
         return carry
 
-    lax.fori_loop(0, n_chips, push, 0)
+    lax.fori_loop(1, n_chips, arrive, 0)
 
     def land(c, carry):
         for i in range(n_in):

time: 232 us -> 228 us (0.983)
  Pallas kernels: 174 us -> 170 us
    pallas_call x1, Pallas kernels: 15.6 us -> 12.7 us  [cross_attention_kernel(): pl.pallas_call(cross_kernel, out_shape=jax.ShapeDtypeStruct(query_rows.sh...]
where the time goes in v7:
time: 228 us; the launch traced here: 227 us
  Pallas kernels  170 us (75%)
  matrix products  24.9 us (11%)
  local copies, waits for them, and re-layouts  18.6 us (8%)
  other arithmetic  12.5 us (5%)
    pallas_call x4, Pallas kernels, fetch_group(): pl.pallas_call(functools.partial(gather_kernel, n_chips, n_in, n_grp), ou...  157 us
    pallas_call x1, Pallas kernels, cross_attention_kernel(): pl.pallas_call(cross_kernel, out_shape=jax.ShapeDtypeStruct(query_rows.sh...  12.7 us
    slice x2, local copies, waits for them, and re-layouts, draft_attention(): cache_keys = cached[:, 0].reshape(requests, -1, local_heads, head_size)  6.76 us
    reduce_sum x3, other arithmetic, rms_scale(): mean_square = jnp.mean(stream * stream, axis=-1, keepdims=True)  4.97 us

profile of v7, /device:TPU:1, one launch (start us, length us, event | category | flops | bytes accessed | tf_op | source)
XLA Modules:
  0.0 226.8 jit_solution(5094358637782303218)
XLA Ops:
  0.6 3.9 %fusion.36 = (bf16[8,1,512,256]{3,2,1,0:T(8,128)(2,1)}, bf16[8,1,512,256]{3,2,1,0:T(8,128)(2,1)S(1)}) fusion(bf16[8,2,512,256]{3,2,1,0:T(8,128)(2,1)} %param.22), kind=kLoop, calls=%fused_computation.75 | loop fusion | bytes 8388608 | tf_op jit(solution)/shard_map/slice | solution.py:36
  4.5 2.4 %copy.38 = bf16[8,1,512,256]{2,3,0,1:T(8,128)(2,1)} copy(bf16[8,1,512,256]{3,2,1,0:T(8,128)(2,1)S(1)} %get-tuple-element.25) | data formatting | bytes 4194304 | tf_op jit(solution)/shard_map/slice | solution.py:37
  6.9 0.2 slice_reduce_fusion
  7.1 0.1 iota_compare_fusion.5
  7.2 2.9 %copy.32 = bf16[8,1,512,256]{2,3,0,1:T(8,128)(2,1)S(1)} copy(bf16[8,1,512,256]{3,2,1,0:T(8,128)(2,1)} %get-tuple-element.24) | data formatting | bytes 4194304 | tf_op jit(solution)/shard_map/slice | solution.py:36
  10.0 1.2 fusion.37
  11.2 0.2 reshape_squeeze.15
  11.4 0.0 copy-start.17
  11.5 2.6 %fusion.2 = (f32[8,4,64]{2,1,0:T(4,128)S(1)}, f32[8,4,64,512]{3,2,1,0:T(8,128)}) fusion(f32[4]{0:T(128)S(1)} %slice_reduce_fusion, pred[8,512]{1,0:T(8,128)(4,1)S(1)} %iota_compare_fusion.5, bf16[8,512,4,64]{1,3,2,0:T(8,128)(2,1)S(1)} %bitcast.69, bf16[8,64,4,64]{3,2,1,0:T(4,128)(2,1)S(1)} %reshape_squeeze.15), kind=kOutput, calls=%fused_computation.6 | convolution fusion | flops 137361408 | bytes 6565904 | tf_op jit(solution)/shard_map/rihd,rphd->rhip/dot_general | solution.py:38
  14.1 0.0 copy-done.17
  14.1 2.6 %fusion = f32[8,64,64,4]{2,3,1,0:T(4,128)S(1)} fusion(s32[8,64,64]{2,1,0:T(8,128)S(1)} %copy-done.17, f32[32,4]{0,1:T(4,128)S(1)} %copy-done.11), kind=kOutput, calls=%fused_computation.1 | convolution fusion | flops 51380224 | bytes 655872 | tf_op jit(solution)/shard_map/rijb,bh->rhij/dot_general | solution.py:47
  16.7 0.3 copy.37
  17.1 0.2 reshape_squeeze.17
  17.3 0.0 copy-start.18
  17.3 0.5 convolution_minimum_fusion.6
  17.9 0.4 convolution_minimum_fusion.5
  18.3 0.4 convolution_minimum_fusion.4
  18.6 0.4 convolution_minimum_fusion.3
  19.0 0.4 convolution_minimum_fusion.2
  19.4 0.4 convolution_minimum_fusion.1
  19.8 0.1 iota_compare_fusion.6
  19.9 0.4 fusion.20
  20.3 0.2 copy.34
  20.5 0.4 fusion.38
  21.0 0.0 copy-start.1
  21.0 3.7 %fusion.3 = f32[8,4,64]{2,1,0:T(4,128)S(1)} fusion(f32[8,4,64,512]{3,2,1,0:T(8,128)} %get-tuple-element.30, f32[8,4,64]{2,1,0:T(4,128)S(1)} %max.8, f32[4]{0:T(128)S(1)} %slice_reduce_fusion, pred[8,512]{1,0:T(8,128)(4,1)S(1)} %iota_compare_fusion.5), kind=kLoop, calls=%fused_computation.7 | loop fusion | flops 4192256 | bytes 4214800 | tf_op jit(solution)/shard_map/reduce_sum | solution.py:60
  24.7 0.2 fusion.21
  24.9 2.2 fusion.7
  27.2 0.2 reshape_squeeze.19
  27.4 1.6 fusion.18
  29.0 0.4 copy.41
  29.5 0.0 copy-start.5
  29.5 0.3 dot_general.73
  29.8 22.1 %shard_map.203 = bf16[32,2,16,256]{3,2,1,0:T(8,128)(2,1)} custom-call(bf16[16,256]{1,0:T(8,128)(2,1)} %bitcast.83), custom_call_target="tpu_custom_call" | custom-call | bytes 1048576 | tf_op jit(solution)/shard_map/pallas_call | solution.py:303
  51.9 1.5 fusion.39
  53.5 0.1 add_dynamic-update-slice_fusion
  53.6 0.0 copy-start.8
  53.6 1.1 convert_element_type.72.refs_3_
  54.7 44.2 %shard_map.204 = (bf16[32,2,16,256]{3,2,1,0:T(8,128)(2,1)}, bf16[32,2,16,256]{3,2,1,0:T(8,128)(2,1)}, bf16[32,2,16,704]{3,2,1,0:T(8,128)(2,1)}, bf16[8,64,1024]{2,1,0:T(8,128)(2,1)}) custom-call(bf16[16,256]{1,0:T(8,128)(2,1)} %refs_0_.2, bf16[16,256]{1,0:T(8,128)(2,1)} %bitcast.84, bf16[16,704]{1,0:T(8,128)(2,1)} %refs_2_.1, ...), custom_call_target="tpu_custom_call" | custom-call | bytes 4980736 | tf_op jit(solution)/shard_map/pallas_call | solution.py:303
  99.0 1.6 fusion.4
  100.5 1.5 fusion.6
  102.1 1.1 convolution_convert_fusion.3
  103.2 12.7 %shard_map.205 = bf16[8,64,256]{2,1,0:T(8,128)(2,1)} custom-call(s32[8]{0:T(128)} %len_ref.1, bf16[8,64,256]{2,1,0:T(8,128)(2,1)} %bitcast.79, bf16[8,2,512,256]{3,2,1,0:T(8,128)(2,1)} %kv_ref.1), custom_call_target="tpu_custom_call" | custom-call | flops 268435456 | bytes 4718592 | tf_op jit(solution)/shard_map/pallas_call | solution.py:113
  115.9 0.0 copy-start.9
  115.9 2.5 %convolution_convert_fusion.1.refs_2_ = bf16[8,64,1024]{2,1,0:T(8,128)(2,1)} fusion(bf16[8,64,256]{2,1,0:T(8,128)(2,1)} %shard_map.205, bf16[1024,256,1]{1,0,2:T(8,128)(2,1)S(1)} %bitcast.78), kind=kOutput, calls=%fused_computation.22 | convolution fusion | flops 268959744 | bytes 1835008 | tf_op jit(solution)/shard_map/rk,ok->ro/dot_general | solution.py:374
  118.4 50.4 %shard_map.206 = (bf16[32,2,16,704]{3,2,1,0:T(8,128)(2,1)}, bf16[32,2,16,704]{3,2,1,0:T(8,128)(2,1)}, bf16[8,64,1024]{2,1,0:T(8,128)(2,1)}) custom-call(bf16[16,704]{1,0:T(8,128)(2,1)} %refs_0_.3, bf16[16,704]{1,0:T(8,128)(2,1)} %bitcast.82, bf16[8,64,1024]{2,1,0:T(8,128)(2,1)} %convolution_convert_fusion.1.refs_2_), custom_call_target="tpu_custom_call" | custom-call | bytes 5767168 | tf_op jit(solution)/shard_map/pallas_call | solution.py:303
  168.8 0.6 copy.49
  169.4 1.6 multiply_reduce_fusion.1
  171.1 0.4 multiply_convert_fusion.1
  171.5 1.0 copy-done.13
  172.5 1.0 fusion.40
  173.4 0.4 copy-done.15
  173.9 2.1 fusion.15
  176.0 1.4 copy.42
  177.3 3.4 %convolution_convert_fusion.refs_1_ = bf16[8,64,1024]{2,1,0:T(8,128)(2,1)} fusion(bf16[8,64,704]{2,1,0:T(8,128)(2,1)S(1)} %bitcast.77, bf16[1024,704,1]{1,0,2:T(8,128)(2,1)} %bitcast.86), kind=kOutput, calls=%fused_computation.21 | convolution fusion | flops 738721792 | bytes 3211264 | tf_op jit(solution)/shard_map/rk,ok->ro/dot_general | solution.py:386
  180.8 40.4 %shard_map.207 = (bf16[32,2,16,768]{3,2,1,0:T(8,128)(2,1)}, bf16[8,64,1024]{2,1,0:T(8,128)(2,1)}) custom-call(bf16[16,768]{1,0:T(8,128)(2,1)} %bitcast.80, bf16[8,64,1024]{2,1,0:T(8,128)(2,1)} %convolution_convert_fusion.refs_1_), custom_call_target="tpu_custom_call" | custom-call | bytes 3145728 | tf_op jit(solution)/shard_map/pallas_call | solution.py:303
  221.2 0.0 copy-start.10
  221.2 1.8 multiply_reduce_fusion
  222.9 0.7 dynamic-slice_convert_fusion
  223.7 0.2 multiply_convert_fusion
  223.9 0.5 copy-done.14
  224.4 1.0 convolution_convert_fusion.2
  225.4 0.4 reshape.154
  225.8 1.0 copy.44
  (33 shorter events, 0.1 us)
Async XLA Ops:
  4.5 2.4 %copy-start.11 = (f32[32,4]{0,1:T(4,128)S(1)}, f32[32,4]{0,1:T(4,128)}, u32[]{:S(2)}) copy-start(f32[32,4]{0,1:T(4,128)} %param.29) | copy-start | bytes 1540
  4.5 2.6 %copy-start.12 = (s32[8]{0:T(128)S(1)}, s32[8]{0:T(128)}, u32[]{:S(2)}) copy-start(s32[8]{0:T(128)} %param.26) | copy-start | bytes 100
  11.4 2.7 %copy-start.17 = (s32[8,64,64]{2,1,0:T(8,128)S(1)}, s32[8,64,64]{2,1,0:T(8,128)}, u32[]{:S(2)}) copy-start(s32[8,64,64]{2,1,0:T(8,128)} %param.28) | copy-start | bytes 393220
  14.1 3.2 %copy-start.7 = (s32[8,64]{1,0:T(8,128)S(1)}, s32[8,64]{1,0:T(8,128)}, u32[]{:S(2)}) copy-start(s32[8,64]{1,0:T(8,128)} %param.24) | copy-start | bytes 6148
  17.3 2.5 %copy-start.18 = (s32[8]{0:T(128)S(1)}, s32[8]{0:T(128)}, u32[]{:S(2)}) copy-start(s32[8]{0:T(128)} %param.25) | copy-start | bytes 100
  20.5 4.4 %copy-start.3 = (bf16[8,1,512,256]{2,3,0,1:T(8,128)(2,1)S(1)}, bf16[8,1,512,256]{2,3,0,1:T(8,128)(2,1)}, u32[]{:S(2)}) copy-start(bf16[8,1,512,256]{2,3,0,1:T(8,128)(2,1)} %copy.38) | copy-start | bytes 6291460
  21.0 4.0 %copy-start.1 = (f32[8,4,64,512]{3,2,1,0:T(8,128)S(1)}, f32[8,4,64,512]{3,2,1,0:T(8,128)}, u32[]{:S(2)}) copy-start(f32[8,4,64,512]{3,2,1,0:T(8,128)} %get-tuple-element.30) | copy-start | bytes 12582916
  29.5 24.0 %copy-start.5 = (bf16[8,16,1024]{2,1,0:T(8,128)(2,1)S(1)}, bf16[8,16,1024]{2,1,0:T(8,128)(2,1)}, u32[]{:S(2)}) copy-start(bf16[8,16,1024]{2,1,0:T(8,128)(2,1)} %param.20) | copy-start | bytes 786436
  53.6 47.0 %copy-start.8 = (f32[1024]{0:T(1024)S(1)}, f32[1024]{0:T(1024)}, u32[]{:S(2)}) copy-start(f32[1024]{0:T(1024)} %param.30) | copy-start | bytes 12292
  99.0 3.1 %copy-start.16 = (bf16[32,2,16,256]{3,2,1,0:T(8,128)(2,1)S(1)}, bf16[32,2,16,256]{3,2,1,0:T(8,128)(2,1)}, u32[]{:S(2)}) copy-start(bf16[32,2,16,256]{3,2,1,0:T(8,128)(2,1)} %get-tuple-element.12) | copy-start | bytes 1572868
  103.2 12.7 %copy-start.4 = (bf16[32,2,16,256]{3,2,1,0:T(8,128)(2,1)S(1)}, bf16[32,2,16,256]{3,2,1,0:T(8,128)(2,1)}, u32[]{:S(2)}) copy-start(bf16[32,2,16,256]{3,2,1,0:T(8,128)(2,1)} %get-tuple-element.13) | copy-start | bytes 1572868
  115.9 52.9 %copy-start.6 = (bf16[16,3,256]{2,0,1:T(8,128)(2,1)S(1)}, bf16[16,3,256]{2,0,1:T(8,128)(2,1)}, u32[]{:S(2)}) copy-start(bf16[16,3,256]{2,0,1:T(8,128)(2,1)} %param.39) | copy-start | bytes 73732
  115.9 53.5 %copy-start = (bf16[8,64,1024]{2,1,0:T(8,128)(2,1)S(1)}, bf16[8,64,1024]{2,1,0:T(8,128)(2,1)}, u32[]{:S(2)}) copy-start(bf16[8,64,1024]{2,1,0:T(8,128)(2,1)} %get-tuple-element.11) | copy-start | bytes 3145732
  115.9 55.2 %copy-start.9 = (f32[1024]{0:T(1024)S(1)}, f32[1024]{0:T(1024)}, u32[]{:S(2)}) copy-start(f32[1024]{0:T(1024)} %param.31) | copy-start | bytes 12292
  168.8 2.3 %copy-start.2 = (bf16[8,64,1024]{2,1,0:T(8,128)(2,1)S(1)}, bf16[8,64,1024]{2,1,0:T(8,128)(2,1)}, u32[]{:S(2)}) copy-start(bf16[8,64,1024]{2,1,0:T(8,128)(2,1)} %get-tuple-element.14) | copy-start | bytes 3145732
  171.0 1.4 copy-start.13
  172.5 1.4 copy-start.15
  221.2 2.5 %copy-start.10 = (f32[1024]{0:T(1024)S(1)}, f32[1024]{0:T(1024)}, u32[]{:S(2)}) copy-start(f32[1024]{0:T(1024)} %param.32) | copy-start | bytes 12292
  222.9 1.5 copy-start.14

commit v8 on v7

--- a/solution.py
+++ b/solution.py
@@ -93,19 +93,22 @@
     keys = kv_ref[0, 0]
     values = kv_ref[0, 1]
     live = lax.broadcasted_iota(jnp.int32, (q.shape[0], keys.shape[0]), 1) < length
+    head_of = lax.broadcasted_iota(jnp.int32, q.shape, 1) // DH
+    result = jnp.zeros(q.shape, jnp.float32)
     for h in range(q.shape[1] // DH):
-        cols = slice(h * DH, (h + 1) * DH)
+        own = head_of == h
         scores = lax.dot_general(
-            q[:, cols], keys[:, cols], (((1,), (1,)), ((), ())), preferred_element_type=jnp.float32
+            jnp.where(own, q, jnp.zeros_like(q)), keys, (((1,), (1,)), ((), ())),
+            preferred_element_type=jnp.float32,
         )
         scores = jnp.where(live, scores, -1e30)
         exp_scores = jnp.exp(scores - scores.max(-1, keepdims=True))
         total = exp_scores.sum(-1, keepdims=True)
         unscaled = jnp.dot(
-            exp_scores.astype(jnp.bfloat16), values[:, cols], preferred_element_type=jnp.float32
+            exp_scores.astype(jnp.bfloat16), values, preferred_element_type=jnp.float32
         )
-        o_ref[0, :, cols] = (unscaled / total).astype(o_ref.dtype)
-
+        result = jnp.where(own, unscaled / total, result)
+    o_ref[0] = result.astype(o_ref.dtype)
 
 def cross_attention_kernel(query_rows, cached, length):
     requests, draft_slots, head_width = query_rows.shape

time: 228 us -> 229 us (level)
  no operation moved by 1% of the time
where the time goes in v8:
time: 229 us; the launch traced here: 228 us
  Pallas kernels  171 us (75%)
  matrix products  24.9 us (11%)
  local copies, waits for them, and re-layouts  18.6 us (8%)
  other arithmetic  12.5 us (5%)
    pallas_call x4, Pallas kernels, fetch_group(): pl.pallas_call(functools.partial(gather_kernel, n_chips, n_in, n_grp), ou...  157 us
    pallas_call x1, Pallas kernels, cross_attention_kernel(): pl.pallas_call(cross_kernel, out_shape=jax.ShapeDtypeStruct(query_rows.sh...  13.9 us
    slice x2, local copies, waits for them, and re-layouts, draft_attention(): cache_keys = cached[:, 0].reshape(requests, -1, local_heads, head_size)  6.76 us
    reduce_sum x3, other arithmetic, rms_scale(): mean_square = jnp.mean(stream * stream, axis=-1, keepdims=True)  4.97 us

profile of v8, /device:TPU:1, one launch (start us, length us, event | category | flops | bytes accessed | tf_op | source)
XLA Modules:
  0.0 228.1 jit_solution(6656646103953187337)
XLA Ops:
  0.6 3.9 %fusion.36 = (bf16[8,1,512,256]{3,2,1,0:T(8,128)(2,1)}, bf16[8,1,512,256]{3,2,1,0:T(8,128)(2,1)S(1)}) fusion(bf16[8,2,512,256]{3,2,1,0:T(8,128)(2,1)} %param.22), kind=kLoop, calls=%fused_computation.75 | loop fusion | bytes 8388608 | tf_op jit(solution)/shard_map/slice | solution.py:36
  4.5 2.4 %copy.38 = bf16[8,1,512,256]{2,3,0,1:T(8,128)(2,1)} copy(bf16[8,1,512,256]{3,2,1,0:T(8,128)(2,1)S(1)} %get-tuple-element.25) | data formatting | bytes 4194304 | tf_op jit(solution)/shard_map/slice | solution.py:37
  6.9 0.2 slice_reduce_fusion
  7.1 0.1 iota_compare_fusion.5
  7.2 2.9 %copy.32 = bf16[8,1,512,256]{2,3,0,1:T(8,128)(2,1)S(1)} copy(bf16[8,1,512,256]{3,2,1,0:T(8,128)(2,1)} %get-tuple-element.24) | data formatting | bytes 4194304 | tf_op jit(solution)/shard_map/slice | solution.py:36
  10.0 1.2 fusion.37
  11.2 0.2 reshape_squeeze.15
  11.4 0.0 copy-start.17
  11.5 2.6 %fusion.2 = (f32[8,4,64]{2,1,0:T(4,128)S(1)}, f32[8,4,64,512]{3,2,1,0:T(8,128)}) fusion(f32[4]{0:T(128)S(1)} %slice_reduce_fusion, pred[8,512]{1,0:T(8,128)(4,1)S(1)} %iota_compare_fusion.5, bf16[8,512,4,64]{1,3,2,0:T(8,128)(2,1)S(1)} %bitcast.69, bf16[8,64,4,64]{3,2,1,0:T(4,128)(2,1)S(1)} %reshape_squeeze.15), kind=kOutput, calls=%fused_computation.6 | convolution fusion | flops 137361408 | bytes 6565904 | tf_op jit(solution)/shard_map/rihd,rphd->rhip/dot_general | solution.py:38
  14.1 0.0 copy-done.17
  14.1 2.6 %fusion = f32[8,64,64,4]{2,3,1,0:T(4,128)S(1)} fusion(s32[8,64,64]{2,1,0:T(8,128)S(1)} %copy-done.17, f32[32,4]{0,1:T(4,128)S(1)} %copy-done.11), kind=kOutput, calls=%fused_computation.1 | convolution fusion | flops 51380224 | bytes 655872 | tf_op jit(solution)/shard_map/rijb,bh->rhij/dot_general | solution.py:47
  16.7 0.3 copy.37
  17.1 0.2 reshape_squeeze.17
  17.3 0.0 copy-start.18
  17.3 0.5 convolution_minimum_fusion.6
  17.9 0.4 convolution_minimum_fusion.5
  18.3 0.4 convolution_minimum_fusion.4
  18.6 0.4 convolution_minimum_fusion.3
  19.0 0.4 convolution_minimum_fusion.2
  19.4 0.4 convolution_minimum_fusion.1
  19.8 0.1 iota_compare_fusion.6
  19.9 0.4 fusion.20
  20.3 0.2 copy.34
  20.5 0.4 fusion.38
  21.0 0.0 copy-start.1
  21.0 3.7 %fusion.3 = f32[8,4,64]{2,1,0:T(4,128)S(1)} fusion(f32[8,4,64,512]{3,2,1,0:T(8,128)} %get-tuple-element.30, f32[8,4,64]{2,1,0:T(4,128)S(1)} %max.8, f32[4]{0:T(128)S(1)} %slice_reduce_fusion, pred[8,512]{1,0:T(8,128)(4,1)S(1)} %iota_compare_fusion.5), kind=kLoop, calls=%fused_computation.7 | loop fusion | flops 4192256 | bytes 4214800 | tf_op jit(solution)/shard_map/reduce_sum | solution.py:60
  24.7 0.2 fusion.21
  24.9 2.2 fusion.7
  27.2 0.2 reshape_squeeze.19
  27.4 1.6 fusion.18
  29.0 0.4 copy.41
  29.5 0.0 copy-start.5
  29.5 0.3 dot_general.73
  29.8 22.1 %shard_map.203 = bf16[32,2,16,256]{3,2,1,0:T(8,128)(2,1)} custom-call(bf16[16,256]{1,0:T(8,128)(2,1)} %bitcast.83), custom_call_target="tpu_custom_call" | custom-call | bytes 1048576 | tf_op jit(solution)/shard_map/pallas_call | solution.py:306
  51.9 1.5 fusion.39
  53.5 0.1 add_dynamic-update-slice_fusion
  53.6 0.0 copy-start.8
  53.6 1.1 convert_element_type.72.refs_3_
  54.7 44.2 %shard_map.204 = (bf16[32,2,16,256]{3,2,1,0:T(8,128)(2,1)}, bf16[32,2,16,256]{3,2,1,0:T(8,128)(2,1)}, bf16[32,2,16,704]{3,2,1,0:T(8,128)(2,1)}, bf16[8,64,1024]{2,1,0:T(8,128)(2,1)}) custom-call(bf16[16,256]{1,0:T(8,128)(2,1)} %refs_0_.2, bf16[16,256]{1,0:T(8,128)(2,1)} %bitcast.84, bf16[16,704]{1,0:T(8,128)(2,1)} %refs_2_.1, ...), custom_call_target="tpu_custom_call" | custom-call | bytes 4980736 | tf_op jit(solution)/shard_map/pallas_call | solution.py:306
  99.0 1.6 fusion.4
  100.5 1.5 fusion.6
  102.1 1.1 convolution_convert_fusion.3
  103.2 13.9 %shard_map.205 = bf16[8,64,256]{2,1,0:T(8,128)(2,1)} custom-call(s32[8]{0:T(128)} %len_ref.1, bf16[8,64,256]{2,1,0:T(8,128)(2,1)} %bitcast.79, bf16[8,2,512,256]{3,2,1,0:T(8,128)(2,1)} %kv_ref.1), custom_call_target="tpu_custom_call" | custom-call | flops 268435456 | bytes 4718592 | tf_op jit(solution)/shard_map/pallas_call | solution.py:116
  117.2 0.0 copy-start.9
  117.2 2.5 %convolution_convert_fusion.1.refs_2_ = bf16[8,64,1024]{2,1,0:T(8,128)(2,1)} fusion(bf16[8,64,256]{2,1,0:T(8,128)(2,1)} %shard_map.205, bf16[1024,256,1]{1,0,2:T(8,128)(2,1)S(1)} %bitcast.78), kind=kOutput, calls=%fused_computation.22 | convolution fusion | flops 268959744 | bytes 1835008 | tf_op jit(solution)/shard_map/rk,ok->ro/dot_general | solution.py:377
  119.6 50.4 %shard_map.206 = (bf16[32,2,16,704]{3,2,1,0:T(8,128)(2,1)}, bf16[32,2,16,704]{3,2,1,0:T(8,128)(2,1)}, bf16[8,64,1024]{2,1,0:T(8,128)(2,1)}) custom-call(bf16[16,704]{1,0:T(8,128)(2,1)} %refs_0_.3, bf16[16,704]{1,0:T(8,128)(2,1)} %bitcast.82, bf16[8,64,1024]{2,1,0:T(8,128)(2,1)} %convolution_convert_fusion.1.refs_2_), custom_call_target="tpu_custom_call" | custom-call | bytes 5767168 | tf_op jit(solution)/shard_map/pallas_call | solution.py:306
  170.1 0.6 copy.49
  170.7 1.6 multiply_reduce_fusion.1
  172.3 0.4 multiply_convert_fusion.1
  172.7 1.0 copy-done.13
  173.7 1.0 fusion.40
  174.7 0.4 copy-done.15
  175.1 2.1 fusion.15
  177.2 1.4 copy.42
  178.6 3.4 %convolution_convert_fusion.refs_1_ = bf16[8,64,1024]{2,1,0:T(8,128)(2,1)} fusion(bf16[8,64,704]{2,1,0:T(8,128)(2,1)S(1)} %bitcast.77, bf16[1024,704,1]{1,0,2:T(8,128)(2,1)} %bitcast.86), kind=kOutput, calls=%fused_computation.21 | convolution fusion | flops 738721792 | bytes 3211264 | tf_op jit(solution)/shard_map/rk,ok->ro/dot_general | solution.py:389
  182.0 40.4 %shard_map.207 = (bf16[32,2,16,768]{3,2,1,0:T(8,128)(2,1)}, bf16[8,64,1024]{2,1,0:T(8,128)(2,1)}) custom-call(bf16[16,768]{1,0:T(8,128)(2,1)} %bitcast.80, bf16[8,64,1024]{2,1,0:T(8,128)(2,1)} %convolution_convert_fusion.refs_1_), custom_call_target="tpu_custom_call" | custom-call | bytes 3145728 | tf_op jit(solution)/shard_map/pallas_call | solution.py:306
  222.4 0.0 copy-start.10
  222.4 1.8 multiply_reduce_fusion
  224.2 0.7 dynamic-slice_convert_fusion
  224.9 0.2 multiply_convert_fusion
  225.2 0.5 copy-done.14
  225.7 1.0 convolution_convert_fusion.2
  226.7 0.4 reshape.154
  227.0 1.0 copy.44
  (33 shorter events, 0.1 us)
Async XLA Ops:
  4.5 2.4 %copy-start.11 = (f32[32,4]{0,1:T(4,128)S(1)}, f32[32,4]{0,1:T(4,128)}, u32[]{:S(2)}) copy-start(f32[32,4]{0,1:T(4,128)} %param.29) | copy-start | bytes 1540
  4.5 2.6 %copy-start.12 = (s32[8]{0:T(128)S(1)}, s32[8]{0:T(128)}, u32[]{:S(2)}) copy-start(s32[8]{0:T(128)} %param.26) | copy-start | bytes 100
  11.4 2.7 %copy-start.17 = (s32[8,64,64]{2,1,0:T(8,128)S(1)}, s32[8,64,64]{2,1,0:T(8,128)}, u32[]{:S(2)}) copy-start(s32[8,64,64]{2,1,0:T(8,128)} %param.28) | copy-start | bytes 393220
  14.1 3.2 %copy-start.7 = (s32[8,64]{1,0:T(8,128)S(1)}, s32[8,64]{1,0:T(8,128)}, u32[]{:S(2)}) copy-start(s32[8,64]{1,0:T(8,128)} %param.24) | copy-start | bytes 6148
  17.3 2.5 %copy-start.18 = (s32[8]{0:T(128)S(1)}, s32[8]{0:T(128)}, u32[]{:S(2)}) copy-start(s32[8]{0:T(128)} %param.25) | copy-start | bytes 100
  20.5 4.4 %copy-start.3 = (bf16[8,1,512,256]{2,3,0,1:T(8,128)(2,1)S(1)}, bf16[8,1,512,256]{2,3,0,1:T(8,128)(2,1)}, u32[]{:S(2)}) copy-start(bf16[8,1,512,256]{2,3,0,1:T(8,128)(2,1)} %copy.38) | copy-start | bytes 6291460
  21.0 4.0 %copy-start.1 = (f32[8,4,64,512]{3,2,1,0:T(8,128)S(1)}, f32[8,4,64,512]{3,2,1,0:T(8,128)}, u32[]{:S(2)}) copy-start(f32[8,4,64,512]{3,2,1,0:T(8,128)} %get-tuple-element.30) | copy-start | bytes 12582916
  29.5 24.0 %copy-start.5 = (bf16[8,16,1024]{2,1,0:T(8,128)(2,1)S(1)}, bf16[8,16,1024]{2,1,0:T(8,128)(2,1)}, u32[]{:S(2)}) copy-start(bf16[8,16,1024]{2,1,0:T(8,128)(2,1)} %param.20) | copy-start | bytes 786436
  53.6 47.0 %copy-start.8 = (f32[1024]{0:T(1024)S(1)}, f32[1024]{0:T(1024)}, u32[]{:S(2)}) copy-start(f32[1024]{0:T(1024)} %param.30) | copy-start | bytes 12292
  99.0 3.1 %copy-start.16 = (bf16[32,2,16,256]{3,2,1,0:T(8,128)(2,1)S(1)}, bf16[32,2,16,256]{3,2,1,0:T(8,128)(2,1)}, u32[]{:S(2)}) copy-start(bf16[32,2,16,256]{3,2,1,0:T(8,128)(2,1)} %get-tuple-element.12) | copy-start | bytes 1572868
  103.2 13.9 %copy-start.4 = (bf16[32,2,16,256]{3,2,1,0:T(8,128)(2,1)S(1)}, bf16[32,2,16,256]{3,2,1,0:T(8,128)(2,1)}, u32[]{:S(2)}) copy-start(bf16[32,2,16,256]{3,2,1,0:T(8,128)(2,1)} %get-tuple-element.13) | copy-start | bytes 1572868
  117.1 52.9 %copy-start.6 = (bf16[16,3,256]{2,0,1:T(8,128)(2,1)S(1)}, bf16[16,3,256]{2,0,1:T(8,128)(2,1)}, u32[]{:S(2)}) copy-start(bf16[16,3,256]{2,0,1:T(8,128)(2,1)} %param.39) | copy-start | bytes 73732
  117.1 53.5 %copy-start = (bf16[8,64,1024]{2,1,0:T(8,128)(2,1)S(1)}, bf16[8,64,1024]{2,1,0:T(8,128)(2,1)}, u32[]{:S(2)}) copy-start(bf16[8,64,1024]{2,1,0:T(8,128)(2,1)} %get-tuple-element.11) | copy-start | bytes 3145732
  117.2 55.2 %copy-start.9 = (f32[1024]{0:T(1024)S(1)}, f32[1024]{0:T(1024)}, u32[]{:S(2)}) copy-start(f32[1024]{0:T(1024)} %param.31) | copy-start | bytes 12292
  170.0 2.3 %copy-start.2 = (bf16[8,64,1024]{2,1,0:T(8,128)(2,1)S(1)}, bf16[8,64,1024]{2,1,0:T(8,128)(2,1)}, u32[]{:S(2)}) copy-start(bf16[8,64,1024]{2,1,0:T(8,128)(2,1)} %get-tuple-element.14) | copy-start | bytes 3145732
  172.3 1.4 copy-start.13
  173.7 1.4 copy-start.15
  222.4 2.5 %copy-start.10 = (f32[1024]{0:T(1024)S(1)}, f32[1024]{0:T(1024)}, u32[]{:S(2)}) copy-start(f32[1024]{0:T(1024)} %param.32) | copy-start | bytes 12292
  224.2 1.5 copy-start.14

commit v9 on v4

--- a/solution.py
+++ b/solution.py
@@ -133,13 +133,6 @@
             device_id_type=mesh_id,
         )
 
-    def send(k, carry):
-        for i in range(n_in):
-            remote(i, k).start()
-        return carry
-
-    lax.fori_loop(1, n_chips, send, 0)
-
     if n_grp:
         quarter = summand.shape[1] // n_grp
 
@@ -156,6 +149,14 @@
 
         for j in range(1, n_grp):
             scatter(j).start()
+    def send(k, carry):
+        for i in range(n_in):
+            remote(i, k).start()
+        return carry
+
+    lax.fori_loop(1, n_chips, send, 0)
+
+    if n_grp:
         for j in range(1, n_grp):
             scatter(j).wait_send()
             source = lax.rem(grp + j, n_grp)

time: 227 us -> 227 us (level)
  no operation moved by 1% of the time
where the time goes in v9:
time: 227 us; the launch traced here: 226 us
  Pallas kernels  157 us (69%)
  local copies, waits for them, and re-layouts  30.3 us (13%)
  matrix products  25.7 us (11%)
  other arithmetic  12 us (5%)
    pallas_call x4, Pallas kernels, fetch_group(): pl.pallas_call(functools.partial(gather_kernel, n_chips, n_in, n_grp), ou...  157 us
    slice x2, local copies, waits for them, and re-layouts, cross_attention(): enc_keys = cached[:, 0].reshape(requests, -1, local_heads, DH)  6.82 us
    slice x2, local copies, waits for them, and re-layouts, draft_attention(): cache_keys = cached[:, 0].reshape(requests, -1, local_heads, head_size)  6.77 us

profile of v9, /device:TPU:1, one launch (start us, length us, event | category | flops | bytes accessed | tf_op | source)
XLA Modules:
  0.0 226.2 jit_solution(7212189320232783664)
XLA Ops:
  0.6 3.9 %fusion.49 = (bf16[8,1,512,256]{3,2,1,0:T(8,128)(2,1)}, bf16[8,1,512,256]{3,2,1,0:T(8,128)(2,1)S(1)}) fusion(bf16[8,2,512,256]{3,2,1,0:T(8,128)(2,1)} %param.22), kind=kLoop, calls=%fused_computation.90 | loop fusion | bytes 8388608 | tf_op jit(solution)/shard_map/slice | solution.py:36
  4.5 2.4 %copy.41 = bf16[8,1,512,256]{2,3,0,1:T(8,128)(2,1)} copy(bf16[8,1,512,256]{3,2,1,0:T(8,128)(2,1)S(1)} %get-tuple-element.27) | data formatting | bytes 4194304 | tf_op jit(solution)/shard_map/slice | solution.py:37
  6.9 0.2 slice_reduce_fusion
  7.2 2.9 %copy.35 = bf16[8,1,512,256]{2,3,0,1:T(8,128)(2,1)S(1)} copy(bf16[8,1,512,256]{3,2,1,0:T(8,128)(2,1)} %get-tuple-element.26) | data formatting | bytes 4194304 | tf_op jit(solution)/shard_map/slice | solution.py:36
  10.1 1.2 fusion.50
  11.2 0.2 reshape_squeeze.21
  11.5 2.6 %fusion.3 = (f32[8,4,64]{2,1,0:T(4,128)S(1)}, f32[8,4,64,512]{3,2,1,0:T(8,128)}) fusion(f32[4]{0:T(128)S(1)} %slice_reduce_fusion, pred[8,512]{1,0:T(8,128)(4,1)S(1)} %iota_compare_fusion.5, bf16[8,512,4,64]{1,3,2,0:T(8,128)(2,1)S(1)} %bitcast.74, bf16[8,64,4,64]{3,2,1,0:T(4,128)(2,1)S(1)} %reshape_squeeze.21), kind=kOutput, calls=%fused_computation.9 | convolution fusion | flops 137361408 | bytes 6565904 | tf_op jit(solution)/shard_map/rihd,rphd->rhip/dot_general | solution.py:38
  14.1 2.6 %fusion.1 = f32[8,64,64,4]{2,3,1,0:T(4,128)S(1)} fusion(s32[8,64,64]{2,1,0:T(8,128)S(1)} %copy-done.19, f32[32,4]{0,1:T(4,128)S(1)} %copy-done.12), kind=kOutput, calls=%fused_computation.2 | convolution fusion | flops 51380224 | bytes 655872 | tf_op jit(solution)/shard_map/rijb,bh->rhij/dot_general | solution.py:47
  16.7 0.3 copy.40
  17.1 0.2 reshape_squeeze.23
  17.4 0.5 convolution_minimum_fusion.6
  17.9 0.4 convolution_minimum_fusion.5
  18.3 0.4 convolution_minimum_fusion.4
  18.7 0.4 convolution_minimum_fusion.3
  19.1 0.4 convolution_minimum_fusion.2
  19.5 0.4 convolution_minimum_fusion.1
  19.9 0.4 fusion.29
  20.3 0.2 copy.37
  20.5 0.4 fusion.51
  21.0 3.7 %fusion.7 = f32[8,4,64]{2,1,0:T(4,128)S(1)} fusion(f32[8,4,64,512]{3,2,1,0:T(8,128)} %get-tuple-element.32, f32[8,4,64]{2,1,0:T(4,128)S(1)} %max.8, f32[4]{0:T(128)S(1)} %slice_reduce_fusion, pred[8,512]{1,0:T(8,128)(4,1)S(1)} %iota_compare_fusion.5), kind=kLoop, calls=%fused_computation.12 | loop fusion | flops 4192256 | bytes 4214800 | tf_op jit(solution)/shard_map/reduce_sum | solution.py:60
  24.7 0.2 fusion.30
  25.0 2.2 fusion.14
  27.2 0.2 reshape_squeeze.25
  27.4 1.6 fusion.27
  29.1 0.4 copy.44
  29.5 0.3 dot_general.81
  29.8 22.1 %shard_map.203 = bf16[32,2,16,256]{3,2,1,0:T(8,128)(2,1)} custom-call(bf16[16,256]{1,0:T(8,128)(2,1)} %bitcast.89), custom_call_target="tpu_custom_call" | custom-call | bytes 1048576 | tf_op jit(solution)/shard_map/pallas_call | solution.py:260
  52.0 1.5 fusion.53
  53.5 0.1 add_dynamic-update-slice_fusion
  53.6 1.1 convert_element_type.81.refs_3_
  54.7 44.3 %shard_map.204 = (bf16[32,2,16,256]{3,2,1,0:T(8,128)(2,1)}, bf16[32,2,16,256]{3,2,1,0:T(8,128)(2,1)}, bf16[32,2,16,704]{3,2,1,0:T(8,128)(2,1)}, bf16[8,64,1024]{2,1,0:T(8,128)(2,1)}) custom-call(bf16[16,256]{1,0:T(8,128)(2,1)} %refs_0_.2, bf16[16,256]{1,0:T(8,128)(2,1)} %bitcast.90, bf16[16,704]{1,0:T(8,128)(2,1)} %refs_2_.1, ...), custom_call_target="tpu_custom_call" | custom-call | bytes 4980736 | tf_op jit(solution)/shard_map/pallas_call | solution.py:260
  99.0 3.9 %fusion.48 = (bf16[8,1,512,256]{3,2,1,0:T(8,128)(2,1)}, bf16[8,1,512,256]{3,2,1,0:T(8,128)(2,1)S(1)}) fusion(bf16[8,2,512,256]{3,2,1,0:T(8,128)(2,1)} %param.23), kind=kLoop, calls=%fused_computation.89 | loop fusion | bytes 8388608 | tf_op jit(solution)/shard_map/slice | solution.py:76
  102.9 2.4 %copy.47 = bf16[8,1,512,256]{2,3,0,1:T(8,128)(2,1)} copy(bf16[8,1,512,256]{3,2,1,0:T(8,128)(2,1)S(1)} %get-tuple-element.25) | data formatting | bytes 4194304 | tf_op jit(solution)/shard_map/slice | solution.py:77
  105.2 2.9 %copy.45 = bf16[8,1,512,256]{2,3,0,1:T(8,128)(2,1)S(1)} copy(bf16[8,1,512,256]{3,2,1,0:T(8,128)(2,1)} %get-tuple-element.24) | data formatting | bytes 4194304 | tf_op jit(solution)/shard_map/slice | solution.py:76
  108.2 0.3 fusion.8
  108.5 0.3 fusion.10
  108.8 0.4 copy-done.18
  109.2 0.4 convolution_convert_fusion.3
  109.7 1.0 reshape_reshape.3
  110.7 1.7 fusion.31
  112.6 1.9 fusion.52
  114.5 0.8 fusion.26
  115.3 0.4 copy.48
  115.8 0.3 dot_general.86
  116.1 0.3 copy-done.5
  116.4 1.4 convolution_convert_fusion.1.refs_2_
  117.8 50.5 %shard_map.205 = (bf16[32,2,16,704]{3,2,1,0:T(8,128)(2,1)}, bf16[32,2,16,704]{3,2,1,0:T(8,128)(2,1)}, bf16[8,64,1024]{2,1,0:T(8,128)(2,1)}) custom-call(bf16[16,704]{1,0:T(8,128)(2,1)} %refs_0_.3, bf16[16,704]{1,0:T(8,128)(2,1)} %bitcast.88, bf16[8,64,1024]{2,1,0:T(8,128)(2,1)} %convolution_convert_fusion.1.refs_2_), custom_call_target="tpu_custom_call" | custom-call | bytes 5767168 | tf_op jit(solution)/shard_map/pallas_call | solution.py:260
  168.3 0.6 copy.56
  168.9 1.6 multiply_reduce_fusion.1
  170.6 0.4 multiply_convert_fusion.1
  171.0 1.0 copy-done.15
  172.0 1.0 fusion.54
  172.9 0.4 copy-done.17
  173.4 2.1 fusion.22
  175.5 1.4 copy.49
  176.9 3.4 %convolution_convert_fusion.refs_1_ = bf16[8,64,1024]{2,1,0:T(8,128)(2,1)} fusion(bf16[8,64,704]{2,1,0:T(8,128)(2,1)S(1)} %bitcast.84, bf16[1024,704,1]{1,0,2:T(8,128)(2,1)} %bitcast.92), kind=kOutput, calls=%fused_computation.29 | convolution fusion | flops 738721792 | bytes 3211264 | tf_op jit(solution)/shard_map/rk,ok->ro/dot_general | solution.py:343
  180.2 40.2 %shard_map.206 = (bf16[32,2,16,768]{3,2,1,0:T(8,128)(2,1)}, bf16[8,64,1024]{2,1,0:T(8,128)(2,1)}) custom-call(bf16[16,768]{1,0:T(8,128)(2,1)} %bitcast.86, bf16[8,64,1024]{2,1,0:T(8,128)(2,1)} %convolution_convert_fusion.refs_1_), custom_call_target="tpu_custom_call" | custom-call | bytes 3145728 | tf_op jit(solution)/shard_map/pallas_call | solution.py:260
  220.5 1.8 multiply_reduce_fusion
  222.3 0.7 dynamic-slice_convert_fusion
  223.0 0.2 multiply_convert_fusion
  223.3 0.5 copy-done.16
  223.8 1.0 convolution_convert_fusion.2
  224.8 0.4 reshape.169
  225.1 1.0 copy.51
  (46 shorter events, 0.3 us)
Async XLA Ops:
  4.5 2.4 %copy-start.12 = (f32[32,4]{0,1:T(4,128)S(1)}, f32[32,4]{0,1:T(4,128)}, u32[]{:S(2)}) copy-start(f32[32,4]{0,1:T(4,128)} %param.29) | copy-start | bytes 1540
  4.5 2.6 %copy-start.13 = (s32[8]{0:T(128)S(1)}, s32[8]{0:T(128)}, u32[]{:S(2)}) copy-start(s32[8]{0:T(128)} %param.26) | copy-start | bytes 100
  11.5 2.6 %copy-start.19 = (s32[8,64,64]{2,1,0:T(8,128)S(1)}, s32[8,64,64]{2,1,0:T(8,128)}, u32[]{:S(2)}) copy-start(s32[8,64,64]{2,1,0:T(8,128)} %param.28) | copy-start | bytes 393220
  14.1 3.2 %copy-start.8 = (s32[8,64]{1,0:T(8,128)S(1)}, s32[8,64]{1,0:T(8,128)}, u32[]{:S(2)}) copy-start(s32[8,64]{1,0:T(8,128)} %param.24) | copy-start | bytes 6148
  17.4 2.5 %copy-start.20 = (s32[8]{0:T(128)S(1)}, s32[8]{0:T(128)}, u32[]{:S(2)}) copy-start(s32[8]{0:T(128)} %param.25) | copy-start | bytes 100
  20.5 4.4 %copy-start.3 = (bf16[8,1,512,256]{2,3,0,1:T(8,128)(2,1)S(1)}, bf16[8,1,512,256]{2,3,0,1:T(8,128)(2,1)}, u32[]{:S(2)}) copy-start(bf16[8,1,512,256]{2,3,0,1:T(8,128)(2,1)} %copy.41) | copy-start | bytes 6291460
  21.0 4.0 %copy-start.1 = (f32[8,4,64,512]{3,2,1,0:T(8,128)S(1)}, f32[8,4,64,512]{3,2,1,0:T(8,128)}, u32[]{:S(2)}) copy-start(f32[8,4,64,512]{3,2,1,0:T(8,128)} %get-tuple-element.32) | copy-start | bytes 12582916
  29.5 24.0 %copy-start.6 = (bf16[8,16,1024]{2,1,0:T(8,128)(2,1)S(1)}, bf16[8,16,1024]{2,1,0:T(8,128)(2,1)}, u32[]{:S(2)}) copy-start(bf16[8,16,1024]{2,1,0:T(8,128)(2,1)} %param.20) | copy-start | bytes 786436
  105.2 3.0 %copy-start = (bf16[8,64,1024]{2,1,0:T(8,128)(2,1)S(1)}, bf16[8,64,1024]{2,1,0:T(8,128)(2,1)}, u32[]{:S(2)}) copy-start(bf16[8,64,1024]{2,1,0:T(8,128)(2,1)} %get-tuple-element.11) | copy-start | bytes 3145732
  105.2 3.3 %copy-start.9 = (f32[1024]{0:T(1024)S(1)}, f32[1024]{0:T(1024)}, u32[]{:S(2)}) copy-start(f32[1024]{0:T(1024)} %param.30) | copy-start | bytes 12292
  108.2 1.0 copy-start.18
  110.7 1.8 copy-start.14
  112.6 2.0 copy-start.4
  115.3 1.0 copy-start.5
  115.7 52.6 %copy-start.7 = (bf16[16,3,256]{2,0,1:T(8,128)(2,1)S(1)}, bf16[16,3,256]{2,0,1:T(8,128)(2,1)}, u32[]{:S(2)}) copy-start(bf16[16,3,256]{2,0,1:T(8,128)(2,1)} %param.39) | copy-start | bytes 73732
  116.4 54.2 %copy-start.10 = (f32[1024]{0:T(1024)S(1)}, f32[1024]{0:T(1024)}, u32[]{:S(2)}) copy-start(f32[1024]{0:T(1024)} %param.31) | copy-start | bytes 12292
  168.3 2.3 %copy-start.2 = (bf16[8,64,1024]{2,1,0:T(8,128)(2,1)S(1)}, bf16[8,64,1024]{2,1,0:T(8,128)(2,1)}, u32[]{:S(2)}) copy-start(bf16[8,64,1024]{2,1,0:T(8,128)(2,1)} %get-tuple-element.14) | copy-start | bytes 3145732
  170.6 1.4 copy-start.15
  172.0 1.4 copy-start.17
  220.5 2.5 %copy-start.11 = (f32[1024]{0:T(1024)S(1)}, f32[1024]{0:T(1024)}, u32[]{:S(2)}) copy-start(f32[1024]{0:T(1024)} %param.32) | copy-start | bytes 12292
  222.3 1.5 copy-start.16
